TPU v7x, 128 devices: a whole 4x4x4 slice. The times are simulated.
128 devices in a mesh: atom: 32 (over z, y, core), dp: 4 (over x).
Axes of the slice: x: 4, y: 4, z: 4, core: 2. Of those that a mesh axis runs over, the one named last changes fastest.
Arguments:
- activations: bfloat16 [512, 8192], P('dp'), may hold values from -6 to 6
- dictionary: bfloat16 [8192, 65536], P('dp', 'atom'), may hold values from -0.03535534 to 0.03535534
Outputs:
- sparse_codes: float32 [512, 65536], P('dp', 'atom')
- residual: float32 [512, 8192], P('atom', 'dp')
- new_dictionary: bfloat16 [8192, 65536], P('dp', 'atom')
All inputs are finite; a program needn't handle non-finite values.
Results may differ from a plain program's by a relative error of at most 0.0025.
Values may be sent and summed in bfloat16 or wider, within the bound.
No kernel may reach another device: no remote copies, remote signals or barrier semaphores. Data moves between devices by JAX's collectives and lax.ppermute only.
A program may use at most 128 MiB of HBM per device.

v0:
```python
import functools

import jax
import jax.numpy as jnp
from jax import lax
from jax.experimental import pallas as pl
from jax.experimental.pallas import tpu as pltpu
from jax.sharding import Mesh, PartitionSpec as P


D = 8192
ITERS = 2
threshold = 0.05
step_size = 2.0
learn_rate = 1.0 / 16384.0
epsilon = 1e-12

BF = jnp.bfloat16
F32 = jnp.float32
ATOM = ("z", "y", "core")
MIB = 1 << 20


def shrink(values):
    return values - jnp.clip(values, -threshold, threshold)


def shift_x(value, step):
    return lax.ppermute(value, "x", [(i, (i + step) % 4) for i in range(4)])


def other_core(value):
    return lax.ppermute(value, "core", [(0, 1), (1, 0)])


def pairs_of(target):
    return [
        (z * 8 + y * 2 + core, target(z, y, core))
        for z in range(4)
        for y in range(4)
        for core in range(2)
    ]


def shift_mixed(value, step, first):
    def target(z, y, core):
        if (core == 0) == first:
            y = (y + step) % 4
        else:
            z = (z + step) % 4
        return z * 8 + y * 2 + core

    return lax.ppermute(value, ATOM, pairs_of(target))


def to_owner(value):
    def target(z, y, core):
        row, part = (y, z) if core == 0 else (z, y)
        return row * 8 + (2 * core + part // 2) * 2 + part % 2

    return lax.ppermute(value, ATOM, pairs_of(target))


def whole():
    return pl.BlockSpec(memory_space=pltpu.VMEM)


def anywhere():
    return pl.BlockSpec(memory_space=pl.ANY)


def scalars():
    return pl.BlockSpec(memory_space=pltpu.SMEM)


def in_vmem(value):
    return pltpu.with_memory_space_constraint(value, pltpu.VMEM)


def params(mib):
    return pltpu.CompilerParams(vmem_limit_bytes=mib * MIB)


def cost(flops, moved):
    return pl.CostEstimate(flops=flops, bytes_accessed=moved, transcendentals=0)


def shaped(rows, columns, dtype):
    return jax.ShapeDtypeStruct((rows, columns), dtype)


STRIP = 16


def strip(i):
    return pl.ds(pl.multiple_of(i * STRIP, STRIP), STRIP)


def fetch(index, pieces, target, sem, wait):
    for t, piece in enumerate(pieces):

        @pl.when(index == t)
        def _():
            copy = pltpu.make_async_copy(piece, target, sem)
            if wait:
                copy.wait()
            else:
                copy.start()


def load_kernel(dict_ref, out_ref, sem):
    copy = pltpu.make_async_copy(dict_ref, out_ref, sem)
    copy.start()
    copy.wait()


def load(dictionary):
    return pl.pallas_call(
        load_kernel,
        in_specs=[pl.BlockSpec(memory_space=pltpu.HBM)],
        out_specs=whole(),
        out_shape=pltpu.VMEM(dictionary.shape, BF),
        scratch_shapes=[pltpu.SemaphoreType.DMA],
        compiler_params=params(10),
        cost_estimate=cost(0, dictionary.size * 2),
        name="load",
    )(pltpu.with_memory_space_constraint(dictionary, pltpu.HBM))


def encode_kernel(size, count, k, index_ref, *refs):
    own, other = refs[:count], refs[count : 2 * count]
    dict_ref, low_ref, high_ref, left, sems = refs[2 * count :]
    half = left.shape[0] // 2
    own_at = index_ref[k, 0] if count > 1 else 0
    other_at = index_ref[k, 1] if count > 1 else 0
    for wait in (False, True):
        fetch(own_at, own, left.at[pl.ds(0, half)], sems.at[0], wait)
        fetch(other_at, other, left.at[pl.ds(half, half)], sems.at[1], wait)

    @pl.loop(0, dict_ref.shape[1] // size)
    def _(n):
        part = pl.ds(pl.multiple_of(n * size, size), size)
        out = jnp.dot(left[...], dict_ref[:, part], preferred_element_type=F32)
        low_ref[:, part] = out[:half].astype(low_ref.dtype)
        high_ref[:, part] = out[half:].astype(high_ref.dtype)


def encode_block(own, other, index, k, dictionary, size):
    half, feats = own[0].shape
    atoms = dictionary.shape[1]
    low = BF if k in (2, 3) else F32
    high = BF if k in (1, 2) else F32
    return pl.pallas_call(
        functools.partial(encode_kernel, size, len(own), k),
        in_specs=[scalars()] + [anywhere()] * (2 * len(own)) + [whole()],
        out_specs=[whole()] * 2,
        out_shape=[shaped(half, atoms, low), shaped(half, atoms, high)],
        scratch_shapes=[
            pltpu.VMEM((2 * half, feats), BF),
            pltpu.SemaphoreType.DMA((2,)),
        ],
        compiler_params=params(12),
        cost_estimate=cost(4 * half * feats * atoms, 2 * feats * atoms),
        name="encode",
    )(index, *own, *other, in_vmem(dictionary))


def add_kernel(sum_ref, piece_ref, out_ref):
    @pl.loop(0, sum_ref.shape[0] // STRIP)
    def _(i):
        here = strip(i)
        out_ref[here, :] = (sum_ref[here, :] + piece_ref[here, :].astype(F32)).astype(BF)


def add(total, piece):
    half, atoms = total.shape
    return pl.pallas_call(
        add_kernel,
        in_specs=[whole()] * 2,
        out_specs=whole(),
        out_shape=shaped(half, atoms, BF),
        compiler_params=params(8),
        cost_estimate=cost(half * atoms, 8 * half * atoms),
        name="add",
    )(in_vmem(total), piece)


def finish_kernel(last, index_ref, *refs):
    drives, received, refs = refs[:2], (refs[2:4], refs[4:6]), refs[6:]
    before_ref = refs[0] if last else None
    codes_ref, *coded = refs[-3:]
    half = drives[0].shape[0]
    strips = half // STRIP
    for h in range(2):

        @pl.loop(0, strips)
        def _(i):
            here, kept = strip(i), strip(i + h * strips)
            drive = drives[h][here, :]
            for piece in received[h]:
                drive = drive + piece[here, :].astype(F32)
            drive = step_size * drive
            codes = shrink(before_ref[kept, :] + drive if last else drive)
            there = kept
            if last:
                there = strip(lax.rem(i + (h + index_ref[4, 1]) * strips, 2 * strips))
            codes_ref[there, :] = codes
            coded[h][here, :] = codes.astype(BF)


def finish(index, drives, received, before):
    half, atoms = drives[0].shape
    last = before is not None
    codes, *coded = pl.pallas_call(
        functools.partial(finish_kernel, last),
        in_specs=[scalars()] + [whole()] * (7 if last else 6),
        out_specs=[whole()] * 3,
        out_shape=[shaped(2 * half, atoms, F32)] + [shaped(half, atoms, BF)] * 2,
        compiler_params=params(12),
        cost_estimate=cost(16 * half * atoms, 32 * half * atoms),
        name="finish",
    )(index, *drives, *received, *([in_vmem(before)] if last else []))
    return codes, coded


def decode_kernel(size, count, *refs):
    coded, dict_ref, keeps = refs[:count], refs[count], refs[count + 1 : -2]
    send_ref, left = refs[-2:]
    base = 0
    for piece in coded:
        left[pl.ds(base, piece.shape[0]), :] = piece[...]
        base += piece.shape[0]
    half = keeps[0].shape[0]

    @pl.loop(0, dict_ref.shape[0] // size)
    def _(n):
        part = pl.ds(pl.multiple_of(n * size, size), size)
        recon = lax.dot_general(
            left[...], dict_ref[part, :], (((1,), (1,)), ((), ())), preferred_element_type=F32
        )
        for b, keep in enumerate(keeps):
            keep[:, part] = recon[2 * b * half : (2 * b + 1) * half]
            send_ref[pl.ds(b * half, half), part] = recon[
                (2 * b + 1) * half : (2 * b + 2) * half
            ].astype(BF)


def decode_blocks(coded, dictionary, half, size):
    feats, atoms = dictionary.shape
    rows = sum(piece.shape[0] for piece in coded)
    count = rows // 2 // half
    outs = pl.pallas_call(
        functools.partial(decode_kernel, size, len(coded)),
        in_specs=[whole()] * (len(coded) + 1),
        out_specs=[whole()] * (count + 1),
        out_shape=[shaped(half, feats, F32)] * count + [shaped(rows // 2, feats, BF)],
        scratch_shapes=[
            pltpu.VMEM((rows, atoms), BF),
        ],
        compiler_params=params(12),
        cost_estimate=cost(2 * rows * feats * atoms, 2 * feats * atoms),
        name="decode",
    )(*coded, in_vmem(dictionary))
    return outs[:-1], outs[-1]


def route_kernel(index_ref, *refs):
    keeps, (sent_own, sent_pair, sent_far), outs = refs[:4], refs[4:7], refs[7:]
    half = outs[0].shape[0]
    sources = [(sent_own, 0), (sent_pair, 0), (sent_far, 0), (sent_pair, half)]
    for j in range(4):
        source, base = sources[j]

        @pl.loop(0, half // STRIP)
        def _(i):
            here = strip(i)
            there = pl.ds(pl.multiple_of(base + i * STRIP, STRIP), STRIP)
            value = (keeps[j][here, :] + source[there, :].astype(F32)).astype(BF)
            for k in range(4):

                @pl.when(index_ref[k, 2] == j)
                def _():
                    outs[k][here, :] = value


def route(index, keeps, sent):
    half, feats = keeps[0].shape
    return pl.pallas_call(
        route_kernel,
        in_specs=[scalars()] + [whole()] * 7,
        out_specs=[whole()] * 4,
        out_shape=[shaped(half, feats, BF)] * 4,
        compiler_params=params(12),
        cost_estimate=cost(8 * half * feats, 32 * half * feats),
        name="route",
    )(index, *keeps, *sent)


def total_of(pieces, here):
    total = pieces[0][here, :].astype(F32)
    for piece in pieces[1:]:
        total = total + piece[here, :].astype(F32)
    return total


def partial_kernel(*refs):
    @pl.loop(0, refs[0].shape[0] // STRIP)
    def _(i):
        refs[-1][strip(i), :] = total_of(refs[:-1], strip(i)).astype(BF)


def partial_sum(pieces):
    half, feats = pieces[0].shape
    return pl.pallas_call(
        partial_kernel,
        in_specs=[whole()] * 4,
        out_specs=whole(),
        out_shape=shaped(half, feats, BF),
        compiler_params=params(8),
        cost_estimate=cost(4 * half * feats, 10 * half * feats),
        name="partial",
    )(*pieces)


def residual_kernel(index_ref, *refs):
    pieces, acts = refs[:4], refs[4:8]
    rounded_ref, mine_ref, act, sem = refs[8:]
    for wait in (False, True):
        fetch(index_ref[0, 2], acts, act, sem, wait)

    @pl.loop(0, act.shape[0] // STRIP)
    def _(i):
        here = strip(i)
        full = act[here, :].astype(F32) - total_of(pieces, here)
        rounded_ref[here, :] = full.astype(BF)

        @pl.when(i == index_ref[4, 0])
        def _():
            mine_ref[...] = full


def residual_block(index, pieces, acts):
    half, feats = pieces[0].shape
    return pl.pallas_call(
        residual_kernel,
        in_specs=[scalars()] + [whole()] * 4 + [anywhere()] * 4,
        out_specs=[whole()] * 2,
        out_shape=[shaped(half, feats, BF), shaped(STRIP, feats, F32)],
        scratch_shapes=[pltpu.VMEM((half, feats), BF), pltpu.SemaphoreType.DMA],
        compiler_params=params(8),
        cost_estimate=cost(5 * half * feats, 14 * half * feats),
        name="residual",
    )(index, *pieces, *acts)


def arrange_kernel(index_ref, *refs):
    low, high, out_ref, sems = refs[:4], refs[4:8], refs[8], refs[9]
    half = low[0].shape[0]
    for wait in (False, True):
        for k in range(4):
            back = (4 - k) % 4
            own, other = pl.ds(2 * k * half, half), pl.ds((2 * k + 1) * half, half)
            fetch(index_ref[back, 2], low, out_ref.at[own], sems.at[k, 0], wait)
            fetch(index_ref[back, 3], high, out_ref.at[other], sems.at[k, 1], wait)


def arrange(index, coded):
    half, atoms = coded[0][0].shape
    low, high = zip(*coded)
    return pl.pallas_call(
        arrange_kernel,
        in_specs=[scalars()] + [anywhere()] * 8,
        out_specs=whole(),
        out_shape=pltpu.VMEM((8 * half, atoms), BF),
        scratch_shapes=[pltpu.SemaphoreType.DMA((4, 2))],
        compiler_params=params(8),
        cost_estimate=cost(0, 32 * half * atoms),
        name="arrange",
    )(index, *low, *high)


def turn_kernel(own_ref, other_ref, out_ref):
    out_ref[...] = jnp.concatenate([own_ref[...], other_ref[...]], axis=0).T


def turn(own, other):
    half, feats = own.shape
    return pl.pallas_call(
        turn_kernel,
        in_specs=[whole()] * 2,
        out_specs=whole(),
        out_shape=pltpu.VMEM((feats, 2 * half), BF),
        compiler_params=params(8),
        cost_estimate=cost(0, 8 * half * feats),
        name="turn",
    )(own, other)


def gradient_kernel(*refs):
    turned, (codes_ref, dict_ref, moved_ref, square_ref) = refs[:4], refs[4:]
    feats = dict_ref.shape[0]
    size, block = 512, 512

    @pl.loop(0, dict_ref.shape[1] // size)
    def _(n):
        part = pl.ds(pl.multiple_of(n * size, size), size)
        codes = codes_ref[:, part]
        total = jnp.zeros((8, size), F32)
        for f in range(feats // block):
            rows = pl.ds(f * block, block)
            left = jnp.concatenate([piece[rows, :] for piece in turned], axis=1)
            grad = jnp.dot(left, codes, preferred_element_type=F32)
            moved = dict_ref[rows, part].astype(F32) + learn_rate * grad
            moved_ref[rows, part] = moved
            total = total + jnp.sum((moved * moved).reshape(block // 8, 8, size), axis=0)
        square_ref[:, part] = jnp.sum(total, axis=0, keepdims=True)


def gradient(turned, codes, dictionary):
    feats, atoms = dictionary.shape
    rows = codes.shape[0]
    return pl.pallas_call(
        gradient_kernel,
        in_specs=[whole()] * 6,
        out_specs=[whole()] * 2,
        out_shape=[pltpu.VMEM((feats, atoms), F32), shaped(1, atoms, F32)],
        compiler_params=params(30),
        cost_estimate=cost(2 * rows * feats * atoms, 6 * feats * atoms),
        name="gradient",
    )(*(in_vmem(piece) for piece in turned), in_vmem(codes), in_vmem(dictionary))


def scale_kernel(moved_ref, *refs):
    squares, (out_ref, ready, sems) = refs[:4], refs[4:]
    square = squares[0][...] + squares[1][...] + squares[2][...] + squares[3][...]
    factor = lax.rsqrt(square / D + epsilon)
    count, block, _ = ready.shape
    copies = []
    for n in range(count):
        rows = pl.ds(n * block, block)

        @pl.loop(0, block // STRIP)
        def _(i):
            from_rows = pl.ds(pl.multiple_of(n * block + i * STRIP, STRIP), STRIP)
            ready[n, strip(i), :] = (moved_ref[from_rows, :] * factor).astype(BF)

        copies.append(pltpu.make_async_copy(ready.at[n], out_ref.at[rows], sems.at[n]))
        copies[n].start()
    for copy in copies:
        copy.wait()


def scale(moved, squares):
    feats, atoms = moved.shape
    count = 8
    return pl.pallas_call(
        scale_kernel,
        in_specs=[whole()] * 5,
        out_specs=pl.BlockSpec(memory_space=pltpu.HBM),
        out_shape=shaped(feats, atoms, BF),
        scratch_shapes=[
            pltpu.VMEM((count, feats // count, atoms), BF),
            pltpu.SemaphoreType.DMA((count,)),
        ],
        compiler_params=params(16),
        cost_estimate=cost(feats * atoms, feats * atoms * 2),
        name="scale",
    )(in_vmem(moved), *squares)


def step(activations, dictionary):
    x = lax.axis_index("x")
    y = lax.axis_index("y")
    z = lax.axis_index("z")
    core = lax.axis_index("core")
    first = jnp.where(core == 0, y, z)
    second = jnp.where(core == 0, z, y)
    rows = activations.shape[0]
    feats = dictionary.shape[0]
    half = rows // 2
    steps = jnp.arange(4, dtype=jnp.int32)[:, None]
    base = jnp.stack([first - x, second - x, x - first, x - second])[None]
    index = jnp.concatenate(
        [lax.rem(base - steps + 8, 4), jnp.stack([second, core, core, core])[None]],
        axis=0,
    )

    def act_of(part, block):
        return lax.dynamic_slice(activations, (part * half, block * feats), (half, feats))

    own_act = [act_of(core, x), None, None, None]
    other_act = [act_of(1 - core, x), None, None, None]
    for k in (2, 1, 3):
        own_act[k] = shift_x(act_of(core, lax.rem(x + k, 4)), k)
    dictionary = load(dictionary)
    for k in (1, 3, 2):
        other_act[k] = other_core(own_act[k])

    def encode(source, before):
        def part(k):
            own, other = source(k)
            size = 512 if k == 0 else 1024
            return encode_block(own, other, index, k, dictionary, size)

        far_low, far_high = part(2)
        far_low = shift_x(far_low, 1)
        far_high = shift_x(far_high, -1)
        up_low, up_high = part(1)
        up_high = shift_x(up_high, 1)
        down_low, down_high = part(3)
        down_low = shift_x(down_low, -1)
        up_low = shift_x(add(up_low, far_low), 1)
        down_high = shift_x(add(down_high, far_high), -1)
        drives = part(0)
        received = (up_low, down_low, up_high, down_high)
        return finish(index, drives, received, before)

    def gather(coded):
        low, high = coded
        up_low = shift_x(low, 1)
        down_high = shift_x(high, -1)
        up_high = shift_x(high, 1)
        down_low = shift_x(low, -1)
        far_low = shift_x(up_low, 1)
        far_high = shift_x(down_high, -1)
        return (low, high), (up_low, up_high), (far_low, far_high), (down_low, down_high)

    def residual_of(coded):
        keeps, sent = [None] * 4, []
        for blocks in ((0,), (1, 3), (2,)):
            pieces = [piece for j in blocks for piece in coded[j]]
            kept, send = decode_blocks(pieces, dictionary, half, 1024 if blocks == (2,) else 512)
            for j, keep in zip(blocks, kept):
                keeps[j] = keep
            sent.append(other_core(send))
        routed = route(index, keeps, sent)
        pieces = [routed[0]]
        for k in (2, 1, 3):
            pieces.append(shift_mixed(routed[k], k, True))
        total = partial_sum(pieces)
        pieces = [total]
        for k in (2, 1, 3):
            pieces.append(shift_mixed(total, k, False))
        rounded, mine = residual_block(index, pieces, own_act)
        own = [rounded, None, None, None]
        other = [None] * 4
        for k in (2, 1, 3):
            own[k] = shift_mixed(rounded, k, True)
        for k in (0, 1, 3, 2):
            other[k] = other_core(own[k])
        return mine, own, other

    codes = None
    source = lambda k: (own_act[(4 - k) % 4 :][:1], other_act[(4 - k) % 4 :][:1])
    for _ in range(ITERS):
        codes, coded = encode(source, codes)
        coded = gather(coded)
        mine, own, other = residual_of(coded)
        source = lambda k, own=own, other=other: (own, other)

    residual = to_owner(mine)
    arranged = arrange(index, coded)
    turned = []
    for k in range(4):
        turned.append(turn(own[k], other[k]))
    moved, square = gradient(turned, arranged, dictionary)
    squares = [square]
    for k in (2, 1, 3):
        squares.append(shift_x(square, k))
    new_dictionary = scale(moved, squares)
    return (codes, residual, new_dictionary)


def solution(mesh):
    mesh = Mesh(mesh.devices.reshape(4, 4, 2, 4), ("z", "y", "core", "x"))
    return jax.shard_map(
        step,
        mesh=mesh,
        in_specs=(P("x", None), P("x", ATOM)),
        out_specs=(P("x", ATOM), P(ATOM, "x"), P("x", ATOM)),
        check_vma=False,
    )
```

profile of v0, /device:TPU:24, one launch (start us, length us, event | category | flops | bytes accessed | tf_op | source)
XLA Modules:
  0.0 234.3 jit_solution(11565271028877877005)
XLA Ops:
  2.0 3.1 %collective-permute-start.2 = (bf16[64,2048]{1,0:T(8,128)(2,1)S(1)}, bf16[64,2048]{1,0:T(8,128)(2,1)S(1)}, u32[]{:S(2)}, u32[]{:S(2)}) collective-permute-start(bf16[64,2048]{1,0:T(8,128)(2,1)S(1)} %get-tuple-element.105), channel_id=1, source_target_pairs={{0,2},{1,3},{2,0},{3,1},{4,6},{5,7},{6,4},{7,5},{8,10},{9,11},{10,... | collective-permute-start | bytes 786440 | tf_op jit(solution)/shard_map/ppermute | solution.py:29
  5.7 2.6 %collective-permute-start = (bf16[64,2048]{1,0:T(8,128)(2,1)S(1)}, bf16[64,2048]{1,0:T(8,128)(2,1)S(1)}, u32[]{:S(2)}, u32[]{:S(2)}) collective-permute-start(bf16[64,2048]{1,0:T(8,128)(2,1)S(1)} %get-tuple-element.102), channel_id=1, source_target_pairs={{0,3},{1,0},{2,1},{3,2},{4,7},{5,4},{6,5},{7,6},{8,11},{9,8},{10,9... | collective-permute-start | bytes 786440 | tf_op jit(solution)/shard_map/ppermute | solution.py:29
  8.4 4.4 %collective-permute-done.2.refs_0_.refs_6_ = bf16[64,2048]{1,0:T(8,128)(2,1)S(1)} collective-permute-done((bf16[64,2048]{1,0:T(8,128)(2,1)S(1)}, bf16[64,2048]{1,0:T(8,128)(2,1)S(1)}, u32[]{:S(2)}, u32[]{:S(2)}) %collective-permute-start.2) | collective-permute-done | bytes 262176 | tf_op jit(solution)/shard_map/ppermute | solution.py:29
  12.8 3.4 %load.1.refs_2_.refs_4_.refs_8_.refs_5_ = bf16[2048,2048]{1,0:T(8,128)(2,1)S(1)} custom-call(bf16[2048,2048]{1,0:T(8,128)(2,1)} %dict_ref.1), custom_call_target="tpu_custom_call" | custom-call | bytes 8388608 | tf_op jit(solution)/shard_map/load/pallas_call | solution.py:118
  20.1 2.2 collective-permute-start.10
  24.5 3.3 %collective-permute-start.8 = (bf16[64,2048]{1,0:T(8,128)(2,1)S(1)}, bf16[64,2048]{1,0:T(8,128)(2,1)S(1)}, u32[]{:S(2)}, u32[]{:S(2)}) collective-permute-start(bf16[64,2048]{1,0:T(8,128)(2,1)S(1)} %get-tuple-element.56), channel_id=1, source_target_pairs={{0,3},{1,0},{2,1},{3,2},{4,7},{5,4},{6,5},{7,6},{8,11},{9,8},{10,9... | collective-permute-start | bytes 786440 | tf_op jit(solution)/shard_map/ppermute | solution.py:29
  30.1 3.3 %collective-permute-start.11 = (bf16[64,2048]{1,0:T(8,128)(2,1)S(1)}, bf16[64,2048]{1,0:T(8,128)(2,1)S(1)}, u32[]{:S(2)}, u32[]{:S(2)}) collective-permute-start(bf16[64,2048]{1,0:T(8,128)(2,1)S(1)} %add.64), channel_id=1, source_target_pairs={{0,3},{1,0},{2,1},{3,2},{4,7},{5,4},{6,5},{7,6},{8,11},{9,8},{10,9... | collective-permute-start | bytes 786440 | tf_op jit(solution)/shard_map/ppermute | solution.py:29
  33.6 2.5 %encode.8 = (f32[64,2048]{1,0:T(8,128)S(1)}, f32[64,2048]{1,0:T(8,128)S(1)}) custom-call(s32[5,4]{1,0:T(8,128)S(1)} %pad_add_fusion.index_ref, bf16[64,2048]{1,0:T(8,128)(2,1)S(1)} %get-tuple-element.104.refs_0_.refs_4_, bf16[64,2048]{1,0:T(8,128)(2,1)S(1)} %get-tuple-element.103.refs_1_, bf16[2048,2048]{1,0:T(8,128)(2,1)S(1)} %load.1.refs_2_.refs_4_.refs_8_.refs_5_), custom_call_target="tpu_custom_call" | custom-call | flops 1073741824 | bytes 8388608 | tf_op jit(solution)/shard_map/encode/pallas_call | solution.py:153
  36.1 4.3 %collective-permute-done.9.refs_4_ = bf16[64,2048]{1,0:T(8,128)(2,1)S(1)} collective-permute-done((bf16[64,2048]{1,0:T(8,128)(2,1)S(1)}, bf16[64,2048]{1,0:T(8,128)(2,1)S(1)}, u32[]{:S(2)}, u32[]{:S(2)}) %collective-permute-start.9) | collective-permute-done | bytes 262176 | tf_op jit(solution)/shard_map/ppermute | solution.py:29
  40.4 4.3 %collective-permute-done.5.refs_2_ = bf16[64,2048]{1,0:T(8,128)(2,1)S(1)} collective-permute-done((bf16[64,2048]{1,0:T(8,128)(2,1)S(1)}, bf16[64,2048]{1,0:T(8,128)(2,1)S(1)}, u32[]{:S(2)}, u32[]{:S(2)}) %collective-permute-start.5) | collective-permute-done | bytes 262176 | tf_op jit(solution)/shard_map/ppermute | solution.py:29
  45.7 3.2 %collective-permute-start.15 = (bf16[64,2048]{1,0:T(8,128)(2,1)S(1)}, bf16[64,2048]{1,0:T(8,128)(2,1)S(1)}, u32[]{:S(2)}, u32[]{:S(2)}) collective-permute-start(bf16[64,2048]{1,0:T(8,128)(2,1)S(1)} %get-tuple-element.61.refs_1_), channel_id=1, source_target_pairs={{0,3},{1,0},{2,1},{3,2},{4,7},{5,4},{6,5},{7,6},{8,11},{9,8},{10,9... | collective-permute-start | bytes 786440 | tf_op jit(solution)/shard_map/ppermute | solution.py:29
  51.0 5.1 %collective-permute-done.12.refs_0_ = bf16[64,2048]{1,0:T(8,128)(2,1)S(1)} collective-permute-done((bf16[64,2048]{1,0:T(8,128)(2,1)S(1)}, bf16[64,2048]{1,0:T(8,128)(2,1)S(1)}, u32[]{:S(2)}, u32[]{:S(2)}) %collective-permute-start.12) | collective-permute-done | bytes 262176 | tf_op jit(solution)/shard_map/ppermute | solution.py:29
  56.1 3.2 %collective-permute-start.17 = (bf16[64,2048]{1,0:T(8,128)(2,1)S(1)}, bf16[64,2048]{1,0:T(8,128)(2,1)S(1)}, u32[]{:S(2)}, u32[]{:S(2)}) collective-permute-start(bf16[64,2048]{1,0:T(8,128)(2,1)S(1)} %collective-permute-done.15.refs_3_), channel_id=1, source_target_pairs={{0,3},{1,0},{2,1},{3,2},{4,7},{5,4},{6,5},{7,6},{8,11},{9,8},{10,9... | collective-permute-start | bytes 786440 | tf_op jit(solution)/shard_map/ppermute | solution.py:29
  61.7 3.0 %decode.7 = (f32[64,2048]{1,0:T(8,128)S(1)}, f32[64,2048]{1,0:T(8,128)S(1)}, bf16[128,2048]{1,0:T(8,128)(2,1)S(1)}) custom-call(bf16[64,2048]{1,0:T(8,128)(2,1)S(1)} %collective-permute-done.12.refs_0_, bf16[64,2048]{1,0:T(8,128)(2,1)S(1)} %collective-permute-done.13.refs_1_, bf16[64,2048]{1,0:T(8,128)(2,1)S(1)} %collective-permute-done.14.refs_2_, ...), custom_call_target="tpu_custom_call" | custom-call | flops 2147483648 | bytes 8388608 | tf_op jit(solution)/shard_map/decode/pallas_call | solution.py:252
  64.8 3.4 %decode.6 = (f32[64,2048]{1,0:T(8,128)S(1)}, bf16[64,2048]{1,0:T(8,128)(2,1)S(1)}) custom-call(bf16[64,2048]{1,0:T(8,128)(2,1)S(1)} %get-tuple-element.60.refs_0_, bf16[64,2048]{1,0:T(8,128)(2,1)S(1)} %get-tuple-element.61.refs_1_, bf16[2048,2048]{1,0:T(8,128)(2,1)S(1)} %load.1.refs_2_.refs_4_.refs_8_.refs_5_), custom_call_target="tpu_custom_call" | custom-call | flops 1073741824 | bytes 8388608 | tf_op jit(solution)/shard_map/decode/pallas_call | solution.py:252
  68.8 3.0 %decode.8 = (f32[64,2048]{1,0:T(8,128)S(1)}, bf16[64,2048]{1,0:T(8,128)(2,1)S(1)}) custom-call(bf16[64,2048]{1,0:T(8,128)(2,1)S(1)} %collective-permute-done.16.refs_0_, bf16[64,2048]{1,0:T(8,128)(2,1)S(1)} %collective-permute-done.17.refs_1_, bf16[2048,2048]{1,0:T(8,128)(2,1)S(1)} %load.1.refs_2_.refs_4_.refs_8_.refs_5_), custom_call_target="tpu_custom_call" | custom-call | flops 1073741824 | bytes 8388608 | tf_op jit(solution)/shard_map/decode/pallas_call | solution.py:252
  78.5 4.5 %collective-permute-done.21.refs_1_ = bf16[64,2048]{1,0:T(8,128)(2,1)S(1)} collective-permute-done((bf16[64,2048]{1,0:T(8,128)(2,1)S(1)}, bf16[64,2048]{1,0:T(8,128)(2,1)S(1)}, u32[]{:S(2)}, u32[]{:S(2)}) %collective-permute-start.21) | collective-permute-done | bytes 262176 | tf_op jit(solution)/shard_map/ppermute | solution.py:53
  83.3 2.8 %collective-permute-done.23.refs_3_ = bf16[64,2048]{1,0:T(8,128)(2,1)S(1)} collective-permute-done((bf16[64,2048]{1,0:T(8,128)(2,1)S(1)}, bf16[64,2048]{1,0:T(8,128)(2,1)S(1)}, u32[]{:S(2)}, u32[]{:S(2)}) %collective-permute-start.23) | collective-permute-done | bytes 262176 | tf_op jit(solution)/shard_map/ppermute | solution.py:53
  86.2 4.1 %collective-permute-start.26 = (bf16[64,2048]{1,0:T(8,128)(2,1)S(1)}, bf16[64,2048]{1,0:T(8,128)(2,1)S(1)}, u32[]{:S(2)}, u32[]{:S(2)}) collective-permute-start(bf16[64,2048]{1,0:T(8,128)(2,1)S(1)} %partial.2.refs_0_), channel_id=1, source_target_pairs={{0,96},{4,28},{8,104},{12,4},{16,112},{20,12},{24,120},{28,20},{32... | collective-permute-start | bytes 786440 | tf_op jit(solution)/shard_map/ppermute | solution.py:53
  94.1 6.5 %collective-permute-done.25.refs_2_ = bf16[64,2048]{1,0:T(8,128)(2,1)S(1)} collective-permute-done((bf16[64,2048]{1,0:T(8,128)(2,1)S(1)}, bf16[64,2048]{1,0:T(8,128)(2,1)S(1)}, u32[]{:S(2)}, u32[]{:S(2)}) %collective-permute-start.25) | collective-permute-done | bytes 262176 | tf_op jit(solution)/shard_map/ppermute | solution.py:53
  106.0 6.7 %collective-permute-done.29.refs_3_ = bf16[64,2048]{1,0:T(8,128)(2,1)S(1)} collective-permute-done((bf16[64,2048]{1,0:T(8,128)(2,1)S(1)}, bf16[64,2048]{1,0:T(8,128)(2,1)S(1)}, u32[]{:S(2)}, u32[]{:S(2)}) %collective-permute-start.29) | collective-permute-done | bytes 262176 | tf_op jit(solution)/shard_map/ppermute | solution.py:53
  115.1 2.2 encode.14
  117.3 3.3 %collective-permute-start.38 = (bf16[64,2048]{1,0:T(8,128)(2,1)S(1)}, bf16[64,2048]{1,0:T(8,128)(2,1)S(1)}, u32[]{:S(2)}, u32[]{:S(2)}) collective-permute-start(bf16[64,2048]{1,0:T(8,128)(2,1)S(1)} %get-tuple-element.81), channel_id=1, source_target_pairs={{0,3},{1,0},{2,1},{3,2},{4,7},{5,4},{6,5},{7,6},{8,11},{9,8},{10,9... | collective-permute-start | bytes 786440 | tf_op jit(solution)/shard_map/ppermute | solution.py:29
  120.6 2.2 encode.15
  122.8 3.3 %collective-permute-start.36 = (bf16[64,2048]{1,0:T(8,128)(2,1)S(1)}, bf16[64,2048]{1,0:T(8,128)(2,1)S(1)}, u32[]{:S(2)}, u32[]{:S(2)}) collective-permute-start(bf16[64,2048]{1,0:T(8,128)(2,1)S(1)} %get-tuple-element.78), channel_id=1, source_target_pairs={{0,3},{1,0},{2,1},{3,2},{4,7},{5,4},{6,5},{7,6},{8,11},{9,8},{10,9... | collective-permute-start | bytes 786440 | tf_op jit(solution)/shard_map/ppermute | solution.py:29
  126.1 2.2 encode.13
  128.5 3.3 %collective-permute-start.39 = (bf16[64,2048]{1,0:T(8,128)(2,1)S(1)}, bf16[64,2048]{1,0:T(8,128)(2,1)S(1)}, u32[]{:S(2)}, u32[]{:S(2)}) collective-permute-start(bf16[64,2048]{1,0:T(8,128)(2,1)S(1)} %add.66), channel_id=1, source_target_pairs={{0,3},{1,0},{2,1},{3,2},{4,7},{5,4},{6,5},{7,6},{8,11},{9,8},{10,9... | collective-permute-start | bytes 786440 | tf_op jit(solution)/shard_map/ppermute | solution.py:29
  132.0 2.6 %encode.12 = (f32[64,2048]{1,0:T(8,128)S(1)}, f32[64,2048]{1,0:T(8,128)S(1)}) custom-call(s32[5,4]{1,0:T(8,128)S(1)} %pad_add_fusion.index_ref, bf16[64,2048]{1,0:T(8,128)(2,1)S(1)} %get-tuple-element.73.refs_0_, bf16[64,2048]{1,0:T(8,128)(2,1)S(1)} %collective-permute-done.27.refs_1_, bf16[64,2048]{1,0:T(8,128)(2,1)S(1)} %collective-permute-done.28.refs_2_, ...), custom_call_target="tpu_custom_call" | custom-call | flops 1073741824 | bytes 8388608 | tf_op jit(solution)/shard_map/encode/pallas_call | solution.py:153
  134.6 4.2 %collective-permute-done.37.refs_4_ = bf16[64,2048]{1,0:T(8,128)(2,1)S(1)} collective-permute-done((bf16[64,2048]{1,0:T(8,128)(2,1)S(1)}, bf16[64,2048]{1,0:T(8,128)(2,1)S(1)}, u32[]{:S(2)}, u32[]{:S(2)}) %collective-permute-start.37) | collective-permute-done | bytes 262176 | tf_op jit(solution)/shard_map/ppermute | solution.py:29
  138.8 4.0 %collective-permute-done.35.refs_2_ = bf16[64,2048]{1,0:T(8,128)(2,1)S(1)} collective-permute-done((bf16[64,2048]{1,0:T(8,128)(2,1)S(1)}, bf16[64,2048]{1,0:T(8,128)(2,1)S(1)}, u32[]{:S(2)}, u32[]{:S(2)}) %collective-permute-start.35) | collective-permute-done | bytes 262176 | tf_op jit(solution)/shard_map/ppermute | solution.py:29
  144.7 3.2 %collective-permute-start.43 = (bf16[64,2048]{1,0:T(8,128)(2,1)S(1)}, bf16[64,2048]{1,0:T(8,128)(2,1)S(1)}, u32[]{:S(2)}, u32[]{:S(2)}) collective-permute-start(bf16[64,2048]{1,0:T(8,128)(2,1)S(1)} %get-tuple-element.85.refs_1_.refs_4_), channel_id=1, source_target_pairs={{0,3},{1,0},{2,1},{3,2},{4,7},{5,4},{6,5},{7,6},{8,11},{9,8},{10,9... | collective-permute-start | bytes 786440 | tf_op jit(solution)/shard_map/ppermute | solution.py:29
  150.0 5.1 %collective-permute-done.40.refs_0_.refs_1_ = bf16[64,2048]{1,0:T(8,128)(2,1)S(1)} collective-permute-done((bf16[64,2048]{1,0:T(8,128)(2,1)S(1)}, bf16[64,2048]{1,0:T(8,128)(2,1)S(1)}, u32[]{:S(2)}, u32[]{:S(2)}) %collective-permute-start.40) | collective-permute-done | bytes 262176 | tf_op jit(solution)/shard_map/ppermute | solution.py:29
  155.1 3.2 %collective-permute-start.45 = (bf16[64,2048]{1,0:T(8,128)(2,1)S(1)}, bf16[64,2048]{1,0:T(8,128)(2,1)S(1)}, u32[]{:S(2)}, u32[]{:S(2)}) collective-permute-start(bf16[64,2048]{1,0:T(8,128)(2,1)S(1)} %collective-permute-done.43.refs_3_.refs_7_), channel_id=1, source_target_pairs={{0,3},{1,0},{2,1},{3,2},{4,7},{5,4},{6,5},{7,6},{8,11},{9,8},{10,9... | collective-permute-start | bytes 786440 | tf_op jit(solution)/shard_map/ppermute | solution.py:29
  160.7 3.0 %decode.10 = (f32[64,2048]{1,0:T(8,128)S(1)}, f32[64,2048]{1,0:T(8,128)S(1)}, bf16[128,2048]{1,0:T(8,128)(2,1)S(1)}) custom-call(bf16[64,2048]{1,0:T(8,128)(2,1)S(1)} %collective-permute-done.40.refs_0_.refs_1_, bf16[64,2048]{1,0:T(8,128)(2,1)S(1)} %collective-permute-done.41.refs_1_.refs_5_, bf16[64,2048]{1,0:T(8,128)(2,1)S(1)} %collective-permute-done.42.refs_2_.refs_3_, ...), custom_call_target="tpu_custom_call" | custom-call | flops 2147483648 | bytes 8388608 | tf_op jit(solution)/shard_map/decode/pallas_call | solution.py:252
  163.8 3.4 %decode.9 = (f32[64,2048]{1,0:T(8,128)S(1)}, bf16[64,2048]{1,0:T(8,128)(2,1)S(1)}) custom-call(bf16[64,2048]{1,0:T(8,128)(2,1)S(1)} %get-tuple-element.84.refs_0_, bf16[64,2048]{1,0:T(8,128)(2,1)S(1)} %get-tuple-element.85.refs_1_.refs_4_, bf16[2048,2048]{1,0:T(8,128)(2,1)S(1)} %load.1.refs_2_.refs_4_.refs_8_.refs_5_), custom_call_target="tpu_custom_call" | custom-call | flops 1073741824 | bytes 8388608 | tf_op jit(solution)/shard_map/decode/pallas_call | solution.py:252
  167.8 3.0 %decode.11 = (f32[64,2048]{1,0:T(8,128)S(1)}, bf16[64,2048]{1,0:T(8,128)(2,1)S(1)}) custom-call(bf16[64,2048]{1,0:T(8,128)(2,1)S(1)} %collective-permute-done.44.refs_0_.refs_2_, bf16[64,2048]{1,0:T(8,128)(2,1)S(1)} %collective-permute-done.45.refs_1_.refs_6_, bf16[2048,2048]{1,0:T(8,128)(2,1)S(1)} %load.1.refs_2_.refs_4_.refs_8_.refs_5_), custom_call_target="tpu_custom_call" | custom-call | flops 1073741824 | bytes 8388608 | tf_op jit(solution)/shard_map/decode/pallas_call | solution.py:252
  177.3 4.4 %collective-permute-done.49.refs_1_ = bf16[64,2048]{1,0:T(8,128)(2,1)S(1)} collective-permute-done((bf16[64,2048]{1,0:T(8,128)(2,1)S(1)}, bf16[64,2048]{1,0:T(8,128)(2,1)S(1)}, u32[]{:S(2)}, u32[]{:S(2)}) %collective-permute-start.49) | collective-permute-done | bytes 262176 | tf_op jit(solution)/shard_map/ppermute | solution.py:53
  181.7 2.8 %collective-permute-done.50.refs_2_ = bf16[64,2048]{1,0:T(8,128)(2,1)S(1)} collective-permute-done((bf16[64,2048]{1,0:T(8,128)(2,1)S(1)}, bf16[64,2048]{1,0:T(8,128)(2,1)S(1)}, u32[]{:S(2)}, u32[]{:S(2)}) %collective-permute-start.50) | collective-permute-done | bytes 262176 | tf_op jit(solution)/shard_map/ppermute | solution.py:53
  187.1 4.0 %collective-permute-done.54.refs_3_ = bf16[64,2048]{1,0:T(8,128)(2,1)S(1)} collective-permute-done((bf16[64,2048]{1,0:T(8,128)(2,1)S(1)}, bf16[64,2048]{1,0:T(8,128)(2,1)S(1)}, u32[]{:S(2)}, u32[]{:S(2)}) %collective-permute-start.54) | collective-permute-done | bytes 262176 | tf_op jit(solution)/shard_map/ppermute | solution.py:53
  191.1 4.7 %collective-permute-done.53.refs_2_ = bf16[64,2048]{1,0:T(8,128)(2,1)S(1)} collective-permute-done((bf16[64,2048]{1,0:T(8,128)(2,1)S(1)}, bf16[64,2048]{1,0:T(8,128)(2,1)S(1)}, u32[]{:S(2)}, u32[]{:S(2)}) %collective-permute-start.53) | collective-permute-done | bytes 262176 | tf_op jit(solution)/shard_map/ppermute | solution.py:53
  197.2 3.7 %collective-permute-start.59 = (bf16[64,2048]{1,0:T(8,128)(2,1)S(1)}, bf16[64,2048]{1,0:T(8,128)(2,1)S(1)}, u32[]{:S(2)}, u32[]{:S(2)}) collective-permute-start(bf16[64,2048]{1,0:T(8,128)(2,1)S(1)} %get-tuple-element.98.own_ref), channel_id=1, source_target_pairs={{0,16},{4,68},{8,24},{12,76},{16,0},{20,84},{24,8},{28,92},{32,48}... | collective-permute-start | bytes 786440 | tf_op jit(solution)/shard_map/ppermute | solution.py:53
  200.9 3.5 %collective-permute-done.61.own_ref = bf16[64,2048]{1,0:T(8,128)(2,1)S(1)} collective-permute-done((bf16[64,2048]{1,0:T(8,128)(2,1)S(1)}, bf16[64,2048]{1,0:T(8,128)(2,1)S(1)}, u32[]{:S(2)}, u32[]{:S(2)}) %collective-permute-start.61) | collective-permute-done | bytes 262176 | tf_op jit(solution)/shard_map/ppermute | solution.py:53
  204.4 3.7 %collective-permute-done.59.own_ref = bf16[64,2048]{1,0:T(8,128)(2,1)S(1)} collective-permute-done((bf16[64,2048]{1,0:T(8,128)(2,1)S(1)}, bf16[64,2048]{1,0:T(8,128)(2,1)S(1)}, u32[]{:S(2)}, u32[]{:S(2)}) %collective-permute-start.59) | collective-permute-done | bytes 262176 | tf_op jit(solution)/shard_map/ppermute | solution.py:53
  209.6 4.3 %collective-permute-start.55 = (f32[16,2048]{1,0:T(8,128)S(1)}, f32[16,2048]{1,0:T(8,128)S(1)}, u32[]{:S(2)}, u32[]{:S(2)}) collective-permute-start(f32[16,2048]{1,0:T(8,128)S(1)} %get-tuple-element.97), channel_id=1, source_target_pairs={{0,0},{4,16},{8,32},{12,20},{16,64},{20,24},{24,96},{28,28},{32,4}... | collective-permute-start | bytes 393224 | tf_op jit(solution)/shard_map/ppermute | solution.py:61
  214.7 6.0 %gradient.1 = (f32[2048,2048]{1,0:T(8,128)S(1)}, f32[1,2048]{1,0:T(1,128)}) custom-call(bf16[2048,128]{1,0:T(8,128)(2,1)S(1)} %turn.4.refs_0_, bf16[2048,128]{1,0:T(8,128)(2,1)S(1)} %turn.5.refs_1_, bf16[2048,128]{1,0:T(8,128)(2,1)S(1)} %turn.6.refs_2_, bf16[2048,128]{1,0:T(8,128)(2,1)S(1)} %turn.7.refs_3_, bf16[512,2048]{1,0:T(8,128)(2,1)S(1)} %arrange.1.refs_4_, ...), custom_call_target="tpu_custom_call" | custom-call | flops 4294967296 | bytes 25165824 | tf_op jit(solution)/shard_map/gradient/pallas_call | solution.py:422
  220.7 3.2 %collective-permute-start.65 = (f32[1,2048]{1,0:T(1,128)}, f32[1,2048]{1,0:T(1,128)S(1)}, u32[]{:S(2)}, u32[]{:S(2)}) collective-permute-start(f32[1,2048]{1,0:T(1,128)} %get-tuple-element.100.refs_0_), channel_id=1, source_target_pairs={{0,3},{1,0},{2,1},{3,2},{4,7},{5,4},{6,5},{7,6},{8,11},{9,8},{10,9... | collective-permute-start | bytes 24584 | tf_op jit(solution)/shard_map/ppermute | solution.py:29
  225.6 3.5 %collective-permute-done.64.refs_2_ = f32[1,2048]{1,0:T(1,128)S(1)} collective-permute-done((f32[1,2048]{1,0:T(1,128)}, f32[1,2048]{1,0:T(1,128)S(1)}, u32[]{:S(2)}, u32[]{:S(2)}) %collective-permute-start.64) | collective-permute-done | bytes 8224 | tf_op jit(solution)/shard_map/ppermute | solution.py:29
  230.1 3.6 %scale.1 = bf16[2048,2048]{1,0:T(8,128)(2,1)} custom-call(f32[2048,2048]{1,0:T(8,128)S(1)} %get-tuple-element.99.moved_ref, f32[1,2048]{1,0:T(1,128)S(1)} %copy-done.2, f32[1,2048]{1,0:T(1,128)S(1)} %collective-permute-done.63.refs_1_, f32[1,2048]{1,0:T(1,128)S(1)} %collective-permute-done.64.refs_2_, f32[1,2048]{1,0:T(1,128)S(1)} %collective-permute-done.65.refs_3_), custom_call_target="tpu_custom_call" | custom-call | flops 4194304 | bytes 8388608 | tf_op jit(solution)/shard_map/scale/pallas_call | solution.py:456
  (130 shorter events, 58.5 us)
Async XLA Ops:
  2.0 10.8 %collective-permute-start.2 = (bf16[64,2048]{1,0:T(8,128)(2,1)S(1)}, bf16[64,2048]{1,0:T(8,128)(2,1)S(1)}, u32[]{:S(2)}, u32[]{:S(2)}) collective-permute-start(bf16[64,2048]{1,0:T(8,128)(2,1)S(1)} %get-tuple-element.105), channel_id=1, source_target_pairs={{0,2},{1,3},{2,0},{3,1},{4,6},{5,7},{6,4},{7,5},{8,10},{9,11},{10,... | collective-permute-start | bytes 786440 | tf_op jit(solution)/shard_map/ppermute | solution.py:29
  5.1 12.1 %collective-permute-start.6 = (bf16[64,2048]{1,0:T(8,128)(2,1)S(1)}, bf16[64,2048]{1,0:T(8,128)(2,1)S(1)}, u32[]{:S(2)}, u32[]{:S(2)}) collective-permute-start(bf16[64,2048]{1,0:T(8,128)(2,1)S(1)} %get-tuple-element.101), channel_id=1, source_target_pairs={{0,1},{1,2},{2,3},{3,0},{4,5},{5,6},{6,7},{7,4},{8,9},{9,10},{10,1... | collective-permute-start | bytes 786440 | tf_op jit(solution)/shard_map/ppermute | solution.py:29
  5.7 11.7 %collective-permute-start = (bf16[64,2048]{1,0:T(8,128)(2,1)S(1)}, bf16[64,2048]{1,0:T(8,128)(2,1)S(1)}, u32[]{:S(2)}, u32[]{:S(2)}) collective-permute-start(bf16[64,2048]{1,0:T(8,128)(2,1)S(1)} %get-tuple-element.102), channel_id=1, source_target_pairs={{0,3},{1,0},{2,1},{3,2},{4,7},{5,4},{6,5},{7,6},{8,11},{9,8},{10,9... | collective-permute-start | bytes 786440 | tf_op jit(solution)/shard_map/ppermute | solution.py:29
  17.4 10.4 %collective-permute-start.1 = (bf16[64,2048]{1,0:T(8,128)(2,1)S(1)}, bf16[64,2048]{1,0:T(8,128)(2,1)S(1)}, u32[]{:S(2)}, u32[]{:S(2)}) collective-permute-start(bf16[64,2048]{1,0:T(8,128)(2,1)S(1)} %collective-permute-done.refs_0_.refs_7_), channel_id=1, source_target_pairs={{0,4},{4,0},{1,5},{5,1},{2,6},{6,2},{3,7},{7,3},{8,12},{12,8},{9,1... | collective-permute-start | bytes 786440 | tf_op jit(solution)/shard_map/ppermute | solution.py:33
  20.1 10.0 %collective-permute-start.10 = (bf16[64,2048]{1,0:T(8,128)(2,1)S(1)}, bf16[64,2048]{1,0:T(8,128)(2,1)S(1)}, u32[]{:S(2)}, u32[]{:S(2)}) collective-permute-start(bf16[64,2048]{1,0:T(8,128)(2,1)S(1)} %get-tuple-element.59), channel_id=1, source_target_pairs={{0,3},{1,0},{2,1},{3,2},{4,7},{5,4},{6,5},{7,6},{8,11},{9,8},{10,9... | collective-permute-start | bytes 786440 | tf_op jit(solution)/shard_map/ppermute | solution.py:29
  22.3 11.1 %collective-permute-start.4 = (bf16[64,2048]{1,0:T(8,128)(2,1)S(1)}, bf16[64,2048]{1,0:T(8,128)(2,1)S(1)}, u32[]{:S(2)}, u32[]{:S(2)}) collective-permute-start(bf16[64,2048]{1,0:T(8,128)(2,1)S(1)} %get-tuple-element.55), channel_id=1, source_target_pairs={{0,1},{1,2},{2,3},{3,0},{4,5},{5,6},{6,7},{7,4},{8,9},{9,10},{10,1... | collective-permute-start | bytes 786440 | tf_op jit(solution)/shard_map/ppermute | solution.py:29
  24.5 11.6 %collective-permute-start.8 = (bf16[64,2048]{1,0:T(8,128)(2,1)S(1)}, bf16[64,2048]{1,0:T(8,128)(2,1)S(1)}, u32[]{:S(2)}, u32[]{:S(2)}) collective-permute-start(bf16[64,2048]{1,0:T(8,128)(2,1)S(1)} %get-tuple-element.56), channel_id=1, source_target_pairs={{0,3},{1,0},{2,1},{3,2},{4,7},{5,4},{6,5},{7,6},{8,11},{9,8},{10,9... | collective-permute-start | bytes 786440 | tf_op jit(solution)/shard_map/ppermute | solution.py:29
  30.0 10.5 %collective-permute-start.9 = (bf16[64,2048]{1,0:T(8,128)(2,1)S(1)}, bf16[64,2048]{1,0:T(8,128)(2,1)S(1)}, u32[]{:S(2)}, u32[]{:S(2)}) collective-permute-start(bf16[64,2048]{1,0:T(8,128)(2,1)S(1)} %get-tuple-element.57), channel_id=1, source_target_pairs={{0,1},{1,2},{2,3},{3,0},{4,5},{5,6},{6,7},{7,4},{8,9},{9,10},{10,1... | collective-permute-start | bytes 786440 | tf_op jit(solution)/shard_map/ppermute | solution.py:29
  30.1 10.3 %collective-permute-start.11 = (bf16[64,2048]{1,0:T(8,128)(2,1)S(1)}, bf16[64,2048]{1,0:T(8,128)(2,1)S(1)}, u32[]{:S(2)}, u32[]{:S(2)}) collective-permute-start(bf16[64,2048]{1,0:T(8,128)(2,1)S(1)} %add.64), channel_id=1, source_target_pairs={{0,3},{1,0},{2,1},{3,2},{4,7},{5,4},{6,5},{7,6},{8,11},{9,8},{10,9... | collective-permute-start | bytes 786440 | tf_op jit(solution)/shard_map/ppermute | solution.py:29
  33.5 11.3 %collective-permute-start.5 = (bf16[64,2048]{1,0:T(8,128)(2,1)S(1)}, bf16[64,2048]{1,0:T(8,128)(2,1)S(1)}, u32[]{:S(2)}, u32[]{:S(2)}) collective-permute-start(bf16[64,2048]{1,0:T(8,128)(2,1)S(1)} %add.63), channel_id=1, source_target_pairs={{0,1},{1,2},{2,3},{3,0},{4,5},{5,6},{6,7},{7,4},{8,9},{9,10},{10,1... | collective-permute-start | bytes 786440 | tf_op jit(solution)/shard_map/ppermute | solution.py:29
  45.6 10.5 %collective-permute-start.12 = (bf16[64,2048]{1,0:T(8,128)(2,1)S(1)}, bf16[64,2048]{1,0:T(8,128)(2,1)S(1)}, u32[]{:S(2)}, u32[]{:S(2)}) collective-permute-start(bf16[64,2048]{1,0:T(8,128)(2,1)S(1)} %get-tuple-element.60.refs_0_), channel_id=1, source_target_pairs={{0,1},{1,2},{2,3},{3,0},{4,5},{5,6},{6,7},{7,4},{8,9},{9,10},{10,1... | collective-permute-start | bytes 786440 | tf_op jit(solution)/shard_map/ppermute | solution.py:29
  45.7 10.4 %collective-permute-start.15 = (bf16[64,2048]{1,0:T(8,128)(2,1)S(1)}, bf16[64,2048]{1,0:T(8,128)(2,1)S(1)}, u32[]{:S(2)}, u32[]{:S(2)}) collective-permute-start(bf16[64,2048]{1,0:T(8,128)(2,1)S(1)} %get-tuple-element.61.refs_1_), channel_id=1, source_target_pairs={{0,3},{1,0},{2,1},{3,2},{4,7},{5,4},{6,5},{7,6},{8,11},{9,8},{10,9... | collective-permute-start | bytes 786440 | tf_op jit(solution)/shard_map/ppermute | solution.py:29
  48.9 12.3 %collective-permute-start.14 = (bf16[64,2048]{1,0:T(8,128)(2,1)S(1)}, bf16[64,2048]{1,0:T(8,128)(2,1)S(1)}, u32[]{:S(2)}, u32[]{:S(2)}) collective-permute-start(bf16[64,2048]{1,0:T(8,128)(2,1)S(1)} %get-tuple-element.60.refs_0_), channel_id=1, source_target_pairs={{0,3},{1,0},{2,1},{3,2},{4,7},{5,4},{6,5},{7,6},{8,11},{9,8},{10,9... | collective-permute-start | bytes 786440 | tf_op jit(solution)/shard_map/ppermute | solution.py:29
  49.0 12.7 %collective-permute-start.13 = (bf16[64,2048]{1,0:T(8,128)(2,1)S(1)}, bf16[64,2048]{1,0:T(8,128)(2,1)S(1)}, u32[]{:S(2)}, u32[]{:S(2)}) collective-permute-start(bf16[64,2048]{1,0:T(8,128)(2,1)S(1)} %get-tuple-element.61.refs_1_), channel_id=1, source_target_pairs={{0,1},{1,2},{2,3},{3,0},{4,5},{5,6},{6,7},{7,4},{8,9},{9,10},{10,1... | collective-permute-start | bytes 786440 | tf_op jit(solution)/shard_map/ppermute | solution.py:29
  56.1 12.7 %collective-permute-start.16 = (bf16[64,2048]{1,0:T(8,128)(2,1)S(1)}, bf16[64,2048]{1,0:T(8,128)(2,1)S(1)}, u32[]{:S(2)}, u32[]{:S(2)}) collective-permute-start(bf16[64,2048]{1,0:T(8,128)(2,1)S(1)} %collective-permute-done.12.refs_0_), channel_id=1, source_target_pairs={{0,1},{1,2},{2,3},{3,0},{4,5},{5,6},{6,7},{7,4},{8,9},{9,10},{10,1... | collective-permute-start | bytes 786440 | tf_op jit(solution)/shard_map/ppermute | solution.py:29
  56.1 12.7 %collective-permute-start.17 = (bf16[64,2048]{1,0:T(8,128)(2,1)S(1)}, bf16[64,2048]{1,0:T(8,128)(2,1)S(1)}, u32[]{:S(2)}, u32[]{:S(2)}) collective-permute-start(bf16[64,2048]{1,0:T(8,128)(2,1)S(1)} %collective-permute-done.15.refs_3_), channel_id=1, source_target_pairs={{0,3},{1,0},{2,1},{3,2},{4,7},{5,4},{6,5},{7,6},{8,11},{9,8},{10,9... | collective-permute-start | bytes 786440 | tf_op jit(solution)/shard_map/ppermute | solution.py:29
  64.8 8.9 %collective-permute-start.19 = (bf16[128,2048]{1,0:T(8,128)(2,1)S(1)}, bf16[128,2048]{1,0:T(8,128)(2,1)S(1)}, u32[]{:S(2)}, u32[]{:S(2)}) collective-permute-start(bf16[128,2048]{1,0:T(8,128)(2,1)S(1)} %get-tuple-element.67), channel_id=1, source_target_pairs={{0,4},{4,0},{1,5},{5,1},{2,6},{6,2},{3,7},{7,3},{8,12},{12,8},{9,1... | collective-permute-start | bytes 1572872 | tf_op jit(solution)/shard_map/ppermute | solution.py:33
  75.0 8.0 %collective-permute-start.21 = (bf16[64,2048]{1,0:T(8,128)(2,1)S(1)}, bf16[64,2048]{1,0:T(8,128)(2,1)S(1)}, u32[]{:S(2)}, u32[]{:S(2)}) collective-permute-start(bf16[64,2048]{1,0:T(8,128)(2,1)S(1)} %get-tuple-element.70), channel_id=1, source_target_pairs={{0,16},{4,68},{8,24},{12,76},{16,0},{20,84},{24,8},{28,92},{32,48}... | collective-permute-start | bytes 786440 | tf_op jit(solution)/shard_map/ppermute | solution.py:53
  78.5 7.6 %collective-permute-start.23 = (bf16[64,2048]{1,0:T(8,128)(2,1)S(1)}, bf16[64,2048]{1,0:T(8,128)(2,1)S(1)}, u32[]{:S(2)}, u32[]{:S(2)}) collective-permute-start(bf16[64,2048]{1,0:T(8,128)(2,1)S(1)} %get-tuple-element.72), channel_id=1, source_target_pairs={{0,24},{4,100},{8,0},{12,108},{16,8},{20,116},{24,16},{28,124},{32... | collective-permute-start | bytes 786440 | tf_op jit(solution)/shard_map/ppermute | solution.py:53
  86.2 7.9 %collective-permute-start.26 = (bf16[64,2048]{1,0:T(8,128)(2,1)S(1)}, bf16[64,2048]{1,0:T(8,128)(2,1)S(1)}, u32[]{:S(2)}, u32[]{:S(2)}) collective-permute-start(bf16[64,2048]{1,0:T(8,128)(2,1)S(1)} %partial.2.refs_0_), channel_id=1, source_target_pairs={{0,96},{4,28},{8,104},{12,4},{16,112},{20,12},{24,120},{28,20},{32... | collective-permute-start | bytes 786440 | tf_op jit(solution)/shard_map/ppermute | solution.py:53
  90.3 10.4 %collective-permute-start.25 = (bf16[64,2048]{1,0:T(8,128)(2,1)S(1)}, bf16[64,2048]{1,0:T(8,128)(2,1)S(1)}, u32[]{:S(2)}, u32[]{:S(2)}) collective-permute-start(bf16[64,2048]{1,0:T(8,128)(2,1)S(1)} %partial.2.refs_0_), channel_id=1, source_target_pairs={{0,32},{4,12},{8,40},{12,20},{16,48},{20,28},{24,56},{28,4},{32,64... | collective-permute-start | bytes 786440 | tf_op jit(solution)/shard_map/ppermute | solution.py:53
  90.3 10.4 %collective-permute-start.24 = (bf16[64,2048]{1,0:T(8,128)(2,1)S(1)}, bf16[64,2048]{1,0:T(8,128)(2,1)S(1)}, u32[]{:S(2)}, u32[]{:S(2)}) collective-permute-start(bf16[64,2048]{1,0:T(8,128)(2,1)S(1)} %partial.2.refs_0_), channel_id=1, source_target_pairs={{0,64},{4,20},{8,72},{12,28},{16,80},{20,4},{24,88},{28,12},{32,96... | collective-permute-start | bytes 786440 | tf_op jit(solution)/shard_map/ppermute | solution.py:53
  102.2 10.5 %collective-permute-start.29 = (bf16[64,2048]{1,0:T(8,128)(2,1)S(1)}, bf16[64,2048]{1,0:T(8,128)(2,1)S(1)}, u32[]{:S(2)}, u32[]{:S(2)}) collective-permute-start(bf16[64,2048]{1,0:T(8,128)(2,1)S(1)} %get-tuple-element.73.refs_0_), channel_id=1, source_target_pairs={{0,24},{4,100},{8,0},{12,108},{16,8},{20,116},{24,16},{28,124},{32... | collective-permute-start | bytes 786440 | tf_op jit(solution)/shard_map/ppermute | solution.py:53
  102.3 10.4 %collective-permute-start.28 = (bf16[64,2048]{1,0:T(8,128)(2,1)S(1)}, bf16[64,2048]{1,0:T(8,128)(2,1)S(1)}, u32[]{:S(2)}, u32[]{:S(2)}) collective-permute-start(bf16[64,2048]{1,0:T(8,128)(2,1)S(1)} %get-tuple-element.73.refs_0_), channel_id=1, source_target_pairs={{0,16},{4,68},{8,24},{12,76},{16,0},{20,84},{24,8},{28,92},{32,48}... | collective-permute-start | bytes 786440 | tf_op jit(solution)/shard_map/ppermute | solution.py:53
  104.0 9.6 %collective-permute-start.27 = (bf16[64,2048]{1,0:T(8,128)(2,1)S(1)}, bf16[64,2048]{1,0:T(8,128)(2,1)S(1)}, u32[]{:S(2)}, u32[]{:S(2)}) collective-permute-start(bf16[64,2048]{1,0:T(8,128)(2,1)S(1)} %get-tuple-element.73.refs_0_), channel_id=1, source_target_pairs={{0,8},{4,36},{8,16},{12,44},{16,24},{20,52},{24,0},{28,60},{32,40}... | collective-permute-start | bytes 786440 | tf_op jit(solution)/shard_map/ppermute | solution.py:53
  106.0 7.6 %collective-permute-start.30 = (bf16[64,2048]{1,0:T(8,128)(2,1)S(1)}, bf16[64,2048]{1,0:T(8,128)(2,1)S(1)}, u32[]{:S(2)}, u32[]{:S(2)}) collective-permute-start(bf16[64,2048]{1,0:T(8,128)(2,1)S(1)} %get-tuple-element.73.refs_0_), channel_id=1, source_target_pairs={{0,4},{4,0},{1,5},{5,1},{2,6},{6,2},{3,7},{7,3},{8,12},{12,8},{9,1... | collective-permute-start | bytes 786440 | tf_op jit(solution)/shard_map/ppermute | solution.py:33
  117.3 11.1 %collective-permute-start.38 = (bf16[64,2048]{1,0:T(8,128)(2,1)S(1)}, bf16[64,2048]{1,0:T(8,128)(2,1)S(1)}, u32[]{:S(2)}, u32[]{:S(2)}) collective-permute-start(bf16[64,2048]{1,0:T(8,128)(2,1)S(1)} %get-tuple-element.81), channel_id=1, source_target_pairs={{0,3},{1,0},{2,1},{3,2},{4,7},{5,4},{6,5},{7,6},{8,11},{9,8},{10,9... | collective-permute-start | bytes 786440 | tf_op jit(solution)/shard_map/ppermute | solution.py:29
  120.6 11.2 %collective-permute-start.34 = (bf16[64,2048]{1,0:T(8,128)(2,1)S(1)}, bf16[64,2048]{1,0:T(8,128)(2,1)S(1)}, u32[]{:S(2)}, u32[]{:S(2)}) collective-permute-start(bf16[64,2048]{1,0:T(8,128)(2,1)S(1)} %get-tuple-element.77), channel_id=1, source_target_pairs={{0,1},{1,2},{2,3},{3,0},{4,5},{5,6},{6,7},{7,4},{8,9},{9,10},{10,1... | collective-permute-start | bytes 786440 | tf_op jit(solution)/shard_map/ppermute | solution.py:29
  122.8 11.7 %collective-permute-start.36 = (bf16[64,2048]{1,0:T(8,128)(2,1)S(1)}, bf16[64,2048]{1,0:T(8,128)(2,1)S(1)}, u32[]{:S(2)}, u32[]{:S(2)}) collective-permute-start(bf16[64,2048]{1,0:T(8,128)(2,1)S(1)} %get-tuple-element.78), channel_id=1, source_target_pairs={{0,3},{1,0},{2,1},{3,2},{4,7},{5,4},{6,5},{7,6},{8,11},{9,8},{10,9... | collective-permute-start | bytes 786440 | tf_op jit(solution)/shard_map/ppermute | solution.py:29
  128.4 10.5 %collective-permute-start.37 = (bf16[64,2048]{1,0:T(8,128)(2,1)S(1)}, bf16[64,2048]{1,0:T(8,128)(2,1)S(1)}, u32[]{:S(2)}, u32[]{:S(2)}) collective-permute-start(bf16[64,2048]{1,0:T(8,128)(2,1)S(1)} %get-tuple-element.79), channel_id=1, source_target_pairs={{0,1},{1,2},{2,3},{3,0},{4,5},{5,6},{6,7},{7,4},{8,9},{9,10},{10,1... | collective-permute-start | bytes 786440 | tf_op jit(solution)/shard_map/ppermute | solution.py:29
  128.5 10.3 %collective-permute-start.39 = (bf16[64,2048]{1,0:T(8,128)(2,1)S(1)}, bf16[64,2048]{1,0:T(8,128)(2,1)S(1)}, u32[]{:S(2)}, u32[]{:S(2)}) collective-permute-start(bf16[64,2048]{1,0:T(8,128)(2,1)S(1)} %add.66), channel_id=1, source_target_pairs={{0,3},{1,0},{2,1},{3,2},{4,7},{5,4},{6,5},{7,6},{8,11},{9,8},{10,9... | collective-permute-start | bytes 786440 | tf_op jit(solution)/shard_map/ppermute | solution.py:29
  131.9 10.9 %collective-permute-start.35 = (bf16[64,2048]{1,0:T(8,128)(2,1)S(1)}, bf16[64,2048]{1,0:T(8,128)(2,1)S(1)}, u32[]{:S(2)}, u32[]{:S(2)}) collective-permute-start(bf16[64,2048]{1,0:T(8,128)(2,1)S(1)} %add.65), channel_id=1, source_target_pairs={{0,1},{1,2},{2,3},{3,0},{4,5},{5,6},{6,7},{7,4},{8,9},{9,10},{10,1... | collective-permute-start | bytes 786440 | tf_op jit(solution)/shard_map/ppermute | solution.py:29
  144.7 10.4 %collective-permute-start.40 = (bf16[64,2048]{1,0:T(8,128)(2,1)S(1)}, bf16[64,2048]{1,0:T(8,128)(2,1)S(1)}, u32[]{:S(2)}, u32[]{:S(2)}) collective-permute-start(bf16[64,2048]{1,0:T(8,128)(2,1)S(1)} %get-tuple-element.84.refs_0_), channel_id=1, source_target_pairs={{0,1},{1,2},{2,3},{3,0},{4,5},{5,6},{6,7},{7,4},{8,9},{9,10},{10,1... | collective-permute-start | bytes 786440 | tf_op jit(solution)/shard_map/ppermute | solution.py:29
  144.7 10.4 %collective-permute-start.43 = (bf16[64,2048]{1,0:T(8,128)(2,1)S(1)}, bf16[64,2048]{1,0:T(8,128)(2,1)S(1)}, u32[]{:S(2)}, u32[]{:S(2)}) collective-permute-start(bf16[64,2048]{1,0:T(8,128)(2,1)S(1)} %get-tuple-element.85.refs_1_.refs_4_), channel_id=1, source_target_pairs={{0,3},{1,0},{2,1},{3,2},{4,7},{5,4},{6,5},{7,6},{8,11},{9,8},{10,9... | collective-permute-start | bytes 786440 | tf_op jit(solution)/shard_map/ppermute | solution.py:29
  147.9 12.3 %collective-permute-start.42 = (bf16[64,2048]{1,0:T(8,128)(2,1)S(1)}, bf16[64,2048]{1,0:T(8,128)(2,1)S(1)}, u32[]{:S(2)}, u32[]{:S(2)}) collective-permute-start(bf16[64,2048]{1,0:T(8,128)(2,1)S(1)} %get-tuple-element.84.refs_0_), channel_id=1, source_target_pairs={{0,3},{1,0},{2,1},{3,2},{4,7},{5,4},{6,5},{7,6},{8,11},{9,8},{10,9... | collective-permute-start | bytes 786440 | tf_op jit(solution)/shard_map/ppermute | solution.py:29
  147.9 12.7 %collective-permute-start.41 = (bf16[64,2048]{1,0:T(8,128)(2,1)S(1)}, bf16[64,2048]{1,0:T(8,128)(2,1)S(1)}, u32[]{:S(2)}, u32[]{:S(2)}) collective-permute-start(bf16[64,2048]{1,0:T(8,128)(2,1)S(1)} %get-tuple-element.85.refs_1_.refs_4_), channel_id=1, source_target_pairs={{0,1},{1,2},{2,3},{3,0},{4,5},{5,6},{6,7},{7,4},{8,9},{9,10},{10,1... | collective-permute-start | bytes 786440 | tf_op jit(solution)/shard_map/ppermute | solution.py:29
  155.1 12.7 %collective-permute-start.44 = (bf16[64,2048]{1,0:T(8,128)(2,1)S(1)}, bf16[64,2048]{1,0:T(8,128)(2,1)S(1)}, u32[]{:S(2)}, u32[]{:S(2)}) collective-permute-start(bf16[64,2048]{1,0:T(8,128)(2,1)S(1)} %collective-permute-done.40.refs_0_.refs_1_), channel_id=1, source_target_pairs={{0,1},{1,2},{2,3},{3,0},{4,5},{5,6},{6,7},{7,4},{8,9},{9,10},{10,1... | collective-permute-start | bytes 786440 | tf_op jit(solution)/shard_map/ppermute | solution.py:29
  155.1 12.7 %collective-permute-start.45 = (bf16[64,2048]{1,0:T(8,128)(2,1)S(1)}, bf16[64,2048]{1,0:T(8,128)(2,1)S(1)}, u32[]{:S(2)}, u32[]{:S(2)}) collective-permute-start(bf16[64,2048]{1,0:T(8,128)(2,1)S(1)} %collective-permute-done.43.refs_3_.refs_7_), channel_id=1, source_target_pairs={{0,3},{1,0},{2,1},{3,2},{4,7},{5,4},{6,5},{7,6},{8,11},{9,8},{10,9... | collective-permute-start | bytes 786440 | tf_op jit(solution)/shard_map/ppermute | solution.py:29
  173.8 8.0 %collective-permute-start.49 = (bf16[64,2048]{1,0:T(8,128)(2,1)S(1)}, bf16[64,2048]{1,0:T(8,128)(2,1)S(1)}, u32[]{:S(2)}, u32[]{:S(2)}) collective-permute-start(bf16[64,2048]{1,0:T(8,128)(2,1)S(1)} %get-tuple-element.94), channel_id=1, source_target_pairs={{0,16},{4,68},{8,24},{12,76},{16,0},{20,84},{24,8},{28,92},{32,48}... | collective-permute-start | bytes 786440 | tf_op jit(solution)/shard_map/ppermute | solution.py:53
  174.9 9.6 %collective-permute-start.50 = (bf16[64,2048]{1,0:T(8,128)(2,1)S(1)}, bf16[64,2048]{1,0:T(8,128)(2,1)S(1)}, u32[]{:S(2)}, u32[]{:S(2)}) collective-permute-start(bf16[64,2048]{1,0:T(8,128)(2,1)S(1)} %get-tuple-element.95), channel_id=1, source_target_pairs={{0,8},{4,36},{8,16},{12,44},{16,24},{20,52},{24,0},{28,60},{32,40}... | collective-permute-start | bytes 786440 | tf_op jit(solution)/shard_map/ppermute | solution.py:53
  176.9 7.6 %collective-permute-start.51 = (bf16[64,2048]{1,0:T(8,128)(2,1)S(1)}, bf16[64,2048]{1,0:T(8,128)(2,1)S(1)}, u32[]{:S(2)}, u32[]{:S(2)}) collective-permute-start(bf16[64,2048]{1,0:T(8,128)(2,1)S(1)} %get-tuple-element.96), channel_id=1, source_target_pairs={{0,24},{4,100},{8,0},{12,108},{16,8},{20,116},{24,16},{28,124},{32... | collective-permute-start | bytes 786440 | tf_op jit(solution)/shard_map/ppermute | solution.py:53
  185.5 10.4 %collective-permute-start.53 = (bf16[64,2048]{1,0:T(8,128)(2,1)S(1)}, bf16[64,2048]{1,0:T(8,128)(2,1)S(1)}, u32[]{:S(2)}, u32[]{:S(2)}) collective-permute-start(bf16[64,2048]{1,0:T(8,128)(2,1)S(1)} %partial.3.refs_0_), channel_id=1, source_target_pairs={{0,32},{4,12},{8,40},{12,20},{16,48},{20,28},{24,56},{28,4},{32,64... | collective-permute-start | bytes 786440 | tf_op jit(solution)/shard_map/ppermute | solution.py:53
  186.8 9.1 %collective-permute-start.52 = (bf16[64,2048]{1,0:T(8,128)(2,1)S(1)}, bf16[64,2048]{1,0:T(8,128)(2,1)S(1)}, u32[]{:S(2)}, u32[]{:S(2)}) collective-permute-start(bf16[64,2048]{1,0:T(8,128)(2,1)S(1)} %partial.3.refs_0_), channel_id=1, source_target_pairs={{0,64},{4,20},{8,72},{12,28},{16,80},{20,4},{24,88},{28,12},{32,96... | collective-permute-start | bytes 786440 | tf_op jit(solution)/shard_map/ppermute | solution.py:53
  196.7 7.7 %collective-permute-start.61 = (bf16[64,2048]{1,0:T(8,128)(2,1)S(1)}, bf16[64,2048]{1,0:T(8,128)(2,1)S(1)}, u32[]{:S(2)}, u32[]{:S(2)}) collective-permute-start(bf16[64,2048]{1,0:T(8,128)(2,1)S(1)} %get-tuple-element.98.own_ref), channel_id=1, source_target_pairs={{0,24},{4,100},{8,0},{12,108},{16,8},{20,116},{24,16},{28,124},{32... | collective-permute-start | bytes 786440 | tf_op jit(solution)/shard_map/ppermute | solution.py:53
  197.2 10.8 %collective-permute-start.59 = (bf16[64,2048]{1,0:T(8,128)(2,1)S(1)}, bf16[64,2048]{1,0:T(8,128)(2,1)S(1)}, u32[]{:S(2)}, u32[]{:S(2)}) collective-permute-start(bf16[64,2048]{1,0:T(8,128)(2,1)S(1)} %get-tuple-element.98.own_ref), channel_id=1, source_target_pairs={{0,16},{4,68},{8,24},{12,76},{16,0},{20,84},{24,8},{28,92},{32,48}... | collective-permute-start | bytes 786440 | tf_op jit(solution)/shard_map/ppermute | solution.py:53
  200.9 13.0 %collective-permute-start.56 = (bf16[64,2048]{1,0:T(8,128)(2,1)S(1)}, bf16[64,2048]{1,0:T(8,128)(2,1)S(1)}, u32[]{:S(2)}, u32[]{:S(2)}) collective-permute-start(bf16[64,2048]{1,0:T(8,128)(2,1)S(1)} %get-tuple-element.98.own_ref), channel_id=1, source_target_pairs={{0,4},{4,0},{1,5},{5,1},{2,6},{6,2},{3,7},{7,3},{8,12},{12,8},{9,1... | collective-permute-start | bytes 786440 | tf_op jit(solution)/shard_map/ppermute | solution.py:33
  204.4 9.7 %collective-permute-start.62 = (bf16[64,2048]{1,0:T(8,128)(2,1)S(1)}, bf16[64,2048]{1,0:T(8,128)(2,1)S(1)}, u32[]{:S(2)}, u32[]{:S(2)}) collective-permute-start(bf16[64,2048]{1,0:T(8,128)(2,1)S(1)} %collective-permute-done.61.own_ref), channel_id=1, source_target_pairs={{0,4},{4,0},{1,5},{5,1},{2,6},{6,2},{3,7},{7,3},{8,12},{12,8},{9,1... | collective-permute-start | bytes 786440 | tf_op jit(solution)/shard_map/ppermute | solution.py:33
  209.6 15.8 %collective-permute-start.55 = (f32[16,2048]{1,0:T(8,128)S(1)}, f32[16,2048]{1,0:T(8,128)S(1)}, u32[]{:S(2)}, u32[]{:S(2)}) collective-permute-start(f32[16,2048]{1,0:T(8,128)S(1)} %get-tuple-element.97), channel_id=1, source_target_pairs={{0,0},{4,16},{8,32},{12,20},{16,64},{20,24},{24,96},{28,28},{32,4}... | collective-permute-start | bytes 393224 | tf_op jit(solution)/shard_map/ppermute | solution.py:61
  (21 other events, 278.0 us)
where the time goes:
time: 236 us; the launch traced here: 234 us
  waiting for transfers between devices  92 us (39%)
  starting transfers between devices  77.9 us (33%)
  Pallas kernels  60.3 us (26%)
  local copies, waits for them, and re-layouts  2.73 us (1%)
    ppermute x30, starting transfers between devices, shift_x(): return lax.ppermute(value, 'x', [(i, (i + step) % 4) for i in range(4)])  47.1 us
    ppermute x18, waiting for transfers between devices, shift_mixed(): return lax.ppermute(value, ATOM, pairs_of(target))  46.3 us
    ppermute x30, waiting for transfers between devices, shift_x(): return lax.ppermute(value, 'x', [(i, (i + step) % 4) for i in range(4)])  41.2 us
    ppermute x18, starting transfers between devices, shift_mixed(): return lax.ppermute(value, ATOM, pairs_of(target))  23.3 us
    pallas_call x6, Pallas kernels, decode_blocks(): pl.pallas_call(functools.partial(decode_kernel, size, len(coded)), in_spe...  18.9 us
    pallas_call x8, Pallas kernels, encode_block(): pl.pallas_call(functools.partial(encode_kernel, size, len(own), k), in_sp...  18.3 us
    pallas_call x1, Pallas kernels, gradient(): pl.pallas_call(gradient_kernel, in_specs=[whole()] * 6, out_specs=[whole(...  6.03 us
  transfers between devices with their start and end apart: 66, of which 34 were waited for; matrix products, arithmetic and copies ran while one was open for 0% of the time, Pallas kernels for 20%

commit v1 on v0

--- a/solution.py
+++ b/solution.py
@@ -108,59 +108,72 @@
                 copy.start()
 
 
-def load_kernel(dict_ref, out_ref, sem):
+def load_kernel(index_ref, dict_ref, out_ref, sem):
     copy = pltpu.make_async_copy(dict_ref, out_ref, sem)
     copy.start()
     copy.wait()
 
 
-def load(dictionary):
+def load(index, dictionary):
     return pl.pallas_call(
         load_kernel,
-        in_specs=[pl.BlockSpec(memory_space=pltpu.HBM)],
+        in_specs=[scalars(), pl.BlockSpec(memory_space=pltpu.HBM)],
         out_specs=whole(),
         out_shape=pltpu.VMEM(dictionary.shape, BF),
         scratch_shapes=[pltpu.SemaphoreType.DMA],
         compiler_params=params(10),
         cost_estimate=cost(0, dictionary.size * 2),
         name="load",
-    )(pltpu.with_memory_space_constraint(dictionary, pltpu.HBM))
-
-
-def encode_kernel(size, count, k, index_ref, *refs):
+    )(index, pltpu.with_memory_space_constraint(dictionary, pltpu.HBM))
+
+
+def encode_kernel(size, ks, counted, kinds, index_ref, *refs):
+    count = 4 if counted else len(ks)
     own, other = refs[:count], refs[count : 2 * count]
-    dict_ref, low_ref, high_ref, left, sems = refs[2 * count :]
-    half = left.shape[0] // 2
-    own_at = index_ref[k, 0] if count > 1 else 0
-    other_at = index_ref[k, 1] if count > 1 else 0
+    dict_ref, outs = refs[2 * count], refs[2 * count + 1 : 2 * count + 1 + len(kinds)]
+    left, sems = refs[-2:]
+    half = own[0].shape[0]
     for wait in (False, True):
-        fetch(own_at, own, left.at[pl.ds(0, half)], sems.at[0], wait)
-        fetch(other_at, other, left.at[pl.ds(half, half)], sems.at[1], wait)
+        for b, k in enumerate(ks):
+            low, high = pl.ds(2 * b * half, half), pl.ds((2 * b + 1) * half, half)
+            if counted:
+                fetch(index_ref[k, 0], own, left.at[low], sems.at[b, 0], wait)
+                fetch(index_ref[k, 1], other, left.at[high], sems.at[b, 1], wait)
+            elif wait:
+                left[low, :] = own[b][...]
+                left[high, :] = other[b][...]
 
     @pl.loop(0, dict_ref.shape[1] // size)
     def _(n):
         part = pl.ds(pl.multiple_of(n * size, size), size)
         out = jnp.dot(left[...], dict_ref[:, part], preferred_element_type=F32)
-        low_ref[:, part] = out[:half].astype(low_ref.dtype)
-        high_ref[:, part] = out[half:].astype(high_ref.dtype)
-
-
-def encode_block(own, other, index, k, dictionary, size):
+        for b, ref in enumerate(outs):
+            ref[:, part] = out[b * half : (b + 1) * half].astype(ref.dtype)
+
+
+def encode_block(own, other, index, ks, dictionary, size):
     half, feats = own[0].shape
     atoms = dictionary.shape[1]
-    low = BF if k in (2, 3) else F32
-    high = BF if k in (1, 2) else F32
-    return pl.pallas_call(
-        functools.partial(encode_kernel, size, len(own), k),
-        in_specs=[scalars()] + [anywhere()] * (2 * len(own)) + [whole()],
-        out_specs=[whole()] * 2,
-        out_shape=[shaped(half, atoms, low), shaped(half, atoms, high)],
+    kinds = []
+    for k in ks:
+        kinds += [BF if k in (2, 3) else F32, BF if k in (1, 2) else F32]
+    counted = index is not None
+    rows = 2 * half * len(ks)
+    if not counted:
+        index = jnp.zeros((1, 1), jnp.int32)
+    return pl.pallas_call(
+        functools.partial(encode_kernel, size, ks, counted, kinds),
+        in_specs=[scalars()]
+        + [anywhere() if counted else whole()] * (2 * len(own))
+        + [whole()],
+        out_specs=[whole()] * len(kinds),
+        out_shape=[shaped(half, atoms, kind) for kind in kinds],
         scratch_shapes=[
-            pltpu.VMEM((2 * half, feats), BF),
-            pltpu.SemaphoreType.DMA((2,)),
+            pltpu.VMEM((rows, feats), BF),
+            pltpu.SemaphoreType.DMA((len(ks), 2)),
         ],
-        compiler_params=params(12),
-        cost_estimate=cost(4 * half * feats * atoms, 2 * feats * atoms),
+        compiler_params=params(16),
+        cost_estimate=cost(2 * rows * feats * atoms, 2 * feats * atoms),
         name="encode",
     )(index, *own, *other, in_vmem(dictionary))
 
@@ -215,7 +228,7 @@
         functools.partial(finish_kernel, last),
         in_specs=[scalars()] + [whole()] * (7 if last else 6),
         out_specs=[whole()] * 3,
-        out_shape=[shaped(2 * half, atoms, F32)] + [shaped(half, atoms, BF)] * 2,
+        out_shape=[pltpu.VMEM((2 * half, atoms), F32)] + [shaped(half, atoms, BF)] * 2,
         compiler_params=params(12),
         cost_estimate=cost(16 * half * atoms, 32 * half * atoms),
         name="finish",
@@ -224,13 +237,11 @@
 
 
 def decode_kernel(size, count, *refs):
-    coded, dict_ref, keeps = refs[:count], refs[count], refs[count + 1 : -2]
+    coded, dict_ref, keeps = refs[: 2 * count], refs[2 * count], refs[2 * count + 1 : -2]
     send_ref, left = refs[-2:]
-    base = 0
-    for piece in coded:
-        left[pl.ds(base, piece.shape[0]), :] = piece[...]
-        base += piece.shape[0]
-    half = keeps[0].shape[0]
+    half = coded[0].shape[0]
+    for b, piece in enumerate(coded):
+        left[pl.ds(b * half, half), :] = piece[...]
 
     @pl.loop(0, dict_ref.shape[0] // size)
     def _(n):
@@ -239,48 +250,42 @@
             left[...], dict_ref[part, :], (((1,), (1,)), ((), ())), preferred_element_type=F32
         )
         for b, keep in enumerate(keeps):
-            keep[:, part] = recon[2 * b * half : (2 * b + 1) * half]
-            send_ref[pl.ds(b * half, half), part] = recon[
-                (2 * b + 1) * half : (2 * b + 2) * half
-            ].astype(BF)
-
-
-def decode_blocks(coded, dictionary, half, size):
+            keep[:, part] = recon[b * half : (b + 1) * half]
+        send_ref[:, part] = recon[count * half :].astype(BF)
+
+
+def decode_blocks(low, high, dictionary, size):
     feats, atoms = dictionary.shape
-    rows = sum(piece.shape[0] for piece in coded)
-    count = rows // 2 // half
+    half, count = low[0].shape[0], len(low)
+    rows = 2 * count * half
     outs = pl.pallas_call(
-        functools.partial(decode_kernel, size, len(coded)),
-        in_specs=[whole()] * (len(coded) + 1),
+        functools.partial(decode_kernel, size, count),
+        in_specs=[whole()] * (2 * count + 1),
         out_specs=[whole()] * (count + 1),
         out_shape=[shaped(half, feats, F32)] * count + [shaped(rows // 2, feats, BF)],
-        scratch_shapes=[
-            pltpu.VMEM((rows, atoms), BF),
-        ],
-        compiler_params=params(12),
+        scratch_shapes=[pltpu.VMEM((rows, atoms), BF)],
+        compiler_params=params(16),
         cost_estimate=cost(2 * rows * feats * atoms, 2 * feats * atoms),
         name="decode",
-    )(*coded, in_vmem(dictionary))
+    )(*low, *high, in_vmem(dictionary))
     return outs[:-1], outs[-1]
 
 
 def route_kernel(index_ref, *refs):
-    keeps, (sent_own, sent_pair, sent_far), outs = refs[:4], refs[4:7], refs[7:]
+    keeps, (sent_own, sent_down, sent_rest), outs = refs[:4], refs[4:7], refs[7:]
     half = outs[0].shape[0]
-    sources = [(sent_own, 0), (sent_pair, 0), (sent_far, 0), (sent_pair, half)]
+    sources = [(sent_own, 0), (sent_rest, 0), (sent_rest, half), (sent_down, 0)]
     for j in range(4):
         source, base = sources[j]
-
-        @pl.loop(0, half // STRIP)
-        def _(i):
-            here = strip(i)
-            there = pl.ds(pl.multiple_of(base + i * STRIP, STRIP), STRIP)
-            value = (keeps[j][here, :] + source[there, :].astype(F32)).astype(BF)
-            for k in range(4):
-
-                @pl.when(index_ref[k, 2] == j)
-                def _():
-                    outs[k][here, :] = value
+        for k in range(4):
+
+            @pl.when(index_ref[k, 2] == j)
+            def _():
+                @pl.loop(0, half // STRIP)
+                def _(i):
+                    there = pl.ds(pl.multiple_of(base + i * STRIP, STRIP), STRIP)
+                    value = keeps[j][strip(i), :] + source[there, :].astype(F32)
+                    outs[k][strip(i), :] = value.astype(BF)
 
 
 def route(index, keeps, sent):
@@ -293,7 +298,7 @@
         compiler_params=params(12),
         cost_estimate=cost(8 * half * feats, 32 * half * feats),
         name="route",
-    )(index, *keeps, *sent)
+    )(index, *(in_vmem(keep) for keep in keeps), *sent)
 
 
 def total_of(pieces, here):
@@ -423,7 +428,7 @@
         gradient_kernel,
         in_specs=[whole()] * 6,
         out_specs=[whole()] * 2,
-        out_shape=[pltpu.VMEM((feats, atoms), F32), shaped(1, atoms, F32)],
+        out_shape=[pltpu.VMEM((feats, atoms), F32), pltpu.VMEM((1, atoms), F32)],
         compiler_params=params(30),
         cost_estimate=cost(2 * rows * feats * atoms, 6 * feats * atoms),
         name="gradient",
@@ -465,7 +470,26 @@
         compiler_params=params(16),
         cost_estimate=cost(feats * atoms, feats * atoms * 2),
         name="scale",
-    )(in_vmem(moved), *squares)
+    )(in_vmem(moved), *(in_vmem(square) for square in squares))
+
+
+def store_kernel(value_ref, out_ref, sem):
+    copy = pltpu.make_async_copy(value_ref, out_ref, sem)
+    copy.start()
+    copy.wait()
+
+
+def store(value):
+    return pl.pallas_call(
+        store_kernel,
+        in_specs=[whole()],
+        out_specs=pl.BlockSpec(memory_space=pltpu.HBM),
+        out_shape=jax.ShapeDtypeStruct(value.shape, value.dtype),
+        scratch_shapes=[pltpu.SemaphoreType.DMA],
+        compiler_params=params(4),
+        cost_estimate=cost(0, 4 * value.size),
+        name="store",
+    )(in_vmem(value))
 
 
 def step(activations, dictionary):
@@ -492,22 +516,21 @@
     other_act = [act_of(1 - core, x), None, None, None]
     for k in (2, 1, 3):
         own_act[k] = shift_x(act_of(core, lax.rem(x + k, 4)), k)
-    dictionary = load(dictionary)
+    dictionary = load(index, dictionary)
     for k in (1, 3, 2):
         other_act[k] = other_core(own_act[k])
 
     def encode(source, before):
-        def part(k):
-            own, other = source(k)
-            size = 512 if k == 0 else 1024
-            return encode_block(own, other, index, k, dictionary, size)
+        def part(*ks):
+            own, other = source(ks)
+            size = 512 if ks == (0,) else 1024
+            return encode_block(own, other, None if before is None else index, ks, dictionary, size)
 
         far_low, far_high = part(2)
         far_low = shift_x(far_low, 1)
         far_high = shift_x(far_high, -1)
-        up_low, up_high = part(1)
+        up_low, up_high, down_low, down_high = part(1, 3)
         up_high = shift_x(up_high, 1)
-        down_low, down_high = part(3)
         down_low = shift_x(down_low, -1)
         up_low = shift_x(add(up_low, far_low), 1)
         down_high = shift_x(add(down_high, far_high), -1)
@@ -527,10 +550,15 @@
 
     def residual_of(coded):
         keeps, sent = [None] * 4, []
-        for blocks in ((0,), (1, 3), (2,)):
-            pieces = [piece for j in blocks for piece in coded[j]]
-            kept, send = decode_blocks(pieces, dictionary, half, 1024 if blocks == (2,) else 512)
-            for j, keep in zip(blocks, kept):
+        groups = (((0,), (0,)), ((1,), (3,)), ((3, 2), (1, 2)))
+        for g, (low, high) in enumerate(groups):
+            kept, send = decode_blocks(
+                [coded[j][0] for j in low],
+                [coded[j][1] for j in high],
+                dictionary,
+                1024 if g == 2 else 512,
+            )
+            for j, keep in zip(low, kept):
                 keeps[j] = keep
             sent.append(other_core(send))
         routed = route(index, keeps, sent)
@@ -551,12 +579,15 @@
         return mine, own, other
 
     codes = None
-    source = lambda k: (own_act[(4 - k) % 4 :][:1], other_act[(4 - k) % 4 :][:1])
+    source = lambda ks: (
+        [own_act[(4 - k) % 4] for k in ks],
+        [other_act[(4 - k) % 4] for k in ks],
+    )
     for _ in range(ITERS):
         codes, coded = encode(source, codes)
         coded = gather(coded)
         mine, own, other = residual_of(coded)
-        source = lambda k, own=own, other=other: (own, other)
+        source = lambda ks, own=own, other=other: (own, other)
 
     residual = to_owner(mine)
     arranged = arrange(index, coded)
@@ -568,6 +599,8 @@
     for k in (2, 1, 3):
         squares.append(shift_x(square, k))
     new_dictionary = scale(moved, squares)
+    codes = store(codes)
+    residual = store(residual)
     return (codes, residual, new_dictionary)
 
 

time: 236 us -> 236 us (level)
  waiting for transfers between devices: 92 us -> 99 us
  Pallas kernels: 60.3 us -> 56.3 us
    ppermute x30, waiting for transfers between devices: 41.2 us -> 48.1 us  [shift_x(): return lax.ppermute(value, 'x', [(i, (i + step) % 4) for i in range(4)])]
  transfers between devices with their start and end apart: 66 -> 66, of which waited for: 34 -> 38; matrix products, arithmetic and copies ran while one was open for 0% -> 0% of each run, Pallas kernels for 20% -> 17%
where the time goes in v1:
time: 236 us; the launch traced here: 234 us
  waiting for transfers between devices  99 us (42%)
  starting transfers between devices  76.3 us (32%)
  Pallas kernels  56.3 us (24%)
    ppermute x30, waiting for transfers between devices, shift_x(): return lax.ppermute(value, 'x', [(i, (i + step) % 4) for i in range(4)])  48.1 us
    ppermute x18, waiting for transfers between devices, shift_mixed(): return lax.ppermute(value, ATOM, pairs_of(target))  46.3 us
    ppermute x30, starting transfers between devices, shift_x(): return lax.ppermute(value, 'x', [(i, (i + step) % 4) for i in range(4)])  45.4 us
    ppermute x18, starting transfers between devices, shift_mixed(): return lax.ppermute(value, ATOM, pairs_of(target))  23.6 us
    pallas_call x6, Pallas kernels, decode_blocks(): pl.pallas_call(functools.partial(decode_kernel, size, count), in_specs=[w...  18.8 us
    pallas_call x6, Pallas kernels, encode_block(): pl.pallas_call(functools.partial(encode_kernel, size, ks, counted, kinds)...  14.3 us
    pallas_call x1, Pallas kernels, gradient(): pl.pallas_call(gradient_kernel, in_specs=[whole()] * 6, out_specs=[whole(...  5.43 us
  transfers between devices with their start and end apart: 66, of which 38 were waited for; matrix products, arithmetic and copies ran while one was open for 0% of the time, Pallas kernels for 17%

profile of v1, /device:TPU:24, one launch (start us, length us, event | category | flops | bytes accessed | tf_op | source)
XLA Modules:
  0.0 234.4 jit_solution(15676518906294830304)
XLA Ops:
  2.0 3.1 %collective-permute-start.4 = (bf16[64,2048]{1,0:T(8,128)(2,1)S(1)}, bf16[64,2048]{1,0:T(8,128)(2,1)S(1)}, u32[]{:S(2)}, u32[]{:S(2)}) collective-permute-start(bf16[64,2048]{1,0:T(8,128)(2,1)S(1)} %get-tuple-element.101), channel_id=1, source_target_pairs={{0,2},{1,3},{2,0},{3,1},{4,6},{5,7},{6,4},{7,5},{8,10},{9,11},{10,... | collective-permute-start | bytes 786440 | tf_op jit(solution)/shard_map/ppermute | solution.py:29
  7.2 5.6 %collective-permute-done.4.refs_0_.refs_6_ = bf16[64,2048]{1,0:T(8,128)(2,1)S(1)} collective-permute-done((bf16[64,2048]{1,0:T(8,128)(2,1)S(1)}, bf16[64,2048]{1,0:T(8,128)(2,1)S(1)}, u32[]{:S(2)}, u32[]{:S(2)}) %collective-permute-start.4) | collective-permute-done | bytes 262176 | tf_op jit(solution)/shard_map/ppermute | solution.py:29
  12.9 4.5 %collective-permute-done.refs_0_.refs_7_ = bf16[64,2048]{1,0:T(8,128)(2,1)S(1)} collective-permute-done((bf16[64,2048]{1,0:T(8,128)(2,1)S(1)}, bf16[64,2048]{1,0:T(8,128)(2,1)S(1)}, u32[]{:S(2)}, u32[]{:S(2)}) %collective-permute-start) | collective-permute-done | bytes 262176 | tf_op jit(solution)/shard_map/ppermute | solution.py:29
  17.9 4.0 %load.1.refs_2_.refs_4_.refs_8_.refs_5_ = bf16[2048,2048]{1,0:T(8,128)(2,1)S(1)} custom-call(s32[5,4]{1,0:T(8,128)S(1)} %pad_add_fusion.index_ref, bf16[2048,2048]{1,0:T(8,128)(2,1)} %dict_ref.1), custom_call_target="tpu_custom_call" | custom-call | bytes 8388608 | tf_op jit(solution)/shard_map/load/pallas_call | solution.py:118
  26.8 2.7 %encode.7 = (f32[64,2048]{1,0:T(8,128)S(1)}, bf16[64,2048]{1,0:T(8,128)(2,1)S(1)}, bf16[64,2048]{1,0:T(8,128)(2,1)S(1)}, f32[64,2048]{1,0:T(8,128)S(1)}) custom-call(s32[1,1]{1,0:T(1,128)} %constant.39.clone.1.index_ref, bf16[64,2048]{1,0:T(8,128)(2,1)S(1)} %collective-permute-done.refs_0_.refs_7_, ...), custom_call_target="tpu_custom_call" | custom-call | flops 2147483648 | bytes 8388608 | tf_op jit(solution)/shard_map/encode/pallas_call | solution.py:164
  34.2 3.1 %collective-permute-start.11 = (bf16[64,2048]{1,0:T(8,128)(2,1)S(1)}, bf16[64,2048]{1,0:T(8,128)(2,1)S(1)}, u32[]{:S(2)}, u32[]{:S(2)}) collective-permute-start(bf16[64,2048]{1,0:T(8,128)(2,1)S(1)} %add.64), channel_id=1, source_target_pairs={{0,3},{1,0},{2,1},{3,2},{4,7},{5,4},{6,5},{7,6},{8,11},{9,8},{10,9... | collective-permute-start | bytes 786440 | tf_op jit(solution)/shard_map/ppermute | solution.py:29
  41.4 3.9 %collective-permute-done.7.refs_2_ = bf16[64,2048]{1,0:T(8,128)(2,1)S(1)} collective-permute-done((bf16[64,2048]{1,0:T(8,128)(2,1)S(1)}, bf16[64,2048]{1,0:T(8,128)(2,1)S(1)}, u32[]{:S(2)}, u32[]{:S(2)}) %collective-permute-start.7) | collective-permute-done | bytes 262176 | tf_op jit(solution)/shard_map/ppermute | solution.py:29
  46.6 2.9 %collective-permute-start.13 = (bf16[64,2048]{1,0:T(8,128)(2,1)S(1)}, bf16[64,2048]{1,0:T(8,128)(2,1)S(1)}, u32[]{:S(2)}, u32[]{:S(2)}) collective-permute-start(bf16[64,2048]{1,0:T(8,128)(2,1)S(1)} %get-tuple-element.61.refs_1_), channel_id=1, source_target_pairs={{0,3},{1,0},{2,1},{3,2},{4,7},{5,4},{6,5},{7,6},{8,11},{9,8},{10,9... | collective-permute-start | bytes 786440 | tf_op jit(solution)/shard_map/ppermute | solution.py:29
  51.5 4.4 %collective-permute-done.12.refs_0_ = bf16[64,2048]{1,0:T(8,128)(2,1)S(1)} collective-permute-done((bf16[64,2048]{1,0:T(8,128)(2,1)S(1)}, bf16[64,2048]{1,0:T(8,128)(2,1)S(1)}, u32[]{:S(2)}, u32[]{:S(2)}) %collective-permute-start.12) | collective-permute-done | bytes 262176 | tf_op jit(solution)/shard_map/ppermute | solution.py:29
  56.1 3.7 %collective-permute-start.17 = (bf16[64,2048]{1,0:T(8,128)(2,1)S(1)}, bf16[64,2048]{1,0:T(8,128)(2,1)S(1)}, u32[]{:S(2)}, u32[]{:S(2)}) collective-permute-start(bf16[64,2048]{1,0:T(8,128)(2,1)S(1)} %collective-permute-done.13.refs_1_), channel_id=1, source_target_pairs={{0,3},{1,0},{2,1},{3,2},{4,7},{5,4},{6,5},{7,6},{8,11},{9,8},{10,9... | collective-permute-start | bytes 786440 | tf_op jit(solution)/shard_map/ppermute | solution.py:29
  61.7 3.5 %collective-permute-done.15.refs_1_ = bf16[64,2048]{1,0:T(8,128)(2,1)S(1)} collective-permute-done((bf16[64,2048]{1,0:T(8,128)(2,1)S(1)}, bf16[64,2048]{1,0:T(8,128)(2,1)S(1)}, u32[]{:S(2)}, u32[]{:S(2)}) %collective-permute-start.15) | collective-permute-done | bytes 262176 | tf_op jit(solution)/shard_map/ppermute | solution.py:29
  65.2 2.6 %decode.8 = (f32[64,2048]{1,0:T(8,128)S(1)}, f32[64,2048]{1,0:T(8,128)S(1)}, bf16[128,2048]{1,0:T(8,128)(2,1)S(1)}) custom-call(bf16[64,2048]{1,0:T(8,128)(2,1)S(1)} %collective-permute-done.14.refs_0_, bf16[64,2048]{1,0:T(8,128)(2,1)S(1)} %collective-permute-done.15.refs_1_, bf16[64,2048]{1,0:T(8,128)(2,1)S(1)} %collective-permute-done.16.refs_2_, ...), custom_call_target="tpu_custom_call" | custom-call | flops 2147483648 | bytes 8388608 | tf_op jit(solution)/shard_map/decode/pallas_call | solution.py:261
  67.9 3.4 %decode.6 = (f32[64,2048]{1,0:T(8,128)S(1)}, bf16[64,2048]{1,0:T(8,128)(2,1)S(1)}) custom-call(bf16[64,2048]{1,0:T(8,128)(2,1)S(1)} %get-tuple-element.60.refs_0_, bf16[64,2048]{1,0:T(8,128)(2,1)S(1)} %get-tuple-element.61.refs_1_, bf16[2048,2048]{1,0:T(8,128)(2,1)S(1)} %load.1.refs_2_.refs_4_.refs_8_.refs_5_), custom_call_target="tpu_custom_call" | custom-call | flops 1073741824 | bytes 8388608 | tf_op jit(solution)/shard_map/decode/pallas_call | solution.py:261
  71.9 3.4 %decode.7 = (f32[64,2048]{1,0:T(8,128)S(1)}, bf16[64,2048]{1,0:T(8,128)(2,1)S(1)}) custom-call(bf16[64,2048]{1,0:T(8,128)(2,1)S(1)} %collective-permute-done.12.refs_0_, bf16[64,2048]{1,0:T(8,128)(2,1)S(1)} %collective-permute-done.13.refs_1_, bf16[2048,2048]{1,0:T(8,128)(2,1)S(1)} %load.1.refs_2_.refs_4_.refs_8_.refs_5_), custom_call_target="tpu_custom_call" | custom-call | flops 1073741824 | bytes 8388608 | tf_op jit(solution)/shard_map/decode/pallas_call | solution.py:261
  79.3 2.2 collective-permute-start.22
  81.6 4.5 %collective-permute-done.21.refs_1_ = bf16[64,2048]{1,0:T(8,128)(2,1)S(1)} collective-permute-done((bf16[64,2048]{1,0:T(8,128)(2,1)S(1)}, bf16[64,2048]{1,0:T(8,128)(2,1)S(1)}, u32[]{:S(2)}, u32[]{:S(2)}) %collective-permute-start.21) | collective-permute-done | bytes 262176 | tf_op jit(solution)/shard_map/ppermute | solution.py:53
  86.3 2.8 %collective-permute-done.23.refs_3_ = bf16[64,2048]{1,0:T(8,128)(2,1)S(1)} collective-permute-done((bf16[64,2048]{1,0:T(8,128)(2,1)S(1)}, bf16[64,2048]{1,0:T(8,128)(2,1)S(1)}, u32[]{:S(2)}, u32[]{:S(2)}) %collective-permute-start.23) | collective-permute-done | bytes 262176 | tf_op jit(solution)/shard_map/ppermute | solution.py:53
  89.3 4.1 %collective-permute-start.26 = (bf16[64,2048]{1,0:T(8,128)(2,1)S(1)}, bf16[64,2048]{1,0:T(8,128)(2,1)S(1)}, u32[]{:S(2)}, u32[]{:S(2)}) collective-permute-start(bf16[64,2048]{1,0:T(8,128)(2,1)S(1)} %partial.2.refs_0_), channel_id=1, source_target_pairs={{0,96},{4,28},{8,104},{12,4},{16,112},{20,12},{24,120},{28,20},{32... | collective-permute-start | bytes 786440 | tf_op jit(solution)/shard_map/ppermute | solution.py:53
  95.2 2.0 collective-permute-done.26.refs_3_
  97.3 6.5 %collective-permute-done.25.refs_2_ = bf16[64,2048]{1,0:T(8,128)(2,1)S(1)} collective-permute-done((bf16[64,2048]{1,0:T(8,128)(2,1)S(1)}, bf16[64,2048]{1,0:T(8,128)(2,1)S(1)}, u32[]{:S(2)}, u32[]{:S(2)}) %collective-permute-start.25) | collective-permute-done | bytes 262176 | tf_op jit(solution)/shard_map/ppermute | solution.py:53
  107.1 2.0 collective-permute-start.27
  109.1 6.7 %collective-permute-done.29.refs_3_ = bf16[64,2048]{1,0:T(8,128)(2,1)S(1)} collective-permute-done((bf16[64,2048]{1,0:T(8,128)(2,1)S(1)}, bf16[64,2048]{1,0:T(8,128)(2,1)S(1)}, u32[]{:S(2)}, u32[]{:S(2)}) %collective-permute-start.29) | collective-permute-done | bytes 262176 | tf_op jit(solution)/shard_map/ppermute | solution.py:53
  118.2 2.2 encode.11
  121.2 2.5 %collective-permute-start.38 = (bf16[64,2048]{1,0:T(8,128)(2,1)S(1)}, bf16[64,2048]{1,0:T(8,128)(2,1)S(1)}, u32[]{:S(2)}, u32[]{:S(2)}) collective-permute-start(bf16[64,2048]{1,0:T(8,128)(2,1)S(1)} %get-tuple-element.81), channel_id=1, source_target_pairs={{0,3},{1,0},{2,1},{3,2},{4,7},{5,4},{6,5},{7,6},{8,11},{9,8},{10,9... | collective-permute-start | bytes 786440 | tf_op jit(solution)/shard_map/ppermute | solution.py:29
  123.7 3.4 %encode.10 = (f32[64,2048]{1,0:T(8,128)S(1)}, bf16[64,2048]{1,0:T(8,128)(2,1)S(1)}, bf16[64,2048]{1,0:T(8,128)(2,1)S(1)}, f32[64,2048]{1,0:T(8,128)S(1)}) custom-call(s32[5,4]{1,0:T(8,128)S(1)} %pad_add_fusion.index_ref, bf16[64,2048]{1,0:T(8,128)(2,1)S(1)} %get-tuple-element.73.refs_0_, bf16[64,2048]{1,0:T(8,128)(2,1)S(1)} %collective-permute-done.27.refs_1_, ...), custom_call_target="tpu_custom_call" | custom-call | flops 2147483648 | bytes 8388608 | tf_op jit(solution)/shard_map/encode/pallas_call | solution.py:164
  130.3 3.7 %collective-permute-start.39 = (bf16[64,2048]{1,0:T(8,128)(2,1)S(1)}, bf16[64,2048]{1,0:T(8,128)(2,1)S(1)}, u32[]{:S(2)}, u32[]{:S(2)}) collective-permute-start(bf16[64,2048]{1,0:T(8,128)(2,1)S(1)} %add.66), channel_id=1, source_target_pairs={{0,3},{1,0},{2,1},{3,2},{4,7},{5,4},{6,5},{7,6},{8,11},{9,8},{10,9... | collective-permute-start | bytes 786440 | tf_op jit(solution)/shard_map/ppermute | solution.py:29
  134.0 2.6 %encode.9 = (f32[64,2048]{1,0:T(8,128)S(1)}, f32[64,2048]{1,0:T(8,128)S(1)}) custom-call(s32[5,4]{1,0:T(8,128)S(1)} %pad_add_fusion.index_ref, bf16[64,2048]{1,0:T(8,128)(2,1)S(1)} %get-tuple-element.73.refs_0_, bf16[64,2048]{1,0:T(8,128)(2,1)S(1)} %collective-permute-done.27.refs_1_, bf16[64,2048]{1,0:T(8,128)(2,1)S(1)} %collective-permute-done.28.refs_2_, ...), custom_call_target="tpu_custom_call" | custom-call | flops 1073741824 | bytes 8388608 | tf_op jit(solution)/shard_map/encode/pallas_call | solution.py:164
  136.6 2.7 %collective-permute-done.37.refs_4_ = bf16[64,2048]{1,0:T(8,128)(2,1)S(1)} collective-permute-done((bf16[64,2048]{1,0:T(8,128)(2,1)S(1)}, bf16[64,2048]{1,0:T(8,128)(2,1)S(1)}, u32[]{:S(2)}, u32[]{:S(2)}) %collective-permute-start.37) | collective-permute-done | bytes 262176 | tf_op jit(solution)/shard_map/ppermute | solution.py:29
  139.3 3.9 %collective-permute-done.35.refs_2_ = bf16[64,2048]{1,0:T(8,128)(2,1)S(1)} collective-permute-done((bf16[64,2048]{1,0:T(8,128)(2,1)S(1)}, bf16[64,2048]{1,0:T(8,128)(2,1)S(1)}, u32[]{:S(2)}, u32[]{:S(2)}) %collective-permute-start.35) | collective-permute-done | bytes 262176 | tf_op jit(solution)/shard_map/ppermute | solution.py:29
  144.3 3.2 %collective-permute-start.41 = (bf16[64,2048]{1,0:T(8,128)(2,1)S(1)}, bf16[64,2048]{1,0:T(8,128)(2,1)S(1)}, u32[]{:S(2)}, u32[]{:S(2)}) collective-permute-start(bf16[64,2048]{1,0:T(8,128)(2,1)S(1)} %get-tuple-element.85.refs_1_.refs_4_), channel_id=1, source_target_pairs={{0,3},{1,0},{2,1},{3,2},{4,7},{5,4},{6,5},{7,6},{8,11},{9,8},{10,9... | collective-permute-start | bytes 786440 | tf_op jit(solution)/shard_map/ppermute | solution.py:29
  149.5 5.0 %collective-permute-done.40.refs_0_.refs_1_ = bf16[64,2048]{1,0:T(8,128)(2,1)S(1)} collective-permute-done((bf16[64,2048]{1,0:T(8,128)(2,1)S(1)}, bf16[64,2048]{1,0:T(8,128)(2,1)S(1)}, u32[]{:S(2)}, u32[]{:S(2)}) %collective-permute-start.40) | collective-permute-done | bytes 262176 | tf_op jit(solution)/shard_map/ppermute | solution.py:29
  154.6 3.3 %collective-permute-start.45 = (bf16[64,2048]{1,0:T(8,128)(2,1)S(1)}, bf16[64,2048]{1,0:T(8,128)(2,1)S(1)}, u32[]{:S(2)}, u32[]{:S(2)}) collective-permute-start(bf16[64,2048]{1,0:T(8,128)(2,1)S(1)} %collective-permute-done.41.refs_1_.refs_7_), channel_id=1, source_target_pairs={{0,3},{1,0},{2,1},{3,2},{4,7},{5,4},{6,5},{7,6},{8,11},{9,8},{10,9... | collective-permute-start | bytes 786440 | tf_op jit(solution)/shard_map/ppermute | solution.py:29
  160.2 3.2 %collective-permute-done.43.refs_1_.refs_2_ = bf16[64,2048]{1,0:T(8,128)(2,1)S(1)} collective-permute-done((bf16[64,2048]{1,0:T(8,128)(2,1)S(1)}, bf16[64,2048]{1,0:T(8,128)(2,1)S(1)}, u32[]{:S(2)}, u32[]{:S(2)}) %collective-permute-start.43) | collective-permute-done | bytes 262176 | tf_op jit(solution)/shard_map/ppermute | solution.py:29
  163.3 2.6 %decode.11 = (f32[64,2048]{1,0:T(8,128)S(1)}, f32[64,2048]{1,0:T(8,128)S(1)}, bf16[128,2048]{1,0:T(8,128)(2,1)S(1)}) custom-call(bf16[64,2048]{1,0:T(8,128)(2,1)S(1)} %collective-permute-done.42.refs_0_.refs_3_, bf16[64,2048]{1,0:T(8,128)(2,1)S(1)} %collective-permute-done.43.refs_1_.refs_2_, bf16[64,2048]{1,0:T(8,128)(2,1)S(1)} %collective-permute-done.44.refs_2_.refs_5_, ...), custom_call_target="tpu_custom_call" | custom-call | flops 2147483648 | bytes 8388608 | tf_op jit(solution)/shard_map/decode/pallas_call | solution.py:261
  166.1 3.4 %decode.9 = (f32[64,2048]{1,0:T(8,128)S(1)}, bf16[64,2048]{1,0:T(8,128)(2,1)S(1)}) custom-call(bf16[64,2048]{1,0:T(8,128)(2,1)S(1)} %get-tuple-element.84.refs_0_, bf16[64,2048]{1,0:T(8,128)(2,1)S(1)} %get-tuple-element.85.refs_1_.refs_4_, bf16[2048,2048]{1,0:T(8,128)(2,1)S(1)} %load.1.refs_2_.refs_4_.refs_8_.refs_5_), custom_call_target="tpu_custom_call" | custom-call | flops 1073741824 | bytes 8388608 | tf_op jit(solution)/shard_map/decode/pallas_call | solution.py:261
  170.0 3.4 %decode.10 = (f32[64,2048]{1,0:T(8,128)S(1)}, bf16[64,2048]{1,0:T(8,128)(2,1)S(1)}) custom-call(bf16[64,2048]{1,0:T(8,128)(2,1)S(1)} %collective-permute-done.40.refs_0_.refs_1_, bf16[64,2048]{1,0:T(8,128)(2,1)S(1)} %collective-permute-done.41.refs_1_.refs_7_, bf16[2048,2048]{1,0:T(8,128)(2,1)S(1)} %load.1.refs_2_.refs_4_.refs_8_.refs_5_), custom_call_target="tpu_custom_call" | custom-call | flops 1073741824 | bytes 8388608 | tf_op jit(solution)/shard_map/decode/pallas_call | solution.py:261
  177.2 2.1 collective-permute-start.50
  179.7 4.3 %collective-permute-done.49.refs_1_ = bf16[64,2048]{1,0:T(8,128)(2,1)S(1)} collective-permute-done((bf16[64,2048]{1,0:T(8,128)(2,1)S(1)}, bf16[64,2048]{1,0:T(8,128)(2,1)S(1)}, u32[]{:S(2)}, u32[]{:S(2)}) %collective-permute-start.49) | collective-permute-done | bytes 262176 | tf_op jit(solution)/shard_map/ppermute | solution.py:53
  184.0 2.9 %collective-permute-done.50.refs_2_ = bf16[64,2048]{1,0:T(8,128)(2,1)S(1)} collective-permute-done((bf16[64,2048]{1,0:T(8,128)(2,1)S(1)}, bf16[64,2048]{1,0:T(8,128)(2,1)S(1)}, u32[]{:S(2)}, u32[]{:S(2)}) %collective-permute-start.50) | collective-permute-done | bytes 262176 | tf_op jit(solution)/shard_map/ppermute | solution.py:53
  189.5 4.0 %collective-permute-done.54.refs_3_ = bf16[64,2048]{1,0:T(8,128)(2,1)S(1)} collective-permute-done((bf16[64,2048]{1,0:T(8,128)(2,1)S(1)}, bf16[64,2048]{1,0:T(8,128)(2,1)S(1)}, u32[]{:S(2)}, u32[]{:S(2)}) %collective-permute-start.54) | collective-permute-done | bytes 262176 | tf_op jit(solution)/shard_map/ppermute | solution.py:53
  193.5 4.7 %collective-permute-done.53.refs_2_ = bf16[64,2048]{1,0:T(8,128)(2,1)S(1)} collective-permute-done((bf16[64,2048]{1,0:T(8,128)(2,1)S(1)}, bf16[64,2048]{1,0:T(8,128)(2,1)S(1)}, u32[]{:S(2)}, u32[]{:S(2)}) %collective-permute-start.53) | collective-permute-done | bytes 262176 | tf_op jit(solution)/shard_map/ppermute | solution.py:53
  199.6 3.7 %collective-permute-start.59 = (bf16[64,2048]{1,0:T(8,128)(2,1)S(1)}, bf16[64,2048]{1,0:T(8,128)(2,1)S(1)}, u32[]{:S(2)}, u32[]{:S(2)}) collective-permute-start(bf16[64,2048]{1,0:T(8,128)(2,1)S(1)} %get-tuple-element.98.own_ref), channel_id=1, source_target_pairs={{0,16},{4,68},{8,24},{12,76},{16,0},{20,84},{24,8},{28,92},{32,48}... | collective-permute-start | bytes 786440 | tf_op jit(solution)/shard_map/ppermute | solution.py:53
  203.3 3.5 %collective-permute-done.61.own_ref = bf16[64,2048]{1,0:T(8,128)(2,1)S(1)} collective-permute-done((bf16[64,2048]{1,0:T(8,128)(2,1)S(1)}, bf16[64,2048]{1,0:T(8,128)(2,1)S(1)}, u32[]{:S(2)}, u32[]{:S(2)}) %collective-permute-start.61) | collective-permute-done | bytes 262176 | tf_op jit(solution)/shard_map/ppermute | solution.py:53
  206.7 3.7 %collective-permute-done.59.own_ref = bf16[64,2048]{1,0:T(8,128)(2,1)S(1)} collective-permute-done((bf16[64,2048]{1,0:T(8,128)(2,1)S(1)}, bf16[64,2048]{1,0:T(8,128)(2,1)S(1)}, u32[]{:S(2)}, u32[]{:S(2)}) %collective-permute-start.59) | collective-permute-done | bytes 262176 | tf_op jit(solution)/shard_map/ppermute | solution.py:53
  212.0 4.2 %collective-permute-start.55 = (f32[16,2048]{1,0:T(8,128)S(1)}, f32[16,2048]{1,0:T(8,128)S(1)}, u32[]{:S(2)}, u32[]{:S(2)}) collective-permute-start(f32[16,2048]{1,0:T(8,128)S(1)} %get-tuple-element.97), channel_id=1, source_target_pairs={{0,0},{4,16},{8,32},{12,20},{16,64},{20,24},{24,96},{28,28},{32,4}... | collective-permute-start | bytes 393224 | tf_op jit(solution)/shard_map/ppermute | solution.py:61
  217.1 5.4 %gradient.1 = (f32[2048,2048]{1,0:T(8,128)S(1)}, f32[1,2048]{1,0:T(1,128)S(1)}) custom-call(bf16[2048,128]{1,0:T(8,128)(2,1)S(1)} %turn.4.refs_0_, bf16[2048,128]{1,0:T(8,128)(2,1)S(1)} %turn.5.refs_1_, bf16[2048,128]{1,0:T(8,128)(2,1)S(1)} %turn.6.refs_2_, bf16[2048,128]{1,0:T(8,128)(2,1)S(1)} %turn.7.refs_3_, bf16[512,2048]{1,0:T(8,128)(2,1)S(1)} %arrange.1.refs_4_, ...), custom_call_target="tpu_custom_call" | custom-call | flops 4294967296 | bytes 25165824 | tf_op jit(solution)/shard_map/gradient/pallas_call | solution.py:427
  222.5 3.0 %collective-permute-start.65 = (f32[1,2048]{1,0:T(1,128)S(1)}, f32[1,2048]{1,0:T(1,128)S(1)}, u32[]{:S(2)}, u32[]{:S(2)}) collective-permute-start(f32[1,2048]{1,0:T(1,128)S(1)} %get-tuple-element.100.refs_0_), channel_id=1, source_target_pairs={{0,3},{1,0},{2,1},{3,2},{4,7},{5,4},{6,5},{7,6},{8,11},{9,8},{10,9... | collective-permute-start | bytes 24584 | tf_op jit(solution)/shard_map/ppermute | solution.py:29
  230.7 3.6 %scale.1 = bf16[2048,2048]{1,0:T(8,128)(2,1)} custom-call(f32[2048,2048]{1,0:T(8,128)S(1)} %get-tuple-element.99.moved_ref, f32[1,2048]{1,0:T(1,128)S(1)} %get-tuple-element.100.refs_0_, f32[1,2048]{1,0:T(1,128)S(1)} %collective-permute-done.63.refs_1_, f32[1,2048]{1,0:T(1,128)S(1)} %collective-permute-done.64.refs_2_, ...), custom_call_target="tpu_custom_call" | custom-call | flops 4194304 | bytes 8388608 | tf_op jit(solution)/shard_map/scale/pallas_call | solution.py:461
  (127 shorter events, 61.4 us)
Async XLA Ops:
  2.0 10.8 %collective-permute-start.4 = (bf16[64,2048]{1,0:T(8,128)(2,1)S(1)}, bf16[64,2048]{1,0:T(8,128)(2,1)S(1)}, u32[]{:S(2)}, u32[]{:S(2)}) collective-permute-start(bf16[64,2048]{1,0:T(8,128)(2,1)S(1)} %get-tuple-element.101), channel_id=1, source_target_pairs={{0,2},{1,3},{2,0},{3,1},{4,6},{5,7},{6,4},{7,5},{8,10},{9,11},{10,... | collective-permute-start | bytes 786440 | tf_op jit(solution)/shard_map/ppermute | solution.py:29
  5.1 12.3 %collective-permute-start = (bf16[64,2048]{1,0:T(8,128)(2,1)S(1)}, bf16[64,2048]{1,0:T(8,128)(2,1)S(1)}, u32[]{:S(2)}, u32[]{:S(2)}) collective-permute-start(bf16[64,2048]{1,0:T(8,128)(2,1)S(1)} %get-tuple-element.102), channel_id=1, source_target_pairs={{0,3},{1,0},{2,1},{3,2},{4,7},{5,4},{6,5},{7,6},{8,11},{9,8},{10,9... | collective-permute-start | bytes 786440 | tf_op jit(solution)/shard_map/ppermute | solution.py:29
  6.3 11.1 %collective-permute-start.1 = (bf16[64,2048]{1,0:T(8,128)(2,1)S(1)}, bf16[64,2048]{1,0:T(8,128)(2,1)S(1)}, u32[]{:S(2)}, u32[]{:S(2)}) collective-permute-start(bf16[64,2048]{1,0:T(8,128)(2,1)S(1)} %get-tuple-element.105), channel_id=1, source_target_pairs={{0,1},{1,2},{2,3},{3,0},{4,5},{5,6},{6,7},{7,4},{8,9},{9,10},{10,1... | collective-permute-start | bytes 786440 | tf_op jit(solution)/shard_map/ppermute | solution.py:29
  12.8 9.2 %collective-permute-start.5 = (bf16[64,2048]{1,0:T(8,128)(2,1)S(1)}, bf16[64,2048]{1,0:T(8,128)(2,1)S(1)}, u32[]{:S(2)}, u32[]{:S(2)}) collective-permute-start(bf16[64,2048]{1,0:T(8,128)(2,1)S(1)} %collective-permute-done.4.refs_0_.refs_6_), channel_id=1, source_target_pairs={{0,4},{4,0},{1,5},{5,1},{2,6},{6,2},{3,7},{7,3},{8,12},{12,8},{9,1... | collective-permute-start | bytes 786440 | tf_op jit(solution)/shard_map/ppermute | solution.py:33
  17.4 9.4 %collective-permute-start.2 = (bf16[64,2048]{1,0:T(8,128)(2,1)S(1)}, bf16[64,2048]{1,0:T(8,128)(2,1)S(1)}, u32[]{:S(2)}, u32[]{:S(2)}) collective-permute-start(bf16[64,2048]{1,0:T(8,128)(2,1)S(1)} %collective-permute-done.refs_0_.refs_7_), channel_id=1, source_target_pairs={{0,4},{4,0},{1,5},{5,1},{2,6},{6,2},{3,7},{7,3},{8,12},{12,8},{9,1... | collective-permute-start | bytes 786440 | tf_op jit(solution)/shard_map/ppermute | solution.py:33
  17.4 9.4 %collective-permute-start.3 = (bf16[64,2048]{1,0:T(8,128)(2,1)S(1)}, bf16[64,2048]{1,0:T(8,128)(2,1)S(1)}, u32[]{:S(2)}, u32[]{:S(2)}) collective-permute-start(bf16[64,2048]{1,0:T(8,128)(2,1)S(1)} %collective-permute-done.1.refs_1_.refs_5_), channel_id=1, source_target_pairs={{0,4},{4,0},{1,5},{5,1},{2,6},{6,2},{3,7},{7,3},{8,12},{12,8},{9,1... | collective-permute-start | bytes 786440 | tf_op jit(solution)/shard_map/ppermute | solution.py:33
  23.5 9.5 %collective-permute-start.6 = (bf16[64,2048]{1,0:T(8,128)(2,1)S(1)}, bf16[64,2048]{1,0:T(8,128)(2,1)S(1)}, u32[]{:S(2)}, u32[]{:S(2)}) collective-permute-start(bf16[64,2048]{1,0:T(8,128)(2,1)S(1)} %get-tuple-element.55), channel_id=1, source_target_pairs={{0,1},{1,2},{2,3},{3,0},{4,5},{5,6},{6,7},{7,4},{8,9},{9,10},{10,1... | collective-permute-start | bytes 786440 | tf_op jit(solution)/shard_map/ppermute | solution.py:29
  25.0 9.2 %collective-permute-start.10 = (bf16[64,2048]{1,0:T(8,128)(2,1)S(1)}, bf16[64,2048]{1,0:T(8,128)(2,1)S(1)}, u32[]{:S(2)}, u32[]{:S(2)}) collective-permute-start(bf16[64,2048]{1,0:T(8,128)(2,1)S(1)} %get-tuple-element.59), channel_id=1, source_target_pairs={{0,3},{1,0},{2,1},{3,2},{4,7},{5,4},{6,5},{7,6},{8,11},{9,8},{10,9... | collective-permute-start | bytes 786440 | tf_op jit(solution)/shard_map/ppermute | solution.py:29
  29.5 10.3 %collective-permute-start.8 = (bf16[64,2048]{1,0:T(8,128)(2,1)S(1)}, bf16[64,2048]{1,0:T(8,128)(2,1)S(1)}, u32[]{:S(2)}, u32[]{:S(2)}) collective-permute-start(bf16[64,2048]{1,0:T(8,128)(2,1)S(1)} %get-tuple-element.56), channel_id=1, source_target_pairs={{0,3},{1,0},{2,1},{3,2},{4,7},{5,4},{6,5},{7,6},{8,11},{9,8},{10,9... | collective-permute-start | bytes 786440 | tf_op jit(solution)/shard_map/ppermute | solution.py:29
  31.0 10.4 %collective-permute-start.9 = (bf16[64,2048]{1,0:T(8,128)(2,1)S(1)}, bf16[64,2048]{1,0:T(8,128)(2,1)S(1)}, u32[]{:S(2)}, u32[]{:S(2)}) collective-permute-start(bf16[64,2048]{1,0:T(8,128)(2,1)S(1)} %get-tuple-element.57), channel_id=1, source_target_pairs={{0,1},{1,2},{2,3},{3,0},{4,5},{5,6},{6,7},{7,4},{8,9},{9,10},{10,1... | collective-permute-start | bytes 786440 | tf_op jit(solution)/shard_map/ppermute | solution.py:29
  33.1 12.1 %collective-permute-start.7 = (bf16[64,2048]{1,0:T(8,128)(2,1)S(1)}, bf16[64,2048]{1,0:T(8,128)(2,1)S(1)}, u32[]{:S(2)}, u32[]{:S(2)}) collective-permute-start(bf16[64,2048]{1,0:T(8,128)(2,1)S(1)} %add.63), channel_id=1, source_target_pairs={{0,1},{1,2},{2,3},{3,0},{4,5},{5,6},{6,7},{7,4},{8,9},{9,10},{10,1... | collective-permute-start | bytes 786440 | tf_op jit(solution)/shard_map/ppermute | solution.py:29
  34.2 11.0 %collective-permute-start.11 = (bf16[64,2048]{1,0:T(8,128)(2,1)S(1)}, bf16[64,2048]{1,0:T(8,128)(2,1)S(1)}, u32[]{:S(2)}, u32[]{:S(2)}) collective-permute-start(bf16[64,2048]{1,0:T(8,128)(2,1)S(1)} %add.64), channel_id=1, source_target_pairs={{0,3},{1,0},{2,1},{3,2},{4,7},{5,4},{6,5},{7,6},{8,11},{9,8},{10,9... | collective-permute-start | bytes 786440 | tf_op jit(solution)/shard_map/ppermute | solution.py:29
  46.1 9.7 %collective-permute-start.12 = (bf16[64,2048]{1,0:T(8,128)(2,1)S(1)}, bf16[64,2048]{1,0:T(8,128)(2,1)S(1)}, u32[]{:S(2)}, u32[]{:S(2)}) collective-permute-start(bf16[64,2048]{1,0:T(8,128)(2,1)S(1)} %get-tuple-element.60.refs_0_), channel_id=1, source_target_pairs={{0,1},{1,2},{2,3},{3,0},{4,5},{5,6},{6,7},{7,4},{8,9},{9,10},{10,1... | collective-permute-start | bytes 786440 | tf_op jit(solution)/shard_map/ppermute | solution.py:29
  46.6 9.6 %collective-permute-start.13 = (bf16[64,2048]{1,0:T(8,128)(2,1)S(1)}, bf16[64,2048]{1,0:T(8,128)(2,1)S(1)}, u32[]{:S(2)}, u32[]{:S(2)}) collective-permute-start(bf16[64,2048]{1,0:T(8,128)(2,1)S(1)} %get-tuple-element.61.refs_1_), channel_id=1, source_target_pairs={{0,3},{1,0},{2,1},{3,2},{4,7},{5,4},{6,5},{7,6},{8,11},{9,8},{10,9... | collective-permute-start | bytes 786440 | tf_op jit(solution)/shard_map/ppermute | solution.py:29
  49.4 12.2 %collective-permute-start.14 = (bf16[64,2048]{1,0:T(8,128)(2,1)S(1)}, bf16[64,2048]{1,0:T(8,128)(2,1)S(1)}, u32[]{:S(2)}, u32[]{:S(2)}) collective-permute-start(bf16[64,2048]{1,0:T(8,128)(2,1)S(1)} %get-tuple-element.60.refs_0_), channel_id=1, source_target_pairs={{0,3},{1,0},{2,1},{3,2},{4,7},{5,4},{6,5},{7,6},{8,11},{9,8},{10,9... | collective-permute-start | bytes 786440 | tf_op jit(solution)/shard_map/ppermute | solution.py:29
  50.2 11.4 %collective-permute-start.16 = (bf16[64,2048]{1,0:T(8,128)(2,1)S(1)}, bf16[64,2048]{1,0:T(8,128)(2,1)S(1)}, u32[]{:S(2)}, u32[]{:S(2)}) collective-permute-start(bf16[64,2048]{1,0:T(8,128)(2,1)S(1)} %get-tuple-element.61.refs_1_), channel_id=1, source_target_pairs={{0,1},{1,2},{2,3},{3,0},{4,5},{5,6},{6,7},{7,4},{8,9},{9,10},{10,1... | collective-permute-start | bytes 786440 | tf_op jit(solution)/shard_map/ppermute | solution.py:29
  55.9 9.3 %collective-permute-start.15 = (bf16[64,2048]{1,0:T(8,128)(2,1)S(1)}, bf16[64,2048]{1,0:T(8,128)(2,1)S(1)}, u32[]{:S(2)}, u32[]{:S(2)}) collective-permute-start(bf16[64,2048]{1,0:T(8,128)(2,1)S(1)} %collective-permute-done.12.refs_0_), channel_id=1, source_target_pairs={{0,1},{1,2},{2,3},{3,0},{4,5},{5,6},{6,7},{7,4},{8,9},{9,10},{10,1... | collective-permute-start | bytes 786440 | tf_op jit(solution)/shard_map/ppermute | solution.py:29
  56.1 9.1 %collective-permute-start.17 = (bf16[64,2048]{1,0:T(8,128)(2,1)S(1)}, bf16[64,2048]{1,0:T(8,128)(2,1)S(1)}, u32[]{:S(2)}, u32[]{:S(2)}) collective-permute-start(bf16[64,2048]{1,0:T(8,128)(2,1)S(1)} %collective-permute-done.13.refs_1_), channel_id=1, source_target_pairs={{0,3},{1,0},{2,1},{3,2},{4,7},{5,4},{6,5},{7,6},{8,11},{9,8},{10,9... | collective-permute-start | bytes 786440 | tf_op jit(solution)/shard_map/ppermute | solution.py:29
  67.9 9.0 %collective-permute-start.20 = (bf16[128,2048]{1,0:T(8,128)(2,1)S(1)}, bf16[128,2048]{1,0:T(8,128)(2,1)S(1)}, u32[]{:S(2)}, u32[]{:S(2)}) collective-permute-start(bf16[128,2048]{1,0:T(8,128)(2,1)S(1)} %get-tuple-element.68), channel_id=1, source_target_pairs={{0,4},{4,0},{1,5},{5,1},{2,6},{6,2},{3,7},{7,3},{8,12},{12,8},{9,1... | collective-permute-start | bytes 1572872 | tf_op jit(solution)/shard_map/ppermute | solution.py:33
  77.9 8.1 %collective-permute-start.21 = (bf16[64,2048]{1,0:T(8,128)(2,1)S(1)}, bf16[64,2048]{1,0:T(8,128)(2,1)S(1)}, u32[]{:S(2)}, u32[]{:S(2)}) collective-permute-start(bf16[64,2048]{1,0:T(8,128)(2,1)S(1)} %get-tuple-element.70), channel_id=1, source_target_pairs={{0,16},{4,68},{8,24},{12,76},{16,0},{20,84},{24,8},{28,92},{32,48}... | collective-permute-start | bytes 786440 | tf_op jit(solution)/shard_map/ppermute | solution.py:53
  89.3 8.0 %collective-permute-start.26 = (bf16[64,2048]{1,0:T(8,128)(2,1)S(1)}, bf16[64,2048]{1,0:T(8,128)(2,1)S(1)}, u32[]{:S(2)}, u32[]{:S(2)}) collective-permute-start(bf16[64,2048]{1,0:T(8,128)(2,1)S(1)} %partial.2.refs_0_), channel_id=1, source_target_pairs={{0,96},{4,28},{8,104},{12,4},{16,112},{20,12},{24,120},{28,20},{32... | collective-permute-start | bytes 786440 | tf_op jit(solution)/shard_map/ppermute | solution.py:53
  93.4 10.4 %collective-permute-start.25 = (bf16[64,2048]{1,0:T(8,128)(2,1)S(1)}, bf16[64,2048]{1,0:T(8,128)(2,1)S(1)}, u32[]{:S(2)}, u32[]{:S(2)}) collective-permute-start(bf16[64,2048]{1,0:T(8,128)(2,1)S(1)} %partial.2.refs_0_), channel_id=1, source_target_pairs={{0,32},{4,12},{8,40},{12,20},{16,48},{20,28},{24,56},{28,4},{32,64... | collective-permute-start | bytes 786440 | tf_op jit(solution)/shard_map/ppermute | solution.py:53
  93.4 10.4 %collective-permute-start.24 = (bf16[64,2048]{1,0:T(8,128)(2,1)S(1)}, bf16[64,2048]{1,0:T(8,128)(2,1)S(1)}, u32[]{:S(2)}, u32[]{:S(2)}) collective-permute-start(bf16[64,2048]{1,0:T(8,128)(2,1)S(1)} %partial.2.refs_0_), channel_id=1, source_target_pairs={{0,64},{4,20},{8,72},{12,28},{16,80},{20,4},{24,88},{28,12},{32,96... | collective-permute-start | bytes 786440 | tf_op jit(solution)/shard_map/ppermute | solution.py:53
  105.3 10.5 %collective-permute-start.29 = (bf16[64,2048]{1,0:T(8,128)(2,1)S(1)}, bf16[64,2048]{1,0:T(8,128)(2,1)S(1)}, u32[]{:S(2)}, u32[]{:S(2)}) collective-permute-start(bf16[64,2048]{1,0:T(8,128)(2,1)S(1)} %get-tuple-element.73.refs_0_), channel_id=1, source_target_pairs={{0,24},{4,100},{8,0},{12,108},{16,8},{20,116},{24,16},{28,124},{32... | collective-permute-start | bytes 786440 | tf_op jit(solution)/shard_map/ppermute | solution.py:53
  105.4 10.4 %collective-permute-start.28 = (bf16[64,2048]{1,0:T(8,128)(2,1)S(1)}, bf16[64,2048]{1,0:T(8,128)(2,1)S(1)}, u32[]{:S(2)}, u32[]{:S(2)}) collective-permute-start(bf16[64,2048]{1,0:T(8,128)(2,1)S(1)} %get-tuple-element.73.refs_0_), channel_id=1, source_target_pairs={{0,16},{4,68},{8,24},{12,76},{16,0},{20,84},{24,8},{28,92},{32,48}... | collective-permute-start | bytes 786440 | tf_op jit(solution)/shard_map/ppermute | solution.py:53
  107.1 9.6 %collective-permute-start.27 = (bf16[64,2048]{1,0:T(8,128)(2,1)S(1)}, bf16[64,2048]{1,0:T(8,128)(2,1)S(1)}, u32[]{:S(2)}, u32[]{:S(2)}) collective-permute-start(bf16[64,2048]{1,0:T(8,128)(2,1)S(1)} %get-tuple-element.73.refs_0_), channel_id=1, source_target_pairs={{0,8},{4,36},{8,16},{12,44},{16,24},{20,52},{24,0},{28,60},{32,40}... | collective-permute-start | bytes 786440 | tf_op jit(solution)/shard_map/ppermute | solution.py:53
  120.4 9.6 %collective-permute-start.34 = (bf16[64,2048]{1,0:T(8,128)(2,1)S(1)}, bf16[64,2048]{1,0:T(8,128)(2,1)S(1)}, u32[]{:S(2)}, u32[]{:S(2)}) collective-permute-start(bf16[64,2048]{1,0:T(8,128)(2,1)S(1)} %get-tuple-element.77), channel_id=1, source_target_pairs={{0,1},{1,2},{2,3},{3,0},{4,5},{5,6},{6,7},{7,4},{8,9},{9,10},{10,1... | collective-permute-start | bytes 786440 | tf_op jit(solution)/shard_map/ppermute | solution.py:29
  121.2 9.0 %collective-permute-start.38 = (bf16[64,2048]{1,0:T(8,128)(2,1)S(1)}, bf16[64,2048]{1,0:T(8,128)(2,1)S(1)}, u32[]{:S(2)}, u32[]{:S(2)}) collective-permute-start(bf16[64,2048]{1,0:T(8,128)(2,1)S(1)} %get-tuple-element.81), channel_id=1, source_target_pairs={{0,3},{1,0},{2,1},{3,2},{4,7},{5,4},{6,5},{7,6},{8,11},{9,8},{10,9... | collective-permute-start | bytes 786440 | tf_op jit(solution)/shard_map/ppermute | solution.py:29
  127.1 9.5 %collective-permute-start.36 = (bf16[64,2048]{1,0:T(8,128)(2,1)S(1)}, bf16[64,2048]{1,0:T(8,128)(2,1)S(1)}, u32[]{:S(2)}, u32[]{:S(2)}) collective-permute-start(bf16[64,2048]{1,0:T(8,128)(2,1)S(1)} %get-tuple-element.78), channel_id=1, source_target_pairs={{0,3},{1,0},{2,1},{3,2},{4,7},{5,4},{6,5},{7,6},{8,11},{9,8},{10,9... | collective-permute-start | bytes 786440 | tf_op jit(solution)/shard_map/ppermute | solution.py:29
  128.9 10.4 %collective-permute-start.37 = (bf16[64,2048]{1,0:T(8,128)(2,1)S(1)}, bf16[64,2048]{1,0:T(8,128)(2,1)S(1)}, u32[]{:S(2)}, u32[]{:S(2)}) collective-permute-start(bf16[64,2048]{1,0:T(8,128)(2,1)S(1)} %get-tuple-element.79), channel_id=1, source_target_pairs={{0,1},{1,2},{2,3},{3,0},{4,5},{5,6},{6,7},{7,4},{8,9},{9,10},{10,1... | collective-permute-start | bytes 786440 | tf_op jit(solution)/shard_map/ppermute | solution.py:29
  130.1 13.1 %collective-permute-start.35 = (bf16[64,2048]{1,0:T(8,128)(2,1)S(1)}, bf16[64,2048]{1,0:T(8,128)(2,1)S(1)}, u32[]{:S(2)}, u32[]{:S(2)}) collective-permute-start(bf16[64,2048]{1,0:T(8,128)(2,1)S(1)} %add.65), channel_id=1, source_target_pairs={{0,1},{1,2},{2,3},{3,0},{4,5},{5,6},{6,7},{7,4},{8,9},{9,10},{10,1... | collective-permute-start | bytes 786440 | tf_op jit(solution)/shard_map/ppermute | solution.py:29
  130.3 13.0 %collective-permute-start.39 = (bf16[64,2048]{1,0:T(8,128)(2,1)S(1)}, bf16[64,2048]{1,0:T(8,128)(2,1)S(1)}, u32[]{:S(2)}, u32[]{:S(2)}) collective-permute-start(bf16[64,2048]{1,0:T(8,128)(2,1)S(1)} %add.66), channel_id=1, source_target_pairs={{0,3},{1,0},{2,1},{3,2},{4,7},{5,4},{6,5},{7,6},{8,11},{9,8},{10,9... | collective-permute-start | bytes 786440 | tf_op jit(solution)/shard_map/ppermute | solution.py:29
  144.2 10.3 %collective-permute-start.40 = (bf16[64,2048]{1,0:T(8,128)(2,1)S(1)}, bf16[64,2048]{1,0:T(8,128)(2,1)S(1)}, u32[]{:S(2)}, u32[]{:S(2)}) collective-permute-start(bf16[64,2048]{1,0:T(8,128)(2,1)S(1)} %get-tuple-element.84.refs_0_), channel_id=1, source_target_pairs={{0,1},{1,2},{2,3},{3,0},{4,5},{5,6},{6,7},{7,4},{8,9},{9,10},{10,1... | collective-permute-start | bytes 786440 | tf_op jit(solution)/shard_map/ppermute | solution.py:29
  144.3 10.3 %collective-permute-start.41 = (bf16[64,2048]{1,0:T(8,128)(2,1)S(1)}, bf16[64,2048]{1,0:T(8,128)(2,1)S(1)}, u32[]{:S(2)}, u32[]{:S(2)}) collective-permute-start(bf16[64,2048]{1,0:T(8,128)(2,1)S(1)} %get-tuple-element.85.refs_1_.refs_4_), channel_id=1, source_target_pairs={{0,3},{1,0},{2,1},{3,2},{4,7},{5,4},{6,5},{7,6},{8,11},{9,8},{10,9... | collective-permute-start | bytes 786440 | tf_op jit(solution)/shard_map/ppermute | solution.py:29
  147.5 12.3 %collective-permute-start.42 = (bf16[64,2048]{1,0:T(8,128)(2,1)S(1)}, bf16[64,2048]{1,0:T(8,128)(2,1)S(1)}, u32[]{:S(2)}, u32[]{:S(2)}) collective-permute-start(bf16[64,2048]{1,0:T(8,128)(2,1)S(1)} %get-tuple-element.84.refs_0_), channel_id=1, source_target_pairs={{0,3},{1,0},{2,1},{3,2},{4,7},{5,4},{6,5},{7,6},{8,11},{9,8},{10,9... | collective-permute-start | bytes 786440 | tf_op jit(solution)/shard_map/ppermute | solution.py:29
  147.5 12.6 %collective-permute-start.44 = (bf16[64,2048]{1,0:T(8,128)(2,1)S(1)}, bf16[64,2048]{1,0:T(8,128)(2,1)S(1)}, u32[]{:S(2)}, u32[]{:S(2)}) collective-permute-start(bf16[64,2048]{1,0:T(8,128)(2,1)S(1)} %get-tuple-element.85.refs_1_.refs_4_), channel_id=1, source_target_pairs={{0,1},{1,2},{2,3},{3,0},{4,5},{5,6},{6,7},{7,4},{8,9},{9,10},{10,1... | collective-permute-start | bytes 786440 | tf_op jit(solution)/shard_map/ppermute | solution.py:29
  154.5 8.8 %collective-permute-start.43 = (bf16[64,2048]{1,0:T(8,128)(2,1)S(1)}, bf16[64,2048]{1,0:T(8,128)(2,1)S(1)}, u32[]{:S(2)}, u32[]{:S(2)}) collective-permute-start(bf16[64,2048]{1,0:T(8,128)(2,1)S(1)} %collective-permute-done.40.refs_0_.refs_1_), channel_id=1, source_target_pairs={{0,1},{1,2},{2,3},{3,0},{4,5},{5,6},{6,7},{7,4},{8,9},{9,10},{10,1... | collective-permute-start | bytes 786440 | tf_op jit(solution)/shard_map/ppermute | solution.py:29
  154.6 8.8 %collective-permute-start.45 = (bf16[64,2048]{1,0:T(8,128)(2,1)S(1)}, bf16[64,2048]{1,0:T(8,128)(2,1)S(1)}, u32[]{:S(2)}, u32[]{:S(2)}) collective-permute-start(bf16[64,2048]{1,0:T(8,128)(2,1)S(1)} %collective-permute-done.41.refs_1_.refs_7_), channel_id=1, source_target_pairs={{0,3},{1,0},{2,1},{3,2},{4,7},{5,4},{6,5},{7,6},{8,11},{9,8},{10,9... | collective-permute-start | bytes 786440 | tf_op jit(solution)/shard_map/ppermute | solution.py:29
  166.0 9.1 %collective-permute-start.48 = (bf16[128,2048]{1,0:T(8,128)(2,1)S(1)}, bf16[128,2048]{1,0:T(8,128)(2,1)S(1)}, u32[]{:S(2)}, u32[]{:S(2)}) collective-permute-start(bf16[128,2048]{1,0:T(8,128)(2,1)S(1)} %get-tuple-element.92), channel_id=1, source_target_pairs={{0,4},{4,0},{1,5},{5,1},{2,6},{6,2},{3,7},{7,3},{8,12},{12,8},{9,1... | collective-permute-start | bytes 1572872 | tf_op jit(solution)/shard_map/ppermute | solution.py:33
  176.1 8.0 %collective-permute-start.49 = (bf16[64,2048]{1,0:T(8,128)(2,1)S(1)}, bf16[64,2048]{1,0:T(8,128)(2,1)S(1)}, u32[]{:S(2)}, u32[]{:S(2)}) collective-permute-start(bf16[64,2048]{1,0:T(8,128)(2,1)S(1)} %get-tuple-element.94), channel_id=1, source_target_pairs={{0,16},{4,68},{8,24},{12,76},{16,0},{20,84},{24,8},{28,92},{32,48}... | collective-permute-start | bytes 786440 | tf_op jit(solution)/shard_map/ppermute | solution.py:53
  177.2 9.6 %collective-permute-start.50 = (bf16[64,2048]{1,0:T(8,128)(2,1)S(1)}, bf16[64,2048]{1,0:T(8,128)(2,1)S(1)}, u32[]{:S(2)}, u32[]{:S(2)}) collective-permute-start(bf16[64,2048]{1,0:T(8,128)(2,1)S(1)} %get-tuple-element.95), channel_id=1, source_target_pairs={{0,8},{4,36},{8,16},{12,44},{16,24},{20,52},{24,0},{28,60},{32,40}... | collective-permute-start | bytes 786440 | tf_op jit(solution)/shard_map/ppermute | solution.py:53
  187.8 10.4 %collective-permute-start.53 = (bf16[64,2048]{1,0:T(8,128)(2,1)S(1)}, bf16[64,2048]{1,0:T(8,128)(2,1)S(1)}, u32[]{:S(2)}, u32[]{:S(2)}) collective-permute-start(bf16[64,2048]{1,0:T(8,128)(2,1)S(1)} %partial.3.refs_0_), channel_id=1, source_target_pairs={{0,32},{4,12},{8,40},{12,20},{16,48},{20,28},{24,56},{28,4},{32,64... | collective-permute-start | bytes 786440 | tf_op jit(solution)/shard_map/ppermute | solution.py:53
  189.1 9.1 %collective-permute-start.52 = (bf16[64,2048]{1,0:T(8,128)(2,1)S(1)}, bf16[64,2048]{1,0:T(8,128)(2,1)S(1)}, u32[]{:S(2)}, u32[]{:S(2)}) collective-permute-start(bf16[64,2048]{1,0:T(8,128)(2,1)S(1)} %partial.3.refs_0_), channel_id=1, source_target_pairs={{0,64},{4,20},{8,72},{12,28},{16,80},{20,4},{24,88},{28,12},{32,96... | collective-permute-start | bytes 786440 | tf_op jit(solution)/shard_map/ppermute | solution.py:53
  199.1 7.7 %collective-permute-start.61 = (bf16[64,2048]{1,0:T(8,128)(2,1)S(1)}, bf16[64,2048]{1,0:T(8,128)(2,1)S(1)}, u32[]{:S(2)}, u32[]{:S(2)}) collective-permute-start(bf16[64,2048]{1,0:T(8,128)(2,1)S(1)} %get-tuple-element.98.own_ref), channel_id=1, source_target_pairs={{0,24},{4,100},{8,0},{12,108},{16,8},{20,116},{24,16},{28,124},{32... | collective-permute-start | bytes 786440 | tf_op jit(solution)/shard_map/ppermute | solution.py:53
  199.6 10.8 %collective-permute-start.59 = (bf16[64,2048]{1,0:T(8,128)(2,1)S(1)}, bf16[64,2048]{1,0:T(8,128)(2,1)S(1)}, u32[]{:S(2)}, u32[]{:S(2)}) collective-permute-start(bf16[64,2048]{1,0:T(8,128)(2,1)S(1)} %get-tuple-element.98.own_ref), channel_id=1, source_target_pairs={{0,16},{4,68},{8,24},{12,76},{16,0},{20,84},{24,8},{28,92},{32,48}... | collective-permute-start | bytes 786440 | tf_op jit(solution)/shard_map/ppermute | solution.py:53
  203.3 13.0 %collective-permute-start.56 = (bf16[64,2048]{1,0:T(8,128)(2,1)S(1)}, bf16[64,2048]{1,0:T(8,128)(2,1)S(1)}, u32[]{:S(2)}, u32[]{:S(2)}) collective-permute-start(bf16[64,2048]{1,0:T(8,128)(2,1)S(1)} %get-tuple-element.98.own_ref), channel_id=1, source_target_pairs={{0,4},{4,0},{1,5},{5,1},{2,6},{6,2},{3,7},{7,3},{8,12},{12,8},{9,1... | collective-permute-start | bytes 786440 | tf_op jit(solution)/shard_map/ppermute | solution.py:33
  206.7 9.7 %collective-permute-start.62 = (bf16[64,2048]{1,0:T(8,128)(2,1)S(1)}, bf16[64,2048]{1,0:T(8,128)(2,1)S(1)}, u32[]{:S(2)}, u32[]{:S(2)}) collective-permute-start(bf16[64,2048]{1,0:T(8,128)(2,1)S(1)} %collective-permute-done.61.own_ref), channel_id=1, source_target_pairs={{0,4},{4,0},{1,5},{5,1},{2,6},{6,2},{3,7},{7,3},{8,12},{12,8},{9,1... | collective-permute-start | bytes 786440 | tf_op jit(solution)/shard_map/ppermute | solution.py:33
  212.0 16.1 %collective-permute-start.55 = (f32[16,2048]{1,0:T(8,128)S(1)}, f32[16,2048]{1,0:T(8,128)S(1)}, u32[]{:S(2)}, u32[]{:S(2)}) collective-permute-start(f32[16,2048]{1,0:T(8,128)S(1)} %get-tuple-element.97), channel_id=1, source_target_pairs={{0,0},{4,16},{8,32},{12,20},{16,64},{20,24},{24,96},{28,28},{32,4}... | collective-permute-start | bytes 393224 | tf_op jit(solution)/shard_map/ppermute | solution.py:61
  (20 other events, 280.3 us)

commit v2 on v1

--- a/solution.py
+++ b/solution.py
@@ -548,7 +548,7 @@
         far_high = shift_x(down_high, -1)
         return (low, high), (up_low, up_high), (far_low, far_high), (down_low, down_high)
 
-    def residual_of(coded):
+    def residual_of(coded, turns):
         keeps, sent = [None] * 4, []
         groups = (((0,), (0,)), ((1,), (3,)), ((3, 2), (1, 2)))
         for g, (low, high) in enumerate(groups):
@@ -563,16 +563,16 @@
             sent.append(other_core(send))
         routed = route(index, keeps, sent)
         pieces = [routed[0]]
-        for k in (2, 1, 3):
+        for k in turns:
             pieces.append(shift_mixed(routed[k], k, True))
         total = partial_sum(pieces)
         pieces = [total]
-        for k in (2, 1, 3):
+        for k in turns:
             pieces.append(shift_mixed(total, k, False))
         rounded, mine = residual_block(index, pieces, own_act)
         own = [rounded, None, None, None]
         other = [None] * 4
-        for k in (2, 1, 3):
+        for k in turns:
             own[k] = shift_mixed(rounded, k, True)
         for k in (0, 1, 3, 2):
             other[k] = other_core(own[k])
@@ -583,10 +583,10 @@
         [own_act[(4 - k) % 4] for k in ks],
         [other_act[(4 - k) % 4] for k in ks],
     )
-    for _ in range(ITERS):
+    for iteration in range(ITERS):
         codes, coded = encode(source, codes)
         coded = gather(coded)
-        mine, own, other = residual_of(coded)
+        mine, own, other = residual_of(coded, (1, 3, 2) if iteration == 0 else (2, 1, 3))
         source = lambda ks, own=own, other=other: (own, other)
 
     residual = to_owner(mine)

time: 236 us -> 235 us (level)
  starting transfers between devices: 76.3 us -> 80 us
  waiting for transfers between devices: 99 us -> 95.5 us
    ppermute x18, waiting for transfers between devices: 46.3 us -> 42.7 us  [shift_mixed(): return lax.ppermute(value, ATOM, pairs_of(target))]
    ppermute x18, starting transfers between devices: 23.6 us -> 26.9 us  [shift_mixed(): return lax.ppermute(value, ATOM, pairs_of(target))]
  transfers between devices with their start and end apart: 66 -> 66, of which waited for: 38 -> 38; matrix products, arithmetic and copies ran while one was open for 0% -> 0% of each run, Pallas kernels for 17% -> 16%
where the time goes in v2:
time: 235 us
  waiting for transfers between devices  95.5 us (41%)
  starting transfers between devices  80 us (34%)
  Pallas kernels  56.3 us (24%)
    ppermute x30, waiting for transfers between devices, shift_x(): return lax.ppermute(value, 'x', [(i, (i + step) % 4) for i in range(4)])  48.3 us
    ppermute x30, starting transfers between devices, shift_x(): return lax.ppermute(value, 'x', [(i, (i + step) % 4) for i in range(4)])  45.3 us
    ppermute x18, waiting for transfers between devices, shift_mixed(): return lax.ppermute(value, ATOM, pairs_of(target))  42.7 us
    ppermute x18, starting transfers between devices, shift_mixed(): return lax.ppermute(value, ATOM, pairs_of(target))  26.9 us
    pallas_call x6, Pallas kernels, decode_blocks(): pl.pallas_call(functools.partial(decode_kernel, size, count), in_specs=[w...  18.7 us
    pallas_call x6, Pallas kernels, encode_block(): pl.pallas_call(functools.partial(encode_kernel, size, ks, counted, kinds)...  14.3 us
    pallas_call x1, Pallas kernels, gradient(): pl.pallas_call(gradient_kernel, in_specs=[whole()] * 6, out_specs=[whole(...  5.43 us
  transfers between devices with their start and end apart: 66, of which 38 were waited for; matrix products, arithmetic and copies ran while one was open for 0% of the time, Pallas kernels for 16%

profile of v2, /device:TPU:24, one launch (start us, length us, event | category | flops | bytes accessed | tf_op | source)
XLA Modules:
  0.0 234.6 jit_solution(13641660633253949028)
XLA Ops:
  2.0 3.1 %collective-permute-start.4 = (bf16[64,2048]{1,0:T(8,128)(2,1)S(1)}, bf16[64,2048]{1,0:T(8,128)(2,1)S(1)}, u32[]{:S(2)}, u32[]{:S(2)}) collective-permute-start(bf16[64,2048]{1,0:T(8,128)(2,1)S(1)} %get-tuple-element.101), channel_id=1, source_target_pairs={{0,2},{1,3},{2,0},{3,1},{4,6},{5,7},{6,4},{7,5},{8,10},{9,11},{10,... | collective-permute-start | bytes 786440 | tf_op jit(solution)/shard_map/ppermute | solution.py:29
  7.2 5.6 %collective-permute-done.4.refs_0_.refs_6_ = bf16[64,2048]{1,0:T(8,128)(2,1)S(1)} collective-permute-done((bf16[64,2048]{1,0:T(8,128)(2,1)S(1)}, bf16[64,2048]{1,0:T(8,128)(2,1)S(1)}, u32[]{:S(2)}, u32[]{:S(2)}) %collective-permute-start.4) | collective-permute-done | bytes 262176 | tf_op jit(solution)/shard_map/ppermute | solution.py:29
  12.9 4.5 %collective-permute-done.refs_0_.refs_7_ = bf16[64,2048]{1,0:T(8,128)(2,1)S(1)} collective-permute-done((bf16[64,2048]{1,0:T(8,128)(2,1)S(1)}, bf16[64,2048]{1,0:T(8,128)(2,1)S(1)}, u32[]{:S(2)}, u32[]{:S(2)}) %collective-permute-start) | collective-permute-done | bytes 262176 | tf_op jit(solution)/shard_map/ppermute | solution.py:29
  17.9 4.0 %load.1.refs_2_.refs_4_.refs_8_.refs_5_ = bf16[2048,2048]{1,0:T(8,128)(2,1)S(1)} custom-call(s32[5,4]{1,0:T(8,128)S(1)} %pad_add_fusion.index_ref, bf16[2048,2048]{1,0:T(8,128)(2,1)} %dict_ref.1), custom_call_target="tpu_custom_call" | custom-call | bytes 8388608 | tf_op jit(solution)/shard_map/load/pallas_call | solution.py:118
  26.8 2.7 %encode.7 = (f32[64,2048]{1,0:T(8,128)S(1)}, bf16[64,2048]{1,0:T(8,128)(2,1)S(1)}, bf16[64,2048]{1,0:T(8,128)(2,1)S(1)}, f32[64,2048]{1,0:T(8,128)S(1)}) custom-call(s32[1,1]{1,0:T(1,128)} %constant.39.clone.1.index_ref, bf16[64,2048]{1,0:T(8,128)(2,1)S(1)} %collective-permute-done.refs_0_.refs_7_, ...), custom_call_target="tpu_custom_call" | custom-call | flops 2147483648 | bytes 8388608 | tf_op jit(solution)/shard_map/encode/pallas_call | solution.py:164
  34.2 3.1 %collective-permute-start.11 = (bf16[64,2048]{1,0:T(8,128)(2,1)S(1)}, bf16[64,2048]{1,0:T(8,128)(2,1)S(1)}, u32[]{:S(2)}, u32[]{:S(2)}) collective-permute-start(bf16[64,2048]{1,0:T(8,128)(2,1)S(1)} %add.64), channel_id=1, source_target_pairs={{0,3},{1,0},{2,1},{3,2},{4,7},{5,4},{6,5},{7,6},{8,11},{9,8},{10,9... | collective-permute-start | bytes 786440 | tf_op jit(solution)/shard_map/ppermute | solution.py:29
  41.4 3.9 %collective-permute-done.7.refs_2_ = bf16[64,2048]{1,0:T(8,128)(2,1)S(1)} collective-permute-done((bf16[64,2048]{1,0:T(8,128)(2,1)S(1)}, bf16[64,2048]{1,0:T(8,128)(2,1)S(1)}, u32[]{:S(2)}, u32[]{:S(2)}) %collective-permute-start.7) | collective-permute-done | bytes 262176 | tf_op jit(solution)/shard_map/ppermute | solution.py:29
  46.6 2.9 %collective-permute-start.13 = (bf16[64,2048]{1,0:T(8,128)(2,1)S(1)}, bf16[64,2048]{1,0:T(8,128)(2,1)S(1)}, u32[]{:S(2)}, u32[]{:S(2)}) collective-permute-start(bf16[64,2048]{1,0:T(8,128)(2,1)S(1)} %get-tuple-element.61.refs_1_), channel_id=1, source_target_pairs={{0,3},{1,0},{2,1},{3,2},{4,7},{5,4},{6,5},{7,6},{8,11},{9,8},{10,9... | collective-permute-start | bytes 786440 | tf_op jit(solution)/shard_map/ppermute | solution.py:29
  51.5 4.4 %collective-permute-done.12.refs_0_ = bf16[64,2048]{1,0:T(8,128)(2,1)S(1)} collective-permute-done((bf16[64,2048]{1,0:T(8,128)(2,1)S(1)}, bf16[64,2048]{1,0:T(8,128)(2,1)S(1)}, u32[]{:S(2)}, u32[]{:S(2)}) %collective-permute-start.12) | collective-permute-done | bytes 262176 | tf_op jit(solution)/shard_map/ppermute | solution.py:29
  56.1 3.7 %collective-permute-start.17 = (bf16[64,2048]{1,0:T(8,128)(2,1)S(1)}, bf16[64,2048]{1,0:T(8,128)(2,1)S(1)}, u32[]{:S(2)}, u32[]{:S(2)}) collective-permute-start(bf16[64,2048]{1,0:T(8,128)(2,1)S(1)} %collective-permute-done.13.refs_1_), channel_id=1, source_target_pairs={{0,3},{1,0},{2,1},{3,2},{4,7},{5,4},{6,5},{7,6},{8,11},{9,8},{10,9... | collective-permute-start | bytes 786440 | tf_op jit(solution)/shard_map/ppermute | solution.py:29
  61.7 3.5 %collective-permute-done.15.refs_1_ = bf16[64,2048]{1,0:T(8,128)(2,1)S(1)} collective-permute-done((bf16[64,2048]{1,0:T(8,128)(2,1)S(1)}, bf16[64,2048]{1,0:T(8,128)(2,1)S(1)}, u32[]{:S(2)}, u32[]{:S(2)}) %collective-permute-start.15) | collective-permute-done | bytes 262176 | tf_op jit(solution)/shard_map/ppermute | solution.py:29
  65.2 2.6 %decode.8 = (f32[64,2048]{1,0:T(8,128)S(1)}, f32[64,2048]{1,0:T(8,128)S(1)}, bf16[128,2048]{1,0:T(8,128)(2,1)S(1)}) custom-call(bf16[64,2048]{1,0:T(8,128)(2,1)S(1)} %collective-permute-done.14.refs_0_, bf16[64,2048]{1,0:T(8,128)(2,1)S(1)} %collective-permute-done.15.refs_1_, bf16[64,2048]{1,0:T(8,128)(2,1)S(1)} %collective-permute-done.16.refs_2_, ...), custom_call_target="tpu_custom_call" | custom-call | flops 2147483648 | bytes 8388608 | tf_op jit(solution)/shard_map/decode/pallas_call | solution.py:261
  67.9 3.4 %decode.6 = (f32[64,2048]{1,0:T(8,128)S(1)}, bf16[64,2048]{1,0:T(8,128)(2,1)S(1)}) custom-call(bf16[64,2048]{1,0:T(8,128)(2,1)S(1)} %get-tuple-element.60.refs_0_, bf16[64,2048]{1,0:T(8,128)(2,1)S(1)} %get-tuple-element.61.refs_1_, bf16[2048,2048]{1,0:T(8,128)(2,1)S(1)} %load.1.refs_2_.refs_4_.refs_8_.refs_5_), custom_call_target="tpu_custom_call" | custom-call | flops 1073741824 | bytes 8388608 | tf_op jit(solution)/shard_map/decode/pallas_call | solution.py:261
  71.9 3.4 %decode.7 = (f32[64,2048]{1,0:T(8,128)S(1)}, bf16[64,2048]{1,0:T(8,128)(2,1)S(1)}) custom-call(bf16[64,2048]{1,0:T(8,128)(2,1)S(1)} %collective-permute-done.12.refs_0_, bf16[64,2048]{1,0:T(8,128)(2,1)S(1)} %collective-permute-done.13.refs_1_, bf16[2048,2048]{1,0:T(8,128)(2,1)S(1)} %load.1.refs_2_.refs_4_.refs_8_.refs_5_), custom_call_target="tpu_custom_call" | custom-call | flops 1073741824 | bytes 8388608 | tf_op jit(solution)/shard_map/decode/pallas_call | solution.py:261
  81.3 3.2 %collective-permute-done.21.refs_1_ = bf16[64,2048]{1,0:T(8,128)(2,1)S(1)} collective-permute-done((bf16[64,2048]{1,0:T(8,128)(2,1)S(1)}, bf16[64,2048]{1,0:T(8,128)(2,1)S(1)}, u32[]{:S(2)}, u32[]{:S(2)}) %collective-permute-start.21) | collective-permute-done | bytes 262176 | tf_op jit(solution)/shard_map/ppermute | solution.py:53
  84.5 4.2 %collective-permute-done.22.refs_2_ = bf16[64,2048]{1,0:T(8,128)(2,1)S(1)} collective-permute-done((bf16[64,2048]{1,0:T(8,128)(2,1)S(1)}, bf16[64,2048]{1,0:T(8,128)(2,1)S(1)}, u32[]{:S(2)}, u32[]{:S(2)}) %collective-permute-start.22) | collective-permute-done | bytes 262176 | tf_op jit(solution)/shard_map/ppermute | solution.py:53
  88.9 4.0 %collective-permute-start.26 = (bf16[64,2048]{1,0:T(8,128)(2,1)S(1)}, bf16[64,2048]{1,0:T(8,128)(2,1)S(1)}, u32[]{:S(2)}, u32[]{:S(2)}) collective-permute-start(bf16[64,2048]{1,0:T(8,128)(2,1)S(1)} %partial.2.refs_0_), channel_id=1, source_target_pairs={{0,64},{4,20},{8,72},{12,28},{16,80},{20,4},{24,88},{28,12},{32,96... | collective-permute-start | bytes 786440 | tf_op jit(solution)/shard_map/ppermute | solution.py:53
  94.9 2.3 collective-permute-done.26.refs_3_
  97.2 3.8 %collective-permute-done.25.refs_2_ = bf16[64,2048]{1,0:T(8,128)(2,1)S(1)} collective-permute-done((bf16[64,2048]{1,0:T(8,128)(2,1)S(1)}, bf16[64,2048]{1,0:T(8,128)(2,1)S(1)}, u32[]{:S(2)}, u32[]{:S(2)}) %collective-permute-start.25) | collective-permute-done | bytes 262176 | tf_op jit(solution)/shard_map/ppermute | solution.py:53
  102.7 2.7 %collective-permute-start.28 = (bf16[64,2048]{1,0:T(8,128)(2,1)S(1)}, bf16[64,2048]{1,0:T(8,128)(2,1)S(1)}, u32[]{:S(2)}, u32[]{:S(2)}) collective-permute-start(bf16[64,2048]{1,0:T(8,128)(2,1)S(1)} %get-tuple-element.73.refs_0_), channel_id=1, source_target_pairs={{0,16},{4,68},{8,24},{12,76},{16,0},{20,84},{24,8},{28,92},{32,48}... | collective-permute-start | bytes 786440 | tf_op jit(solution)/shard_map/ppermute | solution.py:53
  105.4 2.0 collective-permute-start.27
  107.4 5.6 %collective-permute-done.29.refs_3_ = bf16[64,2048]{1,0:T(8,128)(2,1)S(1)} collective-permute-done((bf16[64,2048]{1,0:T(8,128)(2,1)S(1)}, bf16[64,2048]{1,0:T(8,128)(2,1)S(1)}, u32[]{:S(2)}, u32[]{:S(2)}) %collective-permute-start.29) | collective-permute-done | bytes 262176 | tf_op jit(solution)/shard_map/ppermute | solution.py:53
  115.4 2.2 encode.11
  118.5 2.4 %collective-permute-start.38 = (bf16[64,2048]{1,0:T(8,128)(2,1)S(1)}, bf16[64,2048]{1,0:T(8,128)(2,1)S(1)}, u32[]{:S(2)}, u32[]{:S(2)}) collective-permute-start(bf16[64,2048]{1,0:T(8,128)(2,1)S(1)} %get-tuple-element.81), channel_id=1, source_target_pairs={{0,3},{1,0},{2,1},{3,2},{4,7},{5,4},{6,5},{7,6},{8,11},{9,8},{10,9... | collective-permute-start | bytes 786440 | tf_op jit(solution)/shard_map/ppermute | solution.py:29
  121.0 3.4 %encode.10 = (f32[64,2048]{1,0:T(8,128)S(1)}, bf16[64,2048]{1,0:T(8,128)(2,1)S(1)}, bf16[64,2048]{1,0:T(8,128)(2,1)S(1)}, f32[64,2048]{1,0:T(8,128)S(1)}) custom-call(s32[5,4]{1,0:T(8,128)S(1)} %pad_add_fusion.index_ref, bf16[64,2048]{1,0:T(8,128)(2,1)S(1)} %get-tuple-element.73.refs_0_, bf16[64,2048]{1,0:T(8,128)(2,1)S(1)} %collective-permute-done.27.refs_1_, ...), custom_call_target="tpu_custom_call" | custom-call | flops 2147483648 | bytes 8388608 | tf_op jit(solution)/shard_map/encode/pallas_call | solution.py:164
  127.6 3.7 %collective-permute-start.39 = (bf16[64,2048]{1,0:T(8,128)(2,1)S(1)}, bf16[64,2048]{1,0:T(8,128)(2,1)S(1)}, u32[]{:S(2)}, u32[]{:S(2)}) collective-permute-start(bf16[64,2048]{1,0:T(8,128)(2,1)S(1)} %add.66), channel_id=1, source_target_pairs={{0,3},{1,0},{2,1},{3,2},{4,7},{5,4},{6,5},{7,6},{8,11},{9,8},{10,9... | collective-permute-start | bytes 786440 | tf_op jit(solution)/shard_map/ppermute | solution.py:29
  131.3 2.6 %encode.9 = (f32[64,2048]{1,0:T(8,128)S(1)}, f32[64,2048]{1,0:T(8,128)S(1)}) custom-call(s32[5,4]{1,0:T(8,128)S(1)} %pad_add_fusion.index_ref, bf16[64,2048]{1,0:T(8,128)(2,1)S(1)} %get-tuple-element.73.refs_0_, bf16[64,2048]{1,0:T(8,128)(2,1)S(1)} %collective-permute-done.27.refs_1_, bf16[64,2048]{1,0:T(8,128)(2,1)S(1)} %collective-permute-done.28.refs_2_, ...), custom_call_target="tpu_custom_call" | custom-call | flops 1073741824 | bytes 8388608 | tf_op jit(solution)/shard_map/encode/pallas_call | solution.py:164
  133.9 2.7 %collective-permute-done.37.refs_4_ = bf16[64,2048]{1,0:T(8,128)(2,1)S(1)} collective-permute-done((bf16[64,2048]{1,0:T(8,128)(2,1)S(1)}, bf16[64,2048]{1,0:T(8,128)(2,1)S(1)}, u32[]{:S(2)}, u32[]{:S(2)}) %collective-permute-start.37) | collective-permute-done | bytes 262176 | tf_op jit(solution)/shard_map/ppermute | solution.py:29
  136.6 3.9 %collective-permute-done.35.refs_2_ = bf16[64,2048]{1,0:T(8,128)(2,1)S(1)} collective-permute-done((bf16[64,2048]{1,0:T(8,128)(2,1)S(1)}, bf16[64,2048]{1,0:T(8,128)(2,1)S(1)}, u32[]{:S(2)}, u32[]{:S(2)}) %collective-permute-start.35) | collective-permute-done | bytes 262176 | tf_op jit(solution)/shard_map/ppermute | solution.py:29
  141.6 3.2 %collective-permute-start.41 = (bf16[64,2048]{1,0:T(8,128)(2,1)S(1)}, bf16[64,2048]{1,0:T(8,128)(2,1)S(1)}, u32[]{:S(2)}, u32[]{:S(2)}) collective-permute-start(bf16[64,2048]{1,0:T(8,128)(2,1)S(1)} %get-tuple-element.85.refs_1_.refs_4_), channel_id=1, source_target_pairs={{0,3},{1,0},{2,1},{3,2},{4,7},{5,4},{6,5},{7,6},{8,11},{9,8},{10,9... | collective-permute-start | bytes 786440 | tf_op jit(solution)/shard_map/ppermute | solution.py:29
  146.8 5.1 %collective-permute-done.40.refs_0_.refs_1_ = bf16[64,2048]{1,0:T(8,128)(2,1)S(1)} collective-permute-done((bf16[64,2048]{1,0:T(8,128)(2,1)S(1)}, bf16[64,2048]{1,0:T(8,128)(2,1)S(1)}, u32[]{:S(2)}, u32[]{:S(2)}) %collective-permute-start.40) | collective-permute-done | bytes 262176 | tf_op jit(solution)/shard_map/ppermute | solution.py:29
  151.9 3.3 %collective-permute-start.45 = (bf16[64,2048]{1,0:T(8,128)(2,1)S(1)}, bf16[64,2048]{1,0:T(8,128)(2,1)S(1)}, u32[]{:S(2)}, u32[]{:S(2)}) collective-permute-start(bf16[64,2048]{1,0:T(8,128)(2,1)S(1)} %collective-permute-done.41.refs_1_.refs_7_), channel_id=1, source_target_pairs={{0,3},{1,0},{2,1},{3,2},{4,7},{5,4},{6,5},{7,6},{8,11},{9,8},{10,9... | collective-permute-start | bytes 786440 | tf_op jit(solution)/shard_map/ppermute | solution.py:29
  157.5 3.1 %collective-permute-done.43.refs_1_.refs_2_ = bf16[64,2048]{1,0:T(8,128)(2,1)S(1)} collective-permute-done((bf16[64,2048]{1,0:T(8,128)(2,1)S(1)}, bf16[64,2048]{1,0:T(8,128)(2,1)S(1)}, u32[]{:S(2)}, u32[]{:S(2)}) %collective-permute-start.43) | collective-permute-done | bytes 262176 | tf_op jit(solution)/shard_map/ppermute | solution.py:29
  160.7 2.6 %decode.11 = (f32[64,2048]{1,0:T(8,128)S(1)}, f32[64,2048]{1,0:T(8,128)S(1)}, bf16[128,2048]{1,0:T(8,128)(2,1)S(1)}) custom-call(bf16[64,2048]{1,0:T(8,128)(2,1)S(1)} %collective-permute-done.42.refs_0_.refs_3_, bf16[64,2048]{1,0:T(8,128)(2,1)S(1)} %collective-permute-done.43.refs_1_.refs_2_, bf16[64,2048]{1,0:T(8,128)(2,1)S(1)} %collective-permute-done.44.refs_2_.refs_5_, ...), custom_call_target="tpu_custom_call" | custom-call | flops 2147483648 | bytes 8388608 | tf_op jit(solution)/shard_map/decode/pallas_call | solution.py:261
  163.4 3.4 %decode.9 = (f32[64,2048]{1,0:T(8,128)S(1)}, bf16[64,2048]{1,0:T(8,128)(2,1)S(1)}) custom-call(bf16[64,2048]{1,0:T(8,128)(2,1)S(1)} %get-tuple-element.84.refs_0_, bf16[64,2048]{1,0:T(8,128)(2,1)S(1)} %get-tuple-element.85.refs_1_.refs_4_, bf16[2048,2048]{1,0:T(8,128)(2,1)S(1)} %load.1.refs_2_.refs_4_.refs_8_.refs_5_), custom_call_target="tpu_custom_call" | custom-call | flops 1073741824 | bytes 8388608 | tf_op jit(solution)/shard_map/decode/pallas_call | solution.py:261
  167.4 3.4 %decode.10 = (f32[64,2048]{1,0:T(8,128)S(1)}, bf16[64,2048]{1,0:T(8,128)(2,1)S(1)}) custom-call(bf16[64,2048]{1,0:T(8,128)(2,1)S(1)} %collective-permute-done.40.refs_0_.refs_1_, bf16[64,2048]{1,0:T(8,128)(2,1)S(1)} %collective-permute-done.41.refs_1_.refs_7_, bf16[2048,2048]{1,0:T(8,128)(2,1)S(1)} %load.1.refs_2_.refs_4_.refs_8_.refs_5_), custom_call_target="tpu_custom_call" | custom-call | flops 1073741824 | bytes 8388608 | tf_op jit(solution)/shard_map/decode/pallas_call | solution.py:261
  173.4 2.3 collective-permute-start.49
  177.7 3.6 %collective-permute-done.49.refs_1_ = bf16[64,2048]{1,0:T(8,128)(2,1)S(1)} collective-permute-done((bf16[64,2048]{1,0:T(8,128)(2,1)S(1)}, bf16[64,2048]{1,0:T(8,128)(2,1)S(1)}, u32[]{:S(2)}, u32[]{:S(2)}) %collective-permute-start.49) | collective-permute-done | bytes 262176 | tf_op jit(solution)/shard_map/ppermute | solution.py:53
  181.3 2.8 %collective-permute-done.50.refs_2_ = bf16[64,2048]{1,0:T(8,128)(2,1)S(1)} collective-permute-done((bf16[64,2048]{1,0:T(8,128)(2,1)S(1)}, bf16[64,2048]{1,0:T(8,128)(2,1)S(1)}, u32[]{:S(2)}, u32[]{:S(2)}) %collective-permute-start.50) | collective-permute-done | bytes 262176 | tf_op jit(solution)/shard_map/ppermute | solution.py:53
  185.4 2.6 %collective-permute-start.54 = (bf16[64,2048]{1,0:T(8,128)(2,1)S(1)}, bf16[64,2048]{1,0:T(8,128)(2,1)S(1)}, u32[]{:S(2)}, u32[]{:S(2)}) collective-permute-start(bf16[64,2048]{1,0:T(8,128)(2,1)S(1)} %partial.3.refs_0_), channel_id=1, source_target_pairs={{0,96},{4,28},{8,104},{12,4},{16,112},{20,12},{24,120},{28,20},{32... | collective-permute-start | bytes 786440 | tf_op jit(solution)/shard_map/ppermute | solution.py:53
  189.9 2.1 collective-permute-done.54.refs_3_
  191.9 6.5 %collective-permute-done.53.refs_2_ = bf16[64,2048]{1,0:T(8,128)(2,1)S(1)} collective-permute-done((bf16[64,2048]{1,0:T(8,128)(2,1)S(1)}, bf16[64,2048]{1,0:T(8,128)(2,1)S(1)}, u32[]{:S(2)}, u32[]{:S(2)}) %collective-permute-start.53) | collective-permute-done | bytes 262176 | tf_op jit(solution)/shard_map/ppermute | solution.py:53
  199.8 2.6 %collective-permute-start.59 = (bf16[64,2048]{1,0:T(8,128)(2,1)S(1)}, bf16[64,2048]{1,0:T(8,128)(2,1)S(1)}, u32[]{:S(2)}, u32[]{:S(2)}) collective-permute-start(bf16[64,2048]{1,0:T(8,128)(2,1)S(1)} %get-tuple-element.98.own_ref), channel_id=1, source_target_pairs={{0,16},{4,68},{8,24},{12,76},{16,0},{20,84},{24,8},{28,92},{32,48}... | collective-permute-start | bytes 786440 | tf_op jit(solution)/shard_map/ppermute | solution.py:53
  203.1 6.7 %collective-permute-done.61.own_ref = bf16[64,2048]{1,0:T(8,128)(2,1)S(1)} collective-permute-done((bf16[64,2048]{1,0:T(8,128)(2,1)S(1)}, bf16[64,2048]{1,0:T(8,128)(2,1)S(1)}, u32[]{:S(2)}, u32[]{:S(2)}) %collective-permute-start.61) | collective-permute-done | bytes 262176 | tf_op jit(solution)/shard_map/ppermute | solution.py:53
  211.7 4.7 %collective-permute-start.55 = (f32[16,2048]{1,0:T(8,128)S(1)}, f32[16,2048]{1,0:T(8,128)S(1)}, u32[]{:S(2)}, u32[]{:S(2)}) collective-permute-start(f32[16,2048]{1,0:T(8,128)S(1)} %get-tuple-element.97), channel_id=1, source_target_pairs={{0,0},{4,16},{8,32},{12,20},{16,64},{20,24},{24,96},{28,28},{32,4}... | collective-permute-start | bytes 393224 | tf_op jit(solution)/shard_map/ppermute | solution.py:61
  217.3 5.4 %gradient.1 = (f32[2048,2048]{1,0:T(8,128)S(1)}, f32[1,2048]{1,0:T(1,128)S(1)}) custom-call(bf16[2048,128]{1,0:T(8,128)(2,1)S(1)} %turn.4.refs_0_, bf16[2048,128]{1,0:T(8,128)(2,1)S(1)} %turn.5.refs_1_, bf16[2048,128]{1,0:T(8,128)(2,1)S(1)} %turn.6.refs_2_, bf16[2048,128]{1,0:T(8,128)(2,1)S(1)} %turn.7.refs_3_, bf16[512,2048]{1,0:T(8,128)(2,1)S(1)} %arrange.1.refs_4_, ...), custom_call_target="tpu_custom_call" | custom-call | flops 4294967296 | bytes 25165824 | tf_op jit(solution)/shard_map/gradient/pallas_call | solution.py:427
  222.7 3.0 %collective-permute-start.65 = (f32[1,2048]{1,0:T(1,128)S(1)}, f32[1,2048]{1,0:T(1,128)S(1)}, u32[]{:S(2)}, u32[]{:S(2)}) collective-permute-start(f32[1,2048]{1,0:T(1,128)S(1)} %get-tuple-element.100.refs_0_), channel_id=1, source_target_pairs={{0,3},{1,0},{2,1},{3,2},{4,7},{5,4},{6,5},{7,6},{8,11},{9,8},{10,9... | collective-permute-start | bytes 24584 | tf_op jit(solution)/shard_map/ppermute | solution.py:29
  230.9 3.6 %scale.1 = bf16[2048,2048]{1,0:T(8,128)(2,1)} custom-call(f32[2048,2048]{1,0:T(8,128)S(1)} %get-tuple-element.99.moved_ref, f32[1,2048]{1,0:T(1,128)S(1)} %get-tuple-element.100.refs_0_, f32[1,2048]{1,0:T(1,128)S(1)} %collective-permute-done.63.refs_1_, f32[1,2048]{1,0:T(1,128)S(1)} %collective-permute-done.64.refs_2_, ...), custom_call_target="tpu_custom_call" | custom-call | flops 4194304 | bytes 8388608 | tf_op jit(solution)/shard_map/scale/pallas_call | solution.py:461
  (127 shorter events, 63.9 us)
Async XLA Ops:
  2.0 10.8 %collective-permute-start.4 = (bf16[64,2048]{1,0:T(8,128)(2,1)S(1)}, bf16[64,2048]{1,0:T(8,128)(2,1)S(1)}, u32[]{:S(2)}, u32[]{:S(2)}) collective-permute-start(bf16[64,2048]{1,0:T(8,128)(2,1)S(1)} %get-tuple-element.101), channel_id=1, source_target_pairs={{0,2},{1,3},{2,0},{3,1},{4,6},{5,7},{6,4},{7,5},{8,10},{9,11},{10,... | collective-permute-start | bytes 786440 | tf_op jit(solution)/shard_map/ppermute | solution.py:29
  5.1 12.3 %collective-permute-start = (bf16[64,2048]{1,0:T(8,128)(2,1)S(1)}, bf16[64,2048]{1,0:T(8,128)(2,1)S(1)}, u32[]{:S(2)}, u32[]{:S(2)}) collective-permute-start(bf16[64,2048]{1,0:T(8,128)(2,1)S(1)} %get-tuple-element.102), channel_id=1, source_target_pairs={{0,3},{1,0},{2,1},{3,2},{4,7},{5,4},{6,5},{7,6},{8,11},{9,8},{10,9... | collective-permute-start | bytes 786440 | tf_op jit(solution)/shard_map/ppermute | solution.py:29
  6.3 11.1 %collective-permute-start.1 = (bf16[64,2048]{1,0:T(8,128)(2,1)S(1)}, bf16[64,2048]{1,0:T(8,128)(2,1)S(1)}, u32[]{:S(2)}, u32[]{:S(2)}) collective-permute-start(bf16[64,2048]{1,0:T(8,128)(2,1)S(1)} %get-tuple-element.105), channel_id=1, source_target_pairs={{0,1},{1,2},{2,3},{3,0},{4,5},{5,6},{6,7},{7,4},{8,9},{9,10},{10,1... | collective-permute-start | bytes 786440 | tf_op jit(solution)/shard_map/ppermute | solution.py:29
  12.8 9.2 %collective-permute-start.5 = (bf16[64,2048]{1,0:T(8,128)(2,1)S(1)}, bf16[64,2048]{1,0:T(8,128)(2,1)S(1)}, u32[]{:S(2)}, u32[]{:S(2)}) collective-permute-start(bf16[64,2048]{1,0:T(8,128)(2,1)S(1)} %collective-permute-done.4.refs_0_.refs_6_), channel_id=1, source_target_pairs={{0,4},{4,0},{1,5},{5,1},{2,6},{6,2},{3,7},{7,3},{8,12},{12,8},{9,1... | collective-permute-start | bytes 786440 | tf_op jit(solution)/shard_map/ppermute | solution.py:33
  17.4 9.4 %collective-permute-start.2 = (bf16[64,2048]{1,0:T(8,128)(2,1)S(1)}, bf16[64,2048]{1,0:T(8,128)(2,1)S(1)}, u32[]{:S(2)}, u32[]{:S(2)}) collective-permute-start(bf16[64,2048]{1,0:T(8,128)(2,1)S(1)} %collective-permute-done.refs_0_.refs_7_), channel_id=1, source_target_pairs={{0,4},{4,0},{1,5},{5,1},{2,6},{6,2},{3,7},{7,3},{8,12},{12,8},{9,1... | collective-permute-start | bytes 786440 | tf_op jit(solution)/shard_map/ppermute | solution.py:33
  17.4 9.4 %collective-permute-start.3 = (bf16[64,2048]{1,0:T(8,128)(2,1)S(1)}, bf16[64,2048]{1,0:T(8,128)(2,1)S(1)}, u32[]{:S(2)}, u32[]{:S(2)}) collective-permute-start(bf16[64,2048]{1,0:T(8,128)(2,1)S(1)} %collective-permute-done.1.refs_1_.refs_5_), channel_id=1, source_target_pairs={{0,4},{4,0},{1,5},{5,1},{2,6},{6,2},{3,7},{7,3},{8,12},{12,8},{9,1... | collective-permute-start | bytes 786440 | tf_op jit(solution)/shard_map/ppermute | solution.py:33
  23.5 9.5 %collective-permute-start.6 = (bf16[64,2048]{1,0:T(8,128)(2,1)S(1)}, bf16[64,2048]{1,0:T(8,128)(2,1)S(1)}, u32[]{:S(2)}, u32[]{:S(2)}) collective-permute-start(bf16[64,2048]{1,0:T(8,128)(2,1)S(1)} %get-tuple-element.55), channel_id=1, source_target_pairs={{0,1},{1,2},{2,3},{3,0},{4,5},{5,6},{6,7},{7,4},{8,9},{9,10},{10,1... | collective-permute-start | bytes 786440 | tf_op jit(solution)/shard_map/ppermute | solution.py:29
  25.0 9.2 %collective-permute-start.10 = (bf16[64,2048]{1,0:T(8,128)(2,1)S(1)}, bf16[64,2048]{1,0:T(8,128)(2,1)S(1)}, u32[]{:S(2)}, u32[]{:S(2)}) collective-permute-start(bf16[64,2048]{1,0:T(8,128)(2,1)S(1)} %get-tuple-element.59), channel_id=1, source_target_pairs={{0,3},{1,0},{2,1},{3,2},{4,7},{5,4},{6,5},{7,6},{8,11},{9,8},{10,9... | collective-permute-start | bytes 786440 | tf_op jit(solution)/shard_map/ppermute | solution.py:29
  29.5 10.3 %collective-permute-start.8 = (bf16[64,2048]{1,0:T(8,128)(2,1)S(1)}, bf16[64,2048]{1,0:T(8,128)(2,1)S(1)}, u32[]{:S(2)}, u32[]{:S(2)}) collective-permute-start(bf16[64,2048]{1,0:T(8,128)(2,1)S(1)} %get-tuple-element.56), channel_id=1, source_target_pairs={{0,3},{1,0},{2,1},{3,2},{4,7},{5,4},{6,5},{7,6},{8,11},{9,8},{10,9... | collective-permute-start | bytes 786440 | tf_op jit(solution)/shard_map/ppermute | solution.py:29
  31.0 10.4 %collective-permute-start.9 = (bf16[64,2048]{1,0:T(8,128)(2,1)S(1)}, bf16[64,2048]{1,0:T(8,128)(2,1)S(1)}, u32[]{:S(2)}, u32[]{:S(2)}) collective-permute-start(bf16[64,2048]{1,0:T(8,128)(2,1)S(1)} %get-tuple-element.57), channel_id=1, source_target_pairs={{0,1},{1,2},{2,3},{3,0},{4,5},{5,6},{6,7},{7,4},{8,9},{9,10},{10,1... | collective-permute-start | bytes 786440 | tf_op jit(solution)/shard_map/ppermute | solution.py:29
  33.1 12.1 %collective-permute-start.7 = (bf16[64,2048]{1,0:T(8,128)(2,1)S(1)}, bf16[64,2048]{1,0:T(8,128)(2,1)S(1)}, u32[]{:S(2)}, u32[]{:S(2)}) collective-permute-start(bf16[64,2048]{1,0:T(8,128)(2,1)S(1)} %add.63), channel_id=1, source_target_pairs={{0,1},{1,2},{2,3},{3,0},{4,5},{5,6},{6,7},{7,4},{8,9},{9,10},{10,1... | collective-permute-start | bytes 786440 | tf_op jit(solution)/shard_map/ppermute | solution.py:29
  34.2 11.0 %collective-permute-start.11 = (bf16[64,2048]{1,0:T(8,128)(2,1)S(1)}, bf16[64,2048]{1,0:T(8,128)(2,1)S(1)}, u32[]{:S(2)}, u32[]{:S(2)}) collective-permute-start(bf16[64,2048]{1,0:T(8,128)(2,1)S(1)} %add.64), channel_id=1, source_target_pairs={{0,3},{1,0},{2,1},{3,2},{4,7},{5,4},{6,5},{7,6},{8,11},{9,8},{10,9... | collective-permute-start | bytes 786440 | tf_op jit(solution)/shard_map/ppermute | solution.py:29
  46.1 9.7 %collective-permute-start.12 = (bf16[64,2048]{1,0:T(8,128)(2,1)S(1)}, bf16[64,2048]{1,0:T(8,128)(2,1)S(1)}, u32[]{:S(2)}, u32[]{:S(2)}) collective-permute-start(bf16[64,2048]{1,0:T(8,128)(2,1)S(1)} %get-tuple-element.60.refs_0_), channel_id=1, source_target_pairs={{0,1},{1,2},{2,3},{3,0},{4,5},{5,6},{6,7},{7,4},{8,9},{9,10},{10,1... | collective-permute-start | bytes 786440 | tf_op jit(solution)/shard_map/ppermute | solution.py:29
  46.6 9.6 %collective-permute-start.13 = (bf16[64,2048]{1,0:T(8,128)(2,1)S(1)}, bf16[64,2048]{1,0:T(8,128)(2,1)S(1)}, u32[]{:S(2)}, u32[]{:S(2)}) collective-permute-start(bf16[64,2048]{1,0:T(8,128)(2,1)S(1)} %get-tuple-element.61.refs_1_), channel_id=1, source_target_pairs={{0,3},{1,0},{2,1},{3,2},{4,7},{5,4},{6,5},{7,6},{8,11},{9,8},{10,9... | collective-permute-start | bytes 786440 | tf_op jit(solution)/shard_map/ppermute | solution.py:29
  49.4 12.2 %collective-permute-start.14 = (bf16[64,2048]{1,0:T(8,128)(2,1)S(1)}, bf16[64,2048]{1,0:T(8,128)(2,1)S(1)}, u32[]{:S(2)}, u32[]{:S(2)}) collective-permute-start(bf16[64,2048]{1,0:T(8,128)(2,1)S(1)} %get-tuple-element.60.refs_0_), channel_id=1, source_target_pairs={{0,3},{1,0},{2,1},{3,2},{4,7},{5,4},{6,5},{7,6},{8,11},{9,8},{10,9... | collective-permute-start | bytes 786440 | tf_op jit(solution)/shard_map/ppermute | solution.py:29
  50.2 11.4 %collective-permute-start.16 = (bf16[64,2048]{1,0:T(8,128)(2,1)S(1)}, bf16[64,2048]{1,0:T(8,128)(2,1)S(1)}, u32[]{:S(2)}, u32[]{:S(2)}) collective-permute-start(bf16[64,2048]{1,0:T(8,128)(2,1)S(1)} %get-tuple-element.61.refs_1_), channel_id=1, source_target_pairs={{0,1},{1,2},{2,3},{3,0},{4,5},{5,6},{6,7},{7,4},{8,9},{9,10},{10,1... | collective-permute-start | bytes 786440 | tf_op jit(solution)/shard_map/ppermute | solution.py:29
  55.9 9.3 %collective-permute-start.15 = (bf16[64,2048]{1,0:T(8,128)(2,1)S(1)}, bf16[64,2048]{1,0:T(8,128)(2,1)S(1)}, u32[]{:S(2)}, u32[]{:S(2)}) collective-permute-start(bf16[64,2048]{1,0:T(8,128)(2,1)S(1)} %collective-permute-done.12.refs_0_), channel_id=1, source_target_pairs={{0,1},{1,2},{2,3},{3,0},{4,5},{5,6},{6,7},{7,4},{8,9},{9,10},{10,1... | collective-permute-start | bytes 786440 | tf_op jit(solution)/shard_map/ppermute | solution.py:29
  56.1 9.1 %collective-permute-start.17 = (bf16[64,2048]{1,0:T(8,128)(2,1)S(1)}, bf16[64,2048]{1,0:T(8,128)(2,1)S(1)}, u32[]{:S(2)}, u32[]{:S(2)}) collective-permute-start(bf16[64,2048]{1,0:T(8,128)(2,1)S(1)} %collective-permute-done.13.refs_1_), channel_id=1, source_target_pairs={{0,3},{1,0},{2,1},{3,2},{4,7},{5,4},{6,5},{7,6},{8,11},{9,8},{10,9... | collective-permute-start | bytes 786440 | tf_op jit(solution)/shard_map/ppermute | solution.py:29
  67.9 9.0 %collective-permute-start.20 = (bf16[128,2048]{1,0:T(8,128)(2,1)S(1)}, bf16[128,2048]{1,0:T(8,128)(2,1)S(1)}, u32[]{:S(2)}, u32[]{:S(2)}) collective-permute-start(bf16[128,2048]{1,0:T(8,128)(2,1)S(1)} %get-tuple-element.68), channel_id=1, source_target_pairs={{0,4},{4,0},{1,5},{5,1},{2,6},{6,2},{3,7},{7,3},{8,12},{12,8},{9,1... | collective-permute-start | bytes 1572872 | tf_op jit(solution)/shard_map/ppermute | solution.py:33
  78.3 10.4 %collective-permute-start.22 = (bf16[64,2048]{1,0:T(8,128)(2,1)S(1)}, bf16[64,2048]{1,0:T(8,128)(2,1)S(1)}, u32[]{:S(2)}, u32[]{:S(2)}) collective-permute-start(bf16[64,2048]{1,0:T(8,128)(2,1)S(1)} %get-tuple-element.71), channel_id=1, source_target_pairs={{0,24},{4,100},{8,0},{12,108},{16,8},{20,116},{24,16},{28,124},{32... | collective-permute-start | bytes 786440 | tf_op jit(solution)/shard_map/ppermute | solution.py:53
  80.2 8.5 %collective-permute-start.23 = (bf16[64,2048]{1,0:T(8,128)(2,1)S(1)}, bf16[64,2048]{1,0:T(8,128)(2,1)S(1)}, u32[]{:S(2)}, u32[]{:S(2)}) collective-permute-start(bf16[64,2048]{1,0:T(8,128)(2,1)S(1)} %get-tuple-element.72), channel_id=1, source_target_pairs={{0,16},{4,68},{8,24},{12,76},{16,0},{20,84},{24,8},{28,92},{32,48}... | collective-permute-start | bytes 786440 | tf_op jit(solution)/shard_map/ppermute | solution.py:53
  88.9 8.3 %collective-permute-start.26 = (bf16[64,2048]{1,0:T(8,128)(2,1)S(1)}, bf16[64,2048]{1,0:T(8,128)(2,1)S(1)}, u32[]{:S(2)}, u32[]{:S(2)}) collective-permute-start(bf16[64,2048]{1,0:T(8,128)(2,1)S(1)} %partial.2.refs_0_), channel_id=1, source_target_pairs={{0,64},{4,20},{8,72},{12,28},{16,80},{20,4},{24,88},{28,12},{32,96... | collective-permute-start | bytes 786440 | tf_op jit(solution)/shard_map/ppermute | solution.py:53
  92.8 8.2 %collective-permute-start.25 = (bf16[64,2048]{1,0:T(8,128)(2,1)S(1)}, bf16[64,2048]{1,0:T(8,128)(2,1)S(1)}, u32[]{:S(2)}, u32[]{:S(2)}) collective-permute-start(bf16[64,2048]{1,0:T(8,128)(2,1)S(1)} %partial.2.refs_0_), channel_id=1, source_target_pairs={{0,96},{4,28},{8,104},{12,4},{16,112},{20,12},{24,120},{28,20},{32... | collective-permute-start | bytes 786440 | tf_op jit(solution)/shard_map/ppermute | solution.py:53
  102.6 10.5 %collective-permute-start.29 = (bf16[64,2048]{1,0:T(8,128)(2,1)S(1)}, bf16[64,2048]{1,0:T(8,128)(2,1)S(1)}, u32[]{:S(2)}, u32[]{:S(2)}) collective-permute-start(bf16[64,2048]{1,0:T(8,128)(2,1)S(1)} %get-tuple-element.73.refs_0_), channel_id=1, source_target_pairs={{0,24},{4,100},{8,0},{12,108},{16,8},{20,116},{24,16},{28,124},{32... | collective-permute-start | bytes 786440 | tf_op jit(solution)/shard_map/ppermute | solution.py:53
  102.7 10.3 %collective-permute-start.28 = (bf16[64,2048]{1,0:T(8,128)(2,1)S(1)}, bf16[64,2048]{1,0:T(8,128)(2,1)S(1)}, u32[]{:S(2)}, u32[]{:S(2)}) collective-permute-start(bf16[64,2048]{1,0:T(8,128)(2,1)S(1)} %get-tuple-element.73.refs_0_), channel_id=1, source_target_pairs={{0,16},{4,68},{8,24},{12,76},{16,0},{20,84},{24,8},{28,92},{32,48}... | collective-permute-start | bytes 786440 | tf_op jit(solution)/shard_map/ppermute | solution.py:53
  105.4 8.5 %collective-permute-start.27 = (bf16[64,2048]{1,0:T(8,128)(2,1)S(1)}, bf16[64,2048]{1,0:T(8,128)(2,1)S(1)}, u32[]{:S(2)}, u32[]{:S(2)}) collective-permute-start(bf16[64,2048]{1,0:T(8,128)(2,1)S(1)} %get-tuple-element.73.refs_0_), channel_id=1, source_target_pairs={{0,8},{4,36},{8,16},{12,44},{16,24},{20,52},{24,0},{28,60},{32,40}... | collective-permute-start | bytes 786440 | tf_op jit(solution)/shard_map/ppermute | solution.py:53
  117.7 9.7 %collective-permute-start.34 = (bf16[64,2048]{1,0:T(8,128)(2,1)S(1)}, bf16[64,2048]{1,0:T(8,128)(2,1)S(1)}, u32[]{:S(2)}, u32[]{:S(2)}) collective-permute-start(bf16[64,2048]{1,0:T(8,128)(2,1)S(1)} %get-tuple-element.77), channel_id=1, source_target_pairs={{0,1},{1,2},{2,3},{3,0},{4,5},{5,6},{6,7},{7,4},{8,9},{9,10},{10,1... | collective-permute-start | bytes 786440 | tf_op jit(solution)/shard_map/ppermute | solution.py:29
  118.5 8.9 %collective-permute-start.38 = (bf16[64,2048]{1,0:T(8,128)(2,1)S(1)}, bf16[64,2048]{1,0:T(8,128)(2,1)S(1)}, u32[]{:S(2)}, u32[]{:S(2)}) collective-permute-start(bf16[64,2048]{1,0:T(8,128)(2,1)S(1)} %get-tuple-element.81), channel_id=1, source_target_pairs={{0,3},{1,0},{2,1},{3,2},{4,7},{5,4},{6,5},{7,6},{8,11},{9,8},{10,9... | collective-permute-start | bytes 786440 | tf_op jit(solution)/shard_map/ppermute | solution.py:29
  124.3 9.5 %collective-permute-start.36 = (bf16[64,2048]{1,0:T(8,128)(2,1)S(1)}, bf16[64,2048]{1,0:T(8,128)(2,1)S(1)}, u32[]{:S(2)}, u32[]{:S(2)}) collective-permute-start(bf16[64,2048]{1,0:T(8,128)(2,1)S(1)} %get-tuple-element.78), channel_id=1, source_target_pairs={{0,3},{1,0},{2,1},{3,2},{4,7},{5,4},{6,5},{7,6},{8,11},{9,8},{10,9... | collective-permute-start | bytes 786440 | tf_op jit(solution)/shard_map/ppermute | solution.py:29
  126.2 10.4 %collective-permute-start.37 = (bf16[64,2048]{1,0:T(8,128)(2,1)S(1)}, bf16[64,2048]{1,0:T(8,128)(2,1)S(1)}, u32[]{:S(2)}, u32[]{:S(2)}) collective-permute-start(bf16[64,2048]{1,0:T(8,128)(2,1)S(1)} %get-tuple-element.79), channel_id=1, source_target_pairs={{0,1},{1,2},{2,3},{3,0},{4,5},{5,6},{6,7},{7,4},{8,9},{9,10},{10,1... | collective-permute-start | bytes 786440 | tf_op jit(solution)/shard_map/ppermute | solution.py:29
  127.4 13.1 %collective-permute-start.35 = (bf16[64,2048]{1,0:T(8,128)(2,1)S(1)}, bf16[64,2048]{1,0:T(8,128)(2,1)S(1)}, u32[]{:S(2)}, u32[]{:S(2)}) collective-permute-start(bf16[64,2048]{1,0:T(8,128)(2,1)S(1)} %add.65), channel_id=1, source_target_pairs={{0,1},{1,2},{2,3},{3,0},{4,5},{5,6},{6,7},{7,4},{8,9},{9,10},{10,1... | collective-permute-start | bytes 786440 | tf_op jit(solution)/shard_map/ppermute | solution.py:29
  127.6 13.0 %collective-permute-start.39 = (bf16[64,2048]{1,0:T(8,128)(2,1)S(1)}, bf16[64,2048]{1,0:T(8,128)(2,1)S(1)}, u32[]{:S(2)}, u32[]{:S(2)}) collective-permute-start(bf16[64,2048]{1,0:T(8,128)(2,1)S(1)} %add.66), channel_id=1, source_target_pairs={{0,3},{1,0},{2,1},{3,2},{4,7},{5,4},{6,5},{7,6},{8,11},{9,8},{10,9... | collective-permute-start | bytes 786440 | tf_op jit(solution)/shard_map/ppermute | solution.py:29
  141.5 10.4 %collective-permute-start.40 = (bf16[64,2048]{1,0:T(8,128)(2,1)S(1)}, bf16[64,2048]{1,0:T(8,128)(2,1)S(1)}, u32[]{:S(2)}, u32[]{:S(2)}) collective-permute-start(bf16[64,2048]{1,0:T(8,128)(2,1)S(1)} %get-tuple-element.84.refs_0_), channel_id=1, source_target_pairs={{0,1},{1,2},{2,3},{3,0},{4,5},{5,6},{6,7},{7,4},{8,9},{9,10},{10,1... | collective-permute-start | bytes 786440 | tf_op jit(solution)/shard_map/ppermute | solution.py:29
  141.6 10.3 %collective-permute-start.41 = (bf16[64,2048]{1,0:T(8,128)(2,1)S(1)}, bf16[64,2048]{1,0:T(8,128)(2,1)S(1)}, u32[]{:S(2)}, u32[]{:S(2)}) collective-permute-start(bf16[64,2048]{1,0:T(8,128)(2,1)S(1)} %get-tuple-element.85.refs_1_.refs_4_), channel_id=1, source_target_pairs={{0,3},{1,0},{2,1},{3,2},{4,7},{5,4},{6,5},{7,6},{8,11},{9,8},{10,9... | collective-permute-start | bytes 786440 | tf_op jit(solution)/shard_map/ppermute | solution.py:29
  144.8 12.3 %collective-permute-start.42 = (bf16[64,2048]{1,0:T(8,128)(2,1)S(1)}, bf16[64,2048]{1,0:T(8,128)(2,1)S(1)}, u32[]{:S(2)}, u32[]{:S(2)}) collective-permute-start(bf16[64,2048]{1,0:T(8,128)(2,1)S(1)} %get-tuple-element.84.refs_0_), channel_id=1, source_target_pairs={{0,3},{1,0},{2,1},{3,2},{4,7},{5,4},{6,5},{7,6},{8,11},{9,8},{10,9... | collective-permute-start | bytes 786440 | tf_op jit(solution)/shard_map/ppermute | solution.py:29
  144.8 12.7 %collective-permute-start.44 = (bf16[64,2048]{1,0:T(8,128)(2,1)S(1)}, bf16[64,2048]{1,0:T(8,128)(2,1)S(1)}, u32[]{:S(2)}, u32[]{:S(2)}) collective-permute-start(bf16[64,2048]{1,0:T(8,128)(2,1)S(1)} %get-tuple-element.85.refs_1_.refs_4_), channel_id=1, source_target_pairs={{0,1},{1,2},{2,3},{3,0},{4,5},{5,6},{6,7},{7,4},{8,9},{9,10},{10,1... | collective-permute-start | bytes 786440 | tf_op jit(solution)/shard_map/ppermute | solution.py:29
  151.9 8.8 %collective-permute-start.43 = (bf16[64,2048]{1,0:T(8,128)(2,1)S(1)}, bf16[64,2048]{1,0:T(8,128)(2,1)S(1)}, u32[]{:S(2)}, u32[]{:S(2)}) collective-permute-start(bf16[64,2048]{1,0:T(8,128)(2,1)S(1)} %collective-permute-done.40.refs_0_.refs_1_), channel_id=1, source_target_pairs={{0,1},{1,2},{2,3},{3,0},{4,5},{5,6},{6,7},{7,4},{8,9},{9,10},{10,1... | collective-permute-start | bytes 786440 | tf_op jit(solution)/shard_map/ppermute | solution.py:29
  151.9 8.8 %collective-permute-start.45 = (bf16[64,2048]{1,0:T(8,128)(2,1)S(1)}, bf16[64,2048]{1,0:T(8,128)(2,1)S(1)}, u32[]{:S(2)}, u32[]{:S(2)}) collective-permute-start(bf16[64,2048]{1,0:T(8,128)(2,1)S(1)} %collective-permute-done.41.refs_1_.refs_7_), channel_id=1, source_target_pairs={{0,3},{1,0},{2,1},{3,2},{4,7},{5,4},{6,5},{7,6},{8,11},{9,8},{10,9... | collective-permute-start | bytes 786440 | tf_op jit(solution)/shard_map/ppermute | solution.py:29
  163.3 9.1 %collective-permute-start.48 = (bf16[128,2048]{1,0:T(8,128)(2,1)S(1)}, bf16[128,2048]{1,0:T(8,128)(2,1)S(1)}, u32[]{:S(2)}, u32[]{:S(2)}) collective-permute-start(bf16[128,2048]{1,0:T(8,128)(2,1)S(1)} %get-tuple-element.92), channel_id=1, source_target_pairs={{0,4},{4,0},{1,5},{5,1},{2,6},{6,2},{3,7},{7,3},{8,12},{12,8},{9,1... | collective-permute-start | bytes 1572872 | tf_op jit(solution)/shard_map/ppermute | solution.py:33
  173.4 8.0 %collective-permute-start.49 = (bf16[64,2048]{1,0:T(8,128)(2,1)S(1)}, bf16[64,2048]{1,0:T(8,128)(2,1)S(1)}, u32[]{:S(2)}, u32[]{:S(2)}) collective-permute-start(bf16[64,2048]{1,0:T(8,128)(2,1)S(1)} %get-tuple-element.94), channel_id=1, source_target_pairs={{0,16},{4,68},{8,24},{12,76},{16,0},{20,84},{24,8},{28,92},{32,48}... | collective-permute-start | bytes 786440 | tf_op jit(solution)/shard_map/ppermute | solution.py:53
  175.7 8.5 %collective-permute-start.50 = (bf16[64,2048]{1,0:T(8,128)(2,1)S(1)}, bf16[64,2048]{1,0:T(8,128)(2,1)S(1)}, u32[]{:S(2)}, u32[]{:S(2)}) collective-permute-start(bf16[64,2048]{1,0:T(8,128)(2,1)S(1)} %get-tuple-element.95), channel_id=1, source_target_pairs={{0,8},{4,36},{8,16},{12,44},{16,24},{20,52},{24,0},{28,60},{32,40}... | collective-permute-start | bytes 786440 | tf_op jit(solution)/shard_map/ppermute | solution.py:53
  188.0 10.4 %collective-permute-start.53 = (bf16[64,2048]{1,0:T(8,128)(2,1)S(1)}, bf16[64,2048]{1,0:T(8,128)(2,1)S(1)}, u32[]{:S(2)}, u32[]{:S(2)}) collective-permute-start(bf16[64,2048]{1,0:T(8,128)(2,1)S(1)} %partial.3.refs_0_), channel_id=1, source_target_pairs={{0,32},{4,12},{8,40},{12,20},{16,48},{20,28},{24,56},{28,4},{32,64... | collective-permute-start | bytes 786440 | tf_op jit(solution)/shard_map/ppermute | solution.py:53
  188.0 10.4 %collective-permute-start.52 = (bf16[64,2048]{1,0:T(8,128)(2,1)S(1)}, bf16[64,2048]{1,0:T(8,128)(2,1)S(1)}, u32[]{:S(2)}, u32[]{:S(2)}) collective-permute-start(bf16[64,2048]{1,0:T(8,128)(2,1)S(1)} %partial.3.refs_0_), channel_id=1, source_target_pairs={{0,64},{4,20},{8,72},{12,28},{16,80},{20,4},{24,88},{28,12},{32,96... | collective-permute-start | bytes 786440 | tf_op jit(solution)/shard_map/ppermute | solution.py:53
  199.3 10.5 %collective-permute-start.61 = (bf16[64,2048]{1,0:T(8,128)(2,1)S(1)}, bf16[64,2048]{1,0:T(8,128)(2,1)S(1)}, u32[]{:S(2)}, u32[]{:S(2)}) collective-permute-start(bf16[64,2048]{1,0:T(8,128)(2,1)S(1)} %get-tuple-element.98.own_ref), channel_id=1, source_target_pairs={{0,24},{4,100},{8,0},{12,108},{16,8},{20,116},{24,16},{28,124},{32... | collective-permute-start | bytes 786440 | tf_op jit(solution)/shard_map/ppermute | solution.py:53
  199.8 10.0 %collective-permute-start.59 = (bf16[64,2048]{1,0:T(8,128)(2,1)S(1)}, bf16[64,2048]{1,0:T(8,128)(2,1)S(1)}, u32[]{:S(2)}, u32[]{:S(2)}) collective-permute-start(bf16[64,2048]{1,0:T(8,128)(2,1)S(1)} %get-tuple-element.98.own_ref), channel_id=1, source_target_pairs={{0,16},{4,68},{8,24},{12,76},{16,0},{20,84},{24,8},{28,92},{32,48}... | collective-permute-start | bytes 786440 | tf_op jit(solution)/shard_map/ppermute | solution.py:53
  202.4 8.3 %collective-permute-start.57 = (bf16[64,2048]{1,0:T(8,128)(2,1)S(1)}, bf16[64,2048]{1,0:T(8,128)(2,1)S(1)}, u32[]{:S(2)}, u32[]{:S(2)}) collective-permute-start(bf16[64,2048]{1,0:T(8,128)(2,1)S(1)} %get-tuple-element.98.own_ref), channel_id=1, source_target_pairs={{0,8},{4,36},{8,16},{12,44},{16,24},{20,52},{24,0},{28,60},{32,40}... | collective-permute-start | bytes 786440 | tf_op jit(solution)/shard_map/ppermute | solution.py:53
  203.1 13.3 %collective-permute-start.56 = (bf16[64,2048]{1,0:T(8,128)(2,1)S(1)}, bf16[64,2048]{1,0:T(8,128)(2,1)S(1)}, u32[]{:S(2)}, u32[]{:S(2)}) collective-permute-start(bf16[64,2048]{1,0:T(8,128)(2,1)S(1)} %get-tuple-element.98.own_ref), channel_id=1, source_target_pairs={{0,4},{4,0},{1,5},{5,1},{2,6},{6,2},{3,7},{7,3},{8,12},{12,8},{9,1... | collective-permute-start | bytes 786440 | tf_op jit(solution)/shard_map/ppermute | solution.py:33
  211.7 16.5 %collective-permute-start.55 = (f32[16,2048]{1,0:T(8,128)S(1)}, f32[16,2048]{1,0:T(8,128)S(1)}, u32[]{:S(2)}, u32[]{:S(2)}) collective-permute-start(f32[16,2048]{1,0:T(8,128)S(1)} %get-tuple-element.97), channel_id=1, source_target_pairs={{0,0},{4,16},{8,32},{12,20},{16,64},{20,24},{24,96},{28,28},{32,4}... | collective-permute-start | bytes 393224 | tf_op jit(solution)/shard_map/ppermute | solution.py:61
  (20 other events, 279.6 us)
